TPU v7x, 32 devices: a whole 2x2x4 slice. The times are simulated.
32 devices in a mesh: dp: 4 (over x, core), tp: 8 (over z, y).
Axes of the slice: x: 2, y: 2, z: 4, core: 2. Of those that a mesh axis runs over, the one named last changes fastest.
Arguments:
- layer_inputs: bfloat16 [2, 1536, 4608], P(None, 'dp'), may hold values from -120 to 120
- out_grad: bfloat16 [1536, 4608], P('dp'), may hold values from -6 to 6
- gain: float32 [2, 4608], replicated, may hold values from 0.5 to 1.5
- w_query: bfloat16 [2, 4608, 4096], P(None, None, 'tp'), may hold values from -0.09375 to 0.09375
- w_key: bfloat16 [2, 4608, 2048], P(None, None, 'tp'), may hold values from -0.09375 to 0.09375
- w_value: bfloat16 [2, 4608, 2048], P(None, None, 'tp'), may hold values from -0.09375 to 0.09375
- w_out: bfloat16 [2, 4096, 4608], P(None, 'tp'), may hold values from -0.09375 to 0.09375
- doc_lengths: int32 [4, 4], P('dp'), may hold values from 1 to 192, 384 in all within a row
- window_reach: int32 [2], replicated, may hold values from 48 to 384, as said below
Outputs:
- input_grad: bfloat16 [1536, 4608], P('dp')
- grad_w_query: float32 [2, 4608, 4096], P(None, 'dp', 'tp')
- grad_w_key: float32 [2, 4608, 2048], P(None, 'dp', 'tp')
- grad_w_value: float32 [2, 4608, 2048], P(None, 'dp', 'tp')
- grad_w_out: float32 [2, 4096, 4608], P(None, 'tp', 'dp')
- grad_gain: float32 [2, 4608], replicated
Inputs may be any that keep to these rules, and one draw needn't show every extreme that they name: `doc_lengths`: the 4 lengths of a row fill its sequence's 384 positions in order; in every row the longest document has exactly 192 positions. `window_reach`: exactly one sublayer has reach 384 (it sees all earlier positions of its document); the other's reach is at most 192.
All inputs are finite; a program needn't handle non-finite values.
Results may differ from a plain program's by a relative error of at most 0.025.
Values may be sent and summed in bfloat16 or wider, within the bound.
No kernel may reach another device: no remote copies, remote signals or barrier semaphores. Data moves between devices by JAX's collectives and lax.ppermute only.
A program may use at most 192 MiB of HBM per device.

v0:
```python
import math

import jax
import jax.numpy as jnp
from jax import lax
from jax.sharding import PartitionSpec as P

D = 4608
HEADS = 32
HD = 128
SEQ_LEN = 384
LAYERS = 2


softcap = 50.0
epsilon = 1e-06


def swapped(x, axis, bit):
    return lax.ppermute(x, axis, [(i, i ^ 1 << bit) for i in range(lax.axis_size(axis))])


def rope_tables(length, head_width):
    half_width = head_width // 2
    frequencies = jnp.exp(
        -jnp.arange(half_width).astype(jnp.float32) * (2.0 * math.log(10000.0) / head_width)
    )
    angles = jnp.arange(length).astype(jnp.float32)[:, None] * frequencies[None, :]
    return (jnp.cos(angles)[:, None, :], jnp.sin(angles)[:, None, :])


def rotate(values, cosine, sine_table):
    half_width = values.shape[-1] // 2
    first_half = values[..., :half_width]
    second_half = values[..., half_width:]
    return jnp.concatenate(
        [
            first_half * cosine - second_half * sine_table,
            second_half * cosine + first_half * sine_table,
        ],
        axis=-1,
    )


def unrotate(values, cosine, sine_table):
    half_width = values.shape[-1] // 2
    first_half = values[..., :half_width]
    second_half = values[..., half_width:]
    return jnp.concatenate(
        [
            first_half * cosine + second_half * sine_table,
            second_half * cosine - first_half * sine_table,
        ],
        axis=-1,
    )


def allowed_pairs(lengths_row, reach, length):
    doc_ends = jnp.cumsum(lengths_row)
    places = jnp.arange(length, dtype=jnp.int32)
    document = jnp.sum((places[:, None] >= doc_ends[None, :]).astype(jnp.int32), axis=1)
    same_doc = document[:, None] == document[None, :]
    causal = places[None, :] <= places[:, None]
    in_window = places[:, None] - places[None, :] < reach
    return same_doc & causal & in_window


def join_halves(own_part, other_part, parity):
    return jnp.where(
        parity == 0,
        jnp.concatenate([own_part, other_part], axis=-1),
        jnp.concatenate([other_part, own_part], axis=-1),
    )


def split_halves(matrix, parity):
    half_width = matrix.shape[-1] // 2
    lower_part = matrix[..., :half_width]
    upper_part = matrix[..., half_width:]
    return (
        jnp.where(parity == 0, lower_part, upper_part),
        jnp.where(parity == 0, upper_part, lower_part),
    )


def contract_rows(left_side, right_side):
    return lax.dot_general(
        left_side, right_side, (((0,), (0,)), ((), ())), preferred_element_type=jnp.float32
    )


def contract_cols(left_side, right_side):
    return lax.dot_general(
        left_side, right_side, (((1,), (1,)), ((), ())), preferred_element_type=jnp.float32
    )


def pair_stack(each_head, key_heads):
    length = each_head.shape[0]
    grouped = each_head.reshape(length, key_heads, 2, HD)
    return jnp.moveaxis(grouped, 2, 0).reshape(2, length, key_heads * HD)


def norm_backward(inputs, grad_normed, upstream, gain_row):
    matrix_rows = inputs.astype(jnp.float32)
    reciprocal = lax.rsqrt(jnp.mean(matrix_rows * matrix_rows, axis=-1, keepdims=True) + epsilon)
    unit_rows = matrix_rows * reciprocal
    scaled_grad = grad_normed * gain_row
    branch = reciprocal * (
        scaled_grad - unit_rows * jnp.mean(scaled_grad * unit_rows, axis=-1, keepdims=True)
    )
    layer_grad = (upstream.astype(jnp.float32) + branch).astype(jnp.bfloat16)
    return (layer_grad, grad_normed * unit_rows)


def local(layer_inputs, out_grad, gain, w_query, w_key, w_value, w_out, doc_lengths, window_reach):
    device_rank = lax.axis_index("tp")
    parity = device_rank % 2
    local_rows = SEQ_LEN // lax.axis_size("tp")
    query_heads = w_query.shape[2] // HD
    paired = query_heads == 1
    score_scale = (D // HEADS) ** (-0.5)
    cosine_table, sine_table = rope_tables(SEQ_LEN, HD)
    first_own = device_rank * local_rows
    full_upstream = out_grad
    grads_by_layer = [None] * LAYERS
    gain_terms = [None] * LAYERS
    for layer_number in reversed(range(LAYERS)):
        whole_inputs = layer_inputs[layer_number]
        gain_row = gain[layer_number]
        query_weight = w_query[layer_number]
        key_weight = w_key[layer_number]
        value_weight = w_value[layer_number]
        out_weight = w_out[layer_number]
        matrix_rows = whole_inputs.astype(jnp.float32)
        reciprocal = lax.rsqrt(
            jnp.mean(matrix_rows * matrix_rows, axis=-1, keepdims=True) + epsilon
        )
        normed = (matrix_rows * reciprocal * gain_row).astype(jnp.bfloat16)
        queries = rotate(
            jnp.dot(normed, query_weight, preferred_element_type=jnp.float32).reshape(
                SEQ_LEN, query_heads, HD
            ),
            cosine_table,
            sine_table,
        ).astype(jnp.bfloat16)
        if paired:
            partner_key, partner_value = swapped((key_weight, value_weight), "tp", 0)
            full_key_weight = join_halves(key_weight, partner_key, parity)
            full_value_weight = join_halves(value_weight, partner_value, parity)
            key_raw = jnp.dot(normed, full_key_weight, preferred_element_type=jnp.float32)
            value_raw = jnp.dot(normed, full_value_weight, preferred_element_type=jnp.float32)
            key_heads = 1
        else:
            key_raw = jnp.dot(normed, key_weight, preferred_element_type=jnp.float32)
            value_raw = jnp.dot(normed, value_weight, preferred_element_type=jnp.float32)
            key_heads = query_heads // 2
        keys_rope = rotate(
            key_raw.reshape(SEQ_LEN, key_heads, HD), cosine_table, sine_table
        ).astype(jnp.bfloat16)
        values_cast = value_raw.reshape(SEQ_LEN, key_heads, HD).astype(jnp.bfloat16)
        keys_shared = jnp.repeat(keys_rope, query_heads // key_heads, axis=1)
        values_shared = jnp.repeat(values_cast, query_heads // key_heads, axis=1)
        allowed = allowed_pairs(doc_lengths[0], window_reach[layer_number], SEQ_LEN)
        scores = (
            jnp.einsum("thd,shd->hts", queries, keys_shared, preferred_element_type=jnp.float32)
            * score_scale
        )
        squashed = jnp.tanh(scores / softcap)
        raised = jnp.where(allowed[None], jnp.exp(softcap * squashed), 0.0)
        probability = raised / jnp.sum(raised, axis=-1, keepdims=True)
        rounded_prob = probability.astype(jnp.bfloat16)
        attended = jnp.einsum(
            "hts,shd->thd", rounded_prob, values_shared, preferred_element_type=jnp.float32
        ).astype(jnp.bfloat16)
        attended_flat = attended.reshape(SEQ_LEN, query_heads * HD)
        grad_attended = contract_cols(full_upstream, out_weight).astype(jnp.bfloat16)
        grad_w_out = contract_rows(attended_flat, full_upstream)
        grad_heads = grad_attended.reshape(SEQ_LEN, query_heads, HD)
        row_delta = jnp.sum(
            grad_heads.astype(jnp.float32) * attended.astype(jnp.float32), axis=-1
        ).T
        grad_probs = jnp.einsum(
            "thd,shd->hts", grad_heads, values_shared, preferred_element_type=jnp.float32
        )
        grad_scores = (
            probability
            * (grad_probs - row_delta[:, :, None])
            * (1.0 - squashed * squashed)
            * score_scale
        ).astype(jnp.bfloat16)
        grad_queries = (
            unrotate(
                jnp.einsum(
                    "hts,shd->thd", grad_scores, keys_shared, preferred_element_type=jnp.float32
                ),
                cosine_table,
                sine_table,
            )
            .astype(jnp.bfloat16)
            .reshape(SEQ_LEN, query_heads * HD)
        )
        key_each = unrotate(
            jnp.einsum("hts,thd->shd", grad_scores, queries, preferred_element_type=jnp.float32),
            cosine_table,
            sine_table,
        ).astype(jnp.bfloat16)
        value_each = jnp.einsum(
            "hts,thd->shd", rounded_prob, grad_heads, preferred_element_type=jnp.float32
        ).astype(jnp.bfloat16)
        grad_w_query = contract_rows(normed, grad_queries)
        if paired:
            own_key_grad = key_each[:, 0, :]
            own_value_grad = value_each[:, 0, :]
            whole_key_grad = contract_rows(normed, own_key_grad)
            whole_value_grad = contract_rows(normed, own_value_grad)
            kept_key, sent_key = split_halves(whole_key_grad, parity)
            kept_value, sent_value = split_halves(whole_value_grad, parity)
            partner_key_grad, partner_value_grad = (
                swapped(sent_key.astype(jnp.bfloat16), "tp", 0).astype(sent_key.dtype),
                swapped(sent_value.astype(jnp.bfloat16), "tp", 0).astype(sent_value.dtype),
            )
            grad_w_key = kept_key + partner_key_grad
            grad_w_value = kept_value + partner_value_grad
            pair_terms = (
                (own_key_grad[None], full_key_weight),
                (own_value_grad[None], full_value_weight),
            )
        else:
            key_stack = pair_stack(key_each, key_heads)
            value_stack = pair_stack(value_each, key_heads)
            grad_w_key = contract_rows(normed, key_stack[0]) + contract_rows(normed, key_stack[1])
            grad_w_value = contract_rows(normed, value_stack[0]) + contract_rows(
                normed, value_stack[1]
            )
            pair_terms = ((key_stack, key_weight), (value_stack, value_weight))
        totals = contract_cols(grad_queries, query_weight)
        for stacked, weight in pair_terms:
            for grad_member in range(stacked.shape[0]):
                totals = totals + contract_cols(stacked[grad_member], weight)
        whole_grad = lax.psum(totals.astype(jnp.bfloat16), "tp").astype(jnp.float32)
        full_upstream, gain_rows = norm_backward(whole_inputs, whole_grad, full_upstream, gain_row)
        gain_terms[layer_number] = jnp.sum(
            lax.dynamic_slice_in_dim(gain_rows, first_own, local_rows, 0), axis=0
        )
        layer_grads = (grad_w_query, grad_w_key, grad_w_value, grad_w_out)
        grads_by_layer[layer_number] = layer_grads
    stacks = [
        jnp.stack([grads_by_layer[layer_number][member] for layer_number in range(LAYERS)])
        for member in range(4)
    ]
    stacks = (
        lax.psum_scatter(
            stacks[0].astype(jnp.bfloat16), "dp", scatter_dimension=1, tiled=True
        ).astype(jnp.float32),
        lax.psum_scatter(
            stacks[1].astype(jnp.bfloat16), "dp", scatter_dimension=1, tiled=True
        ).astype(jnp.float32),
        lax.psum_scatter(
            stacks[2].astype(jnp.bfloat16), "dp", scatter_dimension=1, tiled=True
        ).astype(jnp.float32),
        lax.psum_scatter(
            stacks[3].astype(jnp.bfloat16), "dp", scatter_dimension=2, tiled=True
        ).astype(jnp.float32),
    )
    group_count = lax.axis_size("dp")
    gain_total = lax.psum(jnp.stack(gain_terms), ("dp", "tp"))
    return (
        full_upstream,
        stacks[0] / group_count,
        stacks[1] / group_count,
        stacks[2] / group_count,
        stacks[3] / group_count,
        gain_total / group_count,
    )


def solution(mesh):
    in_specs = (
        P(None, "dp", None),
        P("dp", None),
        P(),
        P(None, None, "tp"),
        P(None, None, "tp"),
        P(None, None, "tp"),
        P(None, "tp", None),
        P("dp", None),
        P(),
    )
    out_specs = (
        P("dp", None),
        P(None, "dp", "tp"),
        P(None, "dp", "tp"),
        P(None, "dp", "tp"),
        P(None, "tp", "dp"),
        P(),
    )
    return jax.shard_map(local, mesh=mesh, in_specs=in_specs, out_specs=out_specs, check_vma=False)
```

profile of v0, /device:TPU:0, one launch (start us, length us, event | category | flops | bytes accessed | tf_op | source)
XLA Modules:
  0.0 680.4 jit_solution(7879683073365318970)
XLA Ops:
  8.2 2.8 fusion.4
  11.0 4.1 slice_bitcast_fusion.3
  15.1 2.4 copy.75
  17.5 8.1 %slice_bitcast_fusion = (bf16[512,4608]{0,1:T(8,128)(2,1)}, bf16[512,4608]{0,1:T(8,128)(2,1)}) fusion(bf16[2,4608,512]{2,1,0:T(8,128)(2,1)} %param.12), kind=kLoop, calls=%fused_computation.64 | loop fusion | bytes 18874368 | tf_op jit(solution)/shard_map/dot_general | solution.py:141
  25.6 6.9 %copy.76 = bf16[512,4608]{1,0:T(8,128)(2,1)} copy(bf16[512,4608]{0,1:T(8,128)(2,1)} %get-tuple-element.11) | data formatting | bytes 9437184 | tf_op jit(solution)/shard_map/dot_general | solution.py:141
  32.5 4.4 fusion.53
  37.9 2.7 fusion.51
  42.1 4.1 slice_bitcast_fusion.2
  46.2 2.6 copy.79
  48.8 3.9 fusion.90
  52.8 5.4 fusion.84
  58.5 2.1 fusion.102
  67.5 2.0 fusion.30
  73.4 2.9 fusion.10
  76.4 6.8 copy.91
  83.2 2.4 copy.90
  85.6 4.3 copy.94
  89.9 128.1 %all-reduce.3.cloned.1.call-done = bf16[384,4608]{1,0:T(8,128)(2,1)} async-done(((bf16[384,4608]{1,0:T(8,128)(2,1)}), bf16[384,4608]{1,0:T(8,128)(2,1)}) %all-reduce.3.cloned.1.call-update) | async-done | bytes 3538960 | tf_op jit(solution)/shard_map/psum | solution.py:241
  218.0 7.1 %fusion.7 = (f32[384]{0:T(512)S(1)}, f32[384]{0:T(512)S(1)}, f32[384,4608]{1,0:T(8,128)}) fusion(bf16[2,384,4608]{2,1,0:T(8,128)(2,1)} %param.9, f32[384]{0:T(512)S(1)} %add_rsqrt_fusion.1, f32[4608]{0:T(1024)S(1)} %get-tuple-element.9, bf16[384,4608]{1,0:T(8,128)(2,1)} %all-reduce.3.cloned.1.call-done), kind=kLoop, calls=%fused_computation.25 | loop fusion | flops 15924480 | bytes 17717760 | tf_op jit(solution)/shard_map/reduce_sum | solution.py:106
  225.1 5.9 fusion.38
  231.9 2.4 fusion.40
  235.2 3.0 add_convert_fusion.1
  238.2 1.8 copy-done.2
  240.0 2.8 fusion.87
  242.7 1.9 copy.124
  244.6 4.6 fusion.93
  249.2 1.7 copy.95
  252.0 2.1 fusion.81
  256.6 1.4 multiply_convert_fusion
  260.8 2.0 fusion.26
  266.6 2.9 fusion.11
  269.6 3.8 fusion.58
  273.5 4.5 fusion.20
  278.1 1.8 fusion.45
  279.9 2.0 fusion.21
  281.9 2.6 pad_maximum_fusion.3
  284.9 3.9 fusion.55
  288.8 4.0 fusion.22
  292.9 1.8 fusion.42
  294.7 2.0 fusion.23
  296.7 2.5 pad_maximum_fusion.2
  299.6 7.2 %fusion.15 = bf16[1,512,4608]{2,1,0:T(8,128)(2,1)} fusion(bf16[384,512]{0,1:T(8,128)(2,1)} %bitcast.321, bf16[384,4608]{1,0:T(8,128)(2,1)} %param.10), kind=kOutput, calls=%fused_computation.41 | convolution fusion | flops 1814298624 | bytes 8650752 | tf_op jit(solution)/shard_map/dot_general | solution.py:87
  306.8 4.2 fusion.14
  311.0 8.4 %pad_maximum_fusion.1 = bf16[2,512,4608]{2,1,0:T(8,128)(2,1)} fusion(bf16[1,512,4608]{2,1,0:T(8,128)(2,1)} %fusion.15, bf16[1,512,4608]{2,1,0:T(8,128)(2,1)} %fusion.14), kind=kLoop, calls=%fused_computation.1 | loop fusion | flops 4718592 | bytes 18874368 | tf_op jit(solution)/shard_map/stack | solution.py:249
  319.4 23.6 %copy.121 = bf16[2,512,4608]{1,0,2:T(2,128)(2,1)} copy(bf16[2,512,4608]{2,1,0:T(8,128)(2,1)} %pad_maximum_fusion.1) | data formatting | bytes 18874368
  343.0 10.8 %copy.125 = bf16[576,8,2,512]{3,1,2,0:T(8,128)(2,1)} copy(bf16[576,8,2,512]{3,2,1,0:T(2,128)(2,1)} %bitcast.271) | data formatting | bytes 18874368
  354.4 7.1 %fusion.13 = bf16[1,4608,512]{2,1,0:T(8,128)(2,1)} fusion(bf16[384,512]{0,1:T(8,128)(2,1)} %bitcast.288, f32[4608]{0:T(1024)} %copy-done.42, f32[384]{0:T(512)S(1)} %add_rsqrt_fusion.1, bf16[2,384,4608]{2,1,0:T(8,128)(2,1)} %param.9), kind=kOutput, calls=%fused_computation.39 | convolution fusion | flops 1821376512 | bytes 8672768 | tf_op jit(solution)/shard_map/dot_general | solution.py:87
  361.5 6.8 %fusion.12 = bf16[1,4608,512]{2,1,0:T(8,128)(2,1)} fusion(bf16[384,512]{0,1:T(8,128)(2,1)S(1)} %bitcast.290, f32[4608]{0:T(1024)S(1)} %copy-done.40, f32[384]{0:T(512)S(1)} %get-tuple-element.61, bf16[2,384,4608]{2,1,0:T(8,128)(2,1)} %param.9), kind=kOutput, calls=%fused_computation.38 | convolution fusion | flops 1821376512 | bytes 8670720 | tf_op jit(solution)/shard_map/dot_general | solution.py:87
  368.4 8.3 %pad_maximum_fusion = bf16[2,4608,512]{2,1,0:T(8,128)(2,1)} fusion(bf16[1,4608,512]{2,1,0:T(8,128)(2,1)} %fusion.13, bf16[1,4608,512]{2,1,0:T(8,128)(2,1)} %fusion.12), kind=kLoop, calls=%fused_computation | loop fusion | flops 4718592 | bytes 18874368 | tf_op jit(solution)/shard_map/stack | solution.py:249
  379.5 27.9 %all-reduce.5.cloned.1.call-done = bf16[384,4608]{1,0:T(8,128)(2,1)} async-done(((bf16[384,4608]{1,0:T(8,128)(2,1)}), bf16[384,4608]{1,0:T(8,128)(2,1)}) %all-reduce.5.cloned.1.call-update) | async-done | bytes 3538960 | tf_op jit(solution)/shard_map/psum | solution.py:241
  407.4 3.0 convert_element_type.381
  410.5 3.5 fusion
  414.8 40.8 %psum.23 = f32[2,4608]{1,0:T(2,128)} all-reduce(f32[2,4608]{1,0:T(2,128)} %pad_maximum_fusion.14), channel_id=1, replica_groups=mesh['dp'=4,'tp'=8] {'dp','tp'}, use_global_device_ids=true, to_apply=%region_18.19 | all-reduce | flops 9216 | bytes 73728 | tf_op jit(solution)/shard_map/psum | solution.py:267
  455.6 1.4 broadcast_multiply_fusion
  457.0 5.8 add_convert_fusion
  462.8 2.9 convert_multiply_fusion.4
  465.7 42.3 %reduce-scatter.9.cloned.1.call-done = bf16[2,1152,256]{2,1,0:T(8,128)(2,1)} async-done(((bf16[2,4608,256]{2,1,0:T(8,128)(2,1)}), bf16[2,1152,256]{2,1,0:T(8,128)(2,1)}) %reduce-scatter.9.cloned.1.call-update) | async-done | bytes 1179664 | tf_op jit(solution)/shard_map/reduce_scatter | solution.py:256
  508.0 2.9 convert_multiply_fusion.5
  510.9 77.6 %reduce-scatter.13.cloned.1.call-done = bf16[1152,1024]{1,0:T(8,128)(2,1)} async-done(((bf16[4608,1024]{1,0:T(8,128)(2,1)}), bf16[1152,1024]{1,0:T(8,128)(2,1)}) %reduce-scatter.13.cloned.1.call-update) | async-done | bytes 2359312
  588.5 6.6 reshape.561
  595.1 6.0 copy.122
  601.0 3.4 convert_multiply_fusion.2
  604.5 64.4 %reduce-scatter.7.cloned.1.call-done = bf16[2,1152,512]{2,1,0:T(8,128)(2,1)} async-done(((bf16[2,4608,512]{2,1,0:T(8,128)(2,1)}), bf16[2,1152,512]{2,1,0:T(8,128)(2,1)}) %reduce-scatter.7.cloned.1.call-update) | async-done | bytes 2359312 | tf_op jit(solution)/shard_map/reduce_scatter | solution.py:253
  668.8 4.5 convert_multiply_fusion.3
  (227 shorter events, 30.7 us)
Async XLA Ops:
  7.2 210.8 %all-reduce.3.cloned.1.call-start = ((), (), s32[]{:S(2)}) async-start(), calls=%async_computation.4 | async-start | bytes 7077888 | tf_op jit(solution)/shard_map/psum | solution.py:241
  8.2 209.8 %copy-start.42 = (f32[4608]{0:T(1024)}, f32[4608]{0:T(1024)S(1)}, u32[]{:S(2)}) copy-start(f32[4608]{0:T(1024)S(1)} %get-tuple-element.9) | copy-start | bytes 55300
  8.2 216.9 %copy-start.37 = (f32[4608]{0:T(1024)}, f32[4608]{0:T(1024)S(1)}, u32[]{:S(2)}) copy-start(f32[4608]{0:T(1024)S(1)} %get-tuple-element.8) | copy-start | bytes 55300
  25.6 11.3 %slice-start = ((s8[7077888]{0:T(1024)(128)(4,1)}), s8[2883584]{0:T(1024)(128)(4,1)S(1)}, s32[]{:S(2)}) async-start(s8[7077888]{0:T(1024)(128)(4,1)} %bitcast.254), calls=%async_computation.10 | async-start | bytes 5767168
  32.5 4.4 slice-start.1
  32.5 5.4 copy-start.11
  37.9 3.4 copy-start.47
  37.9 4.0 copy-start.48
  41.1 189.9 %copy-start.5 = (f32[384,64]{0,1:T(8,128)}, f32[384,64]{0,1:T(8,128)S(1)}, u32[]{:S(2)}) copy-start(f32[384,64]{0,1:T(8,128)S(1)} %get-tuple-element.47) | copy-start | bytes 294916
  41.1 189.9 %copy-start.8 = (f32[384,64]{0,1:T(8,128)}, f32[384,64]{0,1:T(8,128)S(1)}, u32[]{:S(2)}) copy-start(f32[384,64]{0,1:T(8,128)S(1)} %get-tuple-element.48) | copy-start | bytes 294916
  63.6 3.3 slice-start.16
  63.6 3.5 slice-start.17
  66.7 2.9 slice-start.12
  66.8 2.8 copy-start.20
  66.8 4.0 copy-start.18
  66.9 2.7 copy-start.15
  69.6 2.6 copy-start.21
  69.6 3.8 copy-start.31
  76.4 331.0 %all-reduce.5.cloned.1.call-start = ((), (), s32[]{:S(2)}) async-start(), calls=%async_computation.5 | async-start | bytes 7077888 | tf_op jit(solution)/shard_map/psum | solution.py:241
  76.4 6.8 copy-start.4
  218.0 13.9 %slice-start.2 = ((s8[7077888]{0:T(1024)(128)(4,1)}), s8[4194304]{0:T(1024)(128)(4,1)S(1)}, s32[]{:S(2)}) async-start(s8[7077888]{0:T(1024)(128)(4,1)} %bitcast.256), calls=%async_computation.12 | async-start | bytes 8388608
  225.1 6.8 slice-start.3
  225.1 6.8 copy-start.14
  231.9 3.3 copy-start
  231.9 3.3 copy-start.12
  231.9 3.2 copy-start.43
  231.9 8.0 %slice-start.22 = ((s8[9437184]{0:T(1024)(128)(4,1)}), s8[4194304]{0:T(1024)(128)(4,1)S(1)}, s32[]{:S(2)}) async-start(s8[9437184]{0:T(1024)(128)(4,1)} %bitcast.326), calls=%async_computation.32 | async-start | bytes 8388608
  231.9 8.0 %slice-start.23 = ((s8[9437184]{0:T(1024)(128)(4,1)}), s8[4194304]{0:T(1024)(128)(4,1)S(1)}, s32[]{:S(2)}) async-start(s8[9437184]{0:T(1024)(128)(4,1)} %bitcast.326), calls=%async_computation.33 | async-start | bytes 8388608
  235.2 4.8 slice-start.24
  251.0 3.2 copy-start.35
  252.0 2.9 copy-start.13
  252.0 3.3 copy-start.28
  256.6 3.5 slice-start.19
  256.6 3.8 slice-start.20
  258.0 2.8 slice-start.21
  259.6 5.7 copy-start.26
  259.6 6.9 %copy-start.33 = (bf16[1,384,2,128]{1,3,0,2:T(8,128)(2,1)}, bf16[1,384,2,128]{1,3,0,2:T(8,128)(2,1)S(1)}, u32[]{:S(2)}) copy-start(bf16[1,384,2,128]{1,3,0,2:T(8,128)(2,1)S(1)} %get-tuple-element.35) | copy-start | bytes 589828
  259.6 3.2 slice-start.14
  260.0 2.9 copy-start.24
  260.0 4.0 copy-start.22
  260.0 2.8 copy-start.16
  269.5 193.4 %reduce-scatter.11.cloned.1.call-start = ((), (), s32[]{:S(2)}) async-start(), calls=%async_computation.8 | async-start | bytes 5898240 | tf_op jit(solution)/shard_map/reduce_scatter | solution.py:259
  269.5 3.9 copy-start.32
  269.5 3.9 copy-start.44
  269.6 8.5 %slice-start.4 = ((s8[7077888]{0:T(1024)(128)(4,1)}), s8[4194304]{0:T(1024)(128)(4,1)S(1)}, s32[]{:S(2)}) async-start(s8[7077888]{0:T(1024)(128)(4,1)} %bitcast.258), calls=%async_computation.14 | async-start | bytes 8388608
  273.4 4.6 slice-start.5
  273.5 4.6 copy-start.27
  273.5 4.6 copy-start.38
  284.6 223.5 %reduce-scatter.9.cloned.1.call-start = ((), (), s32[]{:S(2)}) async-start(), calls=%async_computation.7 | async-start | bytes 5898240 | tf_op jit(solution)/shard_map/reduce_scatter | solution.py:256
  284.8 3.9 copy-start.19
  284.8 3.9 copy-start.45
  284.9 8.0 %slice-start.6 = ((s8[7077888]{0:T(1024)(128)(4,1)}), s8[4194304]{0:T(1024)(128)(4,1)S(1)}, s32[]{:S(2)}) async-start(s8[7077888]{0:T(1024)(128)(4,1)} %bitcast.260), calls=%async_computation.16 | async-start | bytes 8388608
  288.8 4.1 slice-start.7
  288.8 4.1 copy-start.25
  288.8 4.1 copy-start.39
  299.3 289.2 %reduce-scatter.13.cloned.1.call-start = ((), (), s32[]{:S(2)}) async-start(), calls=%async_computation.9 | async-start | bytes 11796480
  299.6 7.2 %copy-start.3 = (bf16[384,4608]{1,0:T(8,128)(2,1)S(1)}, bf16[384,4608]{1,0:T(8,128)(2,1)}, u32[]{:S(2)}) copy-start(bf16[384,4608]{1,0:T(8,128)(2,1)} %copy-done.2) | copy-start | bytes 10616836
  299.6 7.2 %copy-start.36 = (bf16[4,128,384]{2,1,0:T(8,128)(2,1)S(1)}, bf16[4,128,384]{2,1,0:T(8,128)(2,1)}, u32[]{:S(2)}) copy-start(bf16[4,128,384]{2,1,0:T(8,128)(2,1)} %get-tuple-element.60) | copy-start | bytes 1179652
  353.8 315.0 %reduce-scatter.7.cloned.1.call-start = ((), (), s32[]{:S(2)}) async-start(), calls=%async_computation.6 | async-start | bytes 11796480 | tf_op jit(solution)/shard_map/reduce_scatter | solution.py:253
  354.3 7.2 %copy-start.17 = (bf16[384,4,128]{0,2,1:T(8,128)(2,1)S(1)}, bf16[384,4,128]{0,2,1:T(8,128)(2,1)}, u32[]{:S(2)}) copy-start(bf16[384,4,128]{0,2,1:T(8,128)(2,1)} %copy-done.16) | copy-start | bytes 1179652
  354.4 7.1 %copy-start.40 = (f32[4608]{0:T(1024)S(1)}, f32[4608]{0:T(1024)}, u32[]{:S(2)}) copy-start(f32[4608]{0:T(1024)} %copy-done.37) | copy-start | bytes 55300
  407.4 3.1 copy-start.1
  407.4 3.1 copy-start.41
  410.4 3.7 copy-start.46
  (16 other events, 31.7 us)
Sparse Core Ops, SparseCore 0:
  76.5 141.4 all-reduce.2
  269.6 137.7 all-reduce.4
  409.9 47.7 reduce-scatter.10
  460.1 47.8 reduce-scatter.8
  510.5 77.9 reduce-scatter.12
  590.9 77.8 reduce-scatter.6
where the time goes:
time: 688 us; the launch traced here: 680 us
  waiting for transfers between devices  340 us (49%)
  matrix products  110 us (16%)
  local copies, waits for them, and re-layouts  100 us (15%)
  other arithmetic  72.7 us (11%)
  blocking collectives  40.8 us (6%)
  between operations  15.6 us (2%)
    psum x2, waiting for transfers between devices, local(): whole_grad = lax.psum(totals.astype(jnp.bfloat16), 'tp').astype(jnp.float32)  156 us
    unnamed x7, waiting for transfers between devices  77.7 us
    reduce_scatter x1, waiting for transfers between devices, local(): lax.psum_scatter(stacks[0].astype(jnp.bfloat16), 'dp', scatter_dimension=...  64.4 us
    unnamed x152, local copies, waits for them, and re-layouts  52.1 us
    dot_general x12, matrix products, contract_rows(): lax.dot_general(left_side, right_side, (((0,), (0,)), ((), ())), preferre...  49.3 us
    reduce_scatter x1, waiting for transfers between devices, local(): lax.psum_scatter(stacks[1].astype(jnp.bfloat16), 'dp', scatter_dimension=...  42.3 us
    psum x1, blocking collectives, local(): gain_total = lax.psum(jnp.stack(gain_terms), ('dp', 'tp'))  40.8 us
    dot_general x12, matrix products, contract_cols(): lax.dot_general(left_side, right_side, (((1,), (1,)), ((), ())), preferre...  25.4 us
  transfers between devices with their start and end apart: 6, of which 5 were waited for; matrix products, arithmetic and copies ran while one was open for 23% of the time, Pallas kernels for 0%

commit v1 on v0

--- a/solution.py
+++ b/solution.py
@@ -1,8 +1,12 @@
+import functools
 import math
 
 import jax
 import jax.numpy as jnp
+import numpy as np
 from jax import lax
+from jax.experimental import pallas as pl
+from jax.experimental.pallas import tpu as pltpu
 from jax.sharding import PartitionSpec as P
 
 D = 4608
@@ -113,7 +117,7 @@
     return (layer_grad, grad_normed * unit_rows)
 
 
-def local(layer_inputs, out_grad, gain, w_query, w_key, w_value, w_out, doc_lengths, window_reach):
+def local_general(layer_inputs, out_grad, gain, w_query, w_key, w_value, w_out, doc_lengths, window_reach):
     device_rank = lax.axis_index("tp")
     parity = device_rank % 2
     local_rows = SEQ_LEN // lax.axis_size("tp")
@@ -275,6 +279,619 @@
     )
 
 
+def rope_wide(length, head_width):
+    half_width = head_width // 2
+    frequencies = np.exp(-np.arange(half_width) * (2.0 * math.log(10000.0) / head_width))
+    angles = np.arange(length)[:, None] * frequencies[None, :]
+    cosine, sine_table = (np.cos(angles), np.sin(angles))
+    return (
+        jnp.asarray(np.concatenate([cosine, cosine], axis=-1), jnp.float32),
+        jnp.asarray(np.concatenate([-sine_table, sine_table], axis=-1), jnp.float32),
+    )
+
+
+def dot_nt(left_side, right_side):
+    return lax.dot_general(
+        left_side, right_side, (((1,), (1,)), ((), ())), preferred_element_type=jnp.float32
+    )
+
+
+def dot_nn(left_side, right_side):
+    return lax.dot_general(
+        left_side, right_side, (((1,), (0,)), ((), ())), preferred_element_type=jnp.float32
+    )
+
+
+def forward_kernel(
+    layer, scale, rank, lengths, reach, x_ref, gain_ref, wq_ref, wk_ref, wv_ref, cos_ref, sin_ref,
+    *rest,
+):
+    normed_refs = rest[: -10]
+    q_ref, k_ref, v_ref, att_ref, prob_ref, slope_ref, recip_ref, accq, acck, accv = rest[-10:]
+    step = pl.program_id(0)
+    length = x_ref.shape[1]
+    width = wq_ref.shape[1]
+    row_block = 128
+
+    @pl.when(step == 0)
+    def _():
+        x = x_ref[0].astype(jnp.float32)
+        mean = jnp.mean(x * x, axis=-1, keepdims=True)
+        recip_ref[...] = jnp.broadcast_to(lax.rsqrt(mean + epsilon), recip_ref.shape)
+        accq[...] = jnp.zeros_like(accq)
+        acck[...] = jnp.zeros_like(acck)
+        accv[...] = jnp.zeros_like(accv)
+
+    columns = pl.ds(pl.multiple_of((step ^ rank[0]) * width, 128), width)
+    x = x_ref[0, :, columns].astype(jnp.float32)
+    normed = (x * recip_ref[:, :1] * gain_ref[layer : layer + 1, columns]).astype(jnp.bfloat16)
+    for mask, normed_ref in enumerate(normed_refs):
+
+        @pl.when(step == mask)
+        def _():
+            normed_ref[...] = normed
+
+    accq[...] += dot_nn(normed, wq_ref[0])
+    acck[...] += dot_nn(normed, wk_ref[0])
+    accv[...] += dot_nn(normed, wv_ref[0])
+
+    @pl.when(step == pl.num_programs(0) - 1)
+    def _():
+        cosine, sine = (cos_ref[...], sin_ref[...])
+
+        def turn(part):
+            return part * cosine + pltpu.roll(part, HD // 2, 1) * sine
+
+        v_ref[...] = accv[...].astype(jnp.bfloat16)
+        for head in range(acck.shape[1] // HD):
+            part = slice(head * HD, (head + 1) * HD)
+            k_ref[:, part] = turn(acck[:, part]).astype(jnp.bfloat16)
+        ends = [lengths[0, 0]]
+        for doc in range(1, lengths.shape[1] - 1):
+            ends.append(ends[-1] + lengths[0, doc])
+        window = reach[layer]
+        heads = accq.shape[1] // HD
+        share = heads // (acck.shape[1] // HD)
+        for head in range(heads):
+            part = slice(head * HD, (head + 1) * HD)
+            q_ref[:, part] = turn(accq[:, part]).astype(jnp.bfloat16)
+        for block in range(length // row_block):
+            rows = slice(block * row_block, (block + 1) * row_block)
+            seen = (block + 1) * row_block
+            row = block * row_block + lax.broadcasted_iota(jnp.int32, (row_block, seen), 0)
+            col = lax.broadcasted_iota(jnp.int32, (row_block, seen), 1)
+            first = row - window + 1
+            for end in ends:
+                first = jnp.maximum(first, jnp.where(row >= end, end, 0))
+            allowed = (col <= row) & (col >= first)
+            for head in range(heads):
+                part = slice(head * HD, (head + 1) * HD)
+                kv = head // share
+                kv_part = slice(kv * HD, (kv + 1) * HD)
+                scores = dot_nt(q_ref[rows, part], k_ref[:seen, kv_part]) * scale
+                squashed = jnp.tanh(scores / softcap)
+                raised = jnp.where(allowed, jnp.exp(softcap * squashed), 0.0)
+                total = jnp.sum(raised, axis=-1, keepdims=True)
+                probability = raised * (1.0 / total)
+                rounded = probability.astype(jnp.bfloat16)
+                prob_ref[head, rows, :seen] = rounded
+                slope_ref[head, rows, :seen] = probability * ((1.0 - squashed * squashed) * scale)
+                att_ref[rows, part] = dot_nn(rounded, v_ref[:seen, kv_part]).astype(jnp.bfloat16)
+
+
+def forward_call(layer, steps, rank, layer_inputs, gain, w_query, w_key, w_value, lengths, reach, cosine, sine):
+    _, length, depth = layer_inputs.shape
+    width = depth // steps
+    q_width, k_width = (w_query.shape[2], w_key.shape[2])
+    heads = q_width // HD
+    scale = (D // HEADS) ** (-0.5)
+    smem = pl.BlockSpec(memory_space=pltpu.SMEM)
+
+    def weight(columns):
+        return pl.BlockSpec((1, width, columns), lambda k, rank: (layer, k ^ rank[0], 0))
+
+    def whole(*shape):
+        return pl.BlockSpec(shape, lambda k, rank: (0,) * len(shape))
+
+    bf, f32 = (jnp.bfloat16, jnp.float32)
+    shapes = [((length, width), bf)] * steps + [
+        ((length, q_width), bf),
+        ((length, k_width), bf),
+        ((length, k_width), bf),
+        ((length, q_width), bf),
+        ((heads, length, length), bf),
+        ((heads, length, length), f32),
+        ((length, HD), f32),
+    ]
+    flops = 2 * length * depth * (q_width + 2 * k_width)
+    return pl.pallas_call(
+        functools.partial(forward_kernel, layer, scale),
+        grid_spec=pltpu.PrefetchScalarGridSpec(
+            num_scalar_prefetch=1,
+            grid=(steps,),
+            in_specs=[
+                smem,
+                smem,
+                pl.BlockSpec((1, length, depth), lambda k, rank: (layer, 0, 0)),
+                whole(*gain.shape),
+                weight(q_width),
+                weight(k_width),
+                weight(k_width),
+                whole(length, HD),
+                whole(length, HD),
+            ],
+            out_specs=[whole(*shape) for shape, _ in shapes],
+            scratch_shapes=[
+                pltpu.VMEM((length, q_width), f32),
+                pltpu.VMEM((length, k_width), f32),
+                pltpu.VMEM((length, k_width), f32),
+            ],
+        ),
+        out_shape=[jax.ShapeDtypeStruct(shape, kind) for shape, kind in shapes],
+        cost_estimate=pl.CostEstimate(
+            flops=flops, transcendentals=heads * length * length, bytes_accessed=20 << 20
+        ),
+    )(rank, lengths, reach, layer_inputs, gain, w_query, w_key, w_value, cosine, sine)
+
+
+def attention_kernel(
+    flat, chunks, side, rank, *refs,
+):
+    g_refs = refs[: 1 if flat else 4]
+    wo_ref, q_ref, k_ref, v_ref, att_ref, prob_ref, slope_ref, cos_ref, sin_ref = refs[
+        len(g_refs) : len(g_refs) + 9
+    ]
+    wq_ref, wk_ref, wv_ref, factor_ref, *rest = refs[len(g_refs) + 9 :]
+    pieces = rest[2 * chunks : -4]
+    acc, heads_ref, dk, dv = rest[-4:]
+    others, owns = (rest[:chunks], rest[chunks : 2 * chunks])
+    step = pl.program_id(0)
+    steps = pl.num_programs(0) // 2
+    length, q_width = acc.shape
+    k_width = dk.shape[1]
+    row_block = 128
+
+    @pl.when(step == 0)
+    def _():
+        acc[...] = jnp.zeros_like(acc)
+
+    if flat:
+
+        @pl.when(step < steps)
+        def _():
+            acc[...] += dot_nt(g_refs[0][...], wo_ref[0])
+
+        for mask, piece in enumerate(pieces):
+
+            @pl.when(step == mask)
+            def _():
+                piece[...] = g_refs[0][...]
+
+    else:
+        for mask, g_ref in enumerate(g_refs):
+
+            @pl.when(step == mask)
+            def _():
+                acc[...] += dot_nt(g_ref[...], wo_ref[0])
+
+    @pl.when(step == steps - 1)
+    def _():
+        cosine, sine = (cos_ref[...], sin_ref[...])
+
+        def unturn(part, rows):
+            return part * cosine[rows] - pltpu.roll(part, HD // 2, 1) * sine[rows]
+
+        heads_ref[...] = acc[...].astype(jnp.bfloat16)
+        dk[...] = jnp.zeros_like(dk)
+        dv[...] = jnp.zeros_like(dv)
+        heads = q_width // HD
+        share = heads // (k_width // HD)
+        for head in range(heads):
+            part = slice(head * HD, (head + 1) * HD)
+            kv = head // share
+            kv_part = slice(kv * HD, (kv + 1) * HD)
+            for block in range(length // row_block):
+                rows = slice(block * row_block, (block + 1) * row_block)
+                seen = (block + 1) * row_block
+                ga = heads_ref[rows, part]
+                delta = jnp.sum(
+                    ga.astype(jnp.float32) * att_ref[rows, part].astype(jnp.float32),
+                    axis=-1,
+                    keepdims=True,
+                )
+                grad_probs = dot_nt(ga, v_ref[:seen, kv_part])
+                grad_scores = (slope_ref[head, rows, :seen] * (grad_probs - delta)).astype(
+                    jnp.bfloat16
+                )
+                gq = dot_nn(grad_scores, k_ref[:seen, kv_part])
+                factor_ref[rows, part] = unturn(gq, rows).astype(jnp.bfloat16)
+                dk[:seen, kv_part] += contract_rows(grad_scores, q_ref[rows, part])
+                dv[:seen, kv_part] += contract_rows(prob_ref[head, rows, :seen], ga)
+        every = slice(0, length)
+        for kv in range(k_width // HD):
+            kv_part = slice(kv * HD, (kv + 1) * HD)
+            factor_ref[:, q_width + kv * HD : q_width + (kv + 1) * HD] = unturn(
+                dk[:, kv_part], every
+            ).astype(jnp.bfloat16)
+        factor_ref[:, q_width + k_width : q_width + 2 * k_width] = dv[...].astype(jnp.bfloat16)
+        factor_ref[:, q_width + 2 * k_width :] = att_ref[...]
+
+    @pl.when(step >= steps)
+    def _():
+        total = dot_nt(factor_ref[:, :q_width], wq_ref[0])
+        total += dot_nt(factor_ref[:, q_width : q_width + k_width], wk_ref[0])
+        total += dot_nt(factor_ref[:, q_width + k_width : q_width + 2 * k_width], wv_ref[0])
+        rows = length // chunks
+
+        @pl.when(step < steps + steps // 2)
+        def _():
+            for chunk in range(chunks):
+                others[chunk][0] = total[chunk * rows : (chunk + 1) * rows].astype(jnp.bfloat16)
+
+        @pl.when(step >= steps + steps // 2)
+        def _():
+            for chunk in range(chunks):
+                owns[chunk][0] = total[chunk * rows : (chunk + 1) * rows].astype(jnp.bfloat16)
+
+
+def attention_call(layer, steps, chunks, side, rank, upstream, w_out, forward, cosine, sine, w_query, w_key, w_value):
+    q, k, v, att, prob, slope = forward[steps:-1]
+    length, q_width = q.shape
+    k_width = k.shape[1]
+    depth = w_out.shape[2]
+    width = depth // steps
+    flat = len(upstream) == 1
+
+    half = steps // 2
+
+    def whole(*shape):
+        return pl.BlockSpec(shape, lambda k, side, rank: (0,) * len(shape))
+
+    def first(k):
+        return jnp.minimum(k, steps - 1)
+
+    def last(k, side):
+        turn = jnp.maximum(k - steps, 0)
+        block = turn + half * (1 - side[0])
+        return jnp.where(block >= steps, block - steps, block)
+
+    def weight(columns):
+        return pl.BlockSpec((1, width, columns), lambda k, side, rank: (layer, last(k, side), 0))
+
+    if flat:
+        g_specs = [pl.BlockSpec((length, width), lambda k, side, rank: (0, first(k) ^ rank[0]))]
+    else:
+        g_specs = [whole(length, width)] * steps
+    pieces = steps if flat else 0
+    rows = length // chunks
+    other_spec = pl.BlockSpec(
+        (1, rows, width), lambda k, side, rank: (jnp.clip(k - steps, 0, half - 1), 0, 0)
+    )
+    own_spec = pl.BlockSpec(
+        (1, rows, width), lambda k, side, rank: (jnp.clip(k - steps - half, 0, half - 1), 0, 0)
+    )
+    bf, f32 = (jnp.bfloat16, jnp.float32)
+    f_width = 2 * (q_width + k_width)
+    return pl.pallas_call(
+        functools.partial(attention_kernel, flat, chunks),
+        grid_spec=pltpu.PrefetchScalarGridSpec(
+        num_scalar_prefetch=2,
+        grid=(2 * steps,),
+        in_specs=g_specs
+        + [
+            pl.BlockSpec((1, q_width, width), lambda k, side, rank: (layer, 0, first(k) ^ rank[0])),
+            whole(*q.shape),
+            whole(*k.shape),
+            whole(*v.shape),
+            whole(*att.shape),
+            whole(*prob.shape),
+            whole(*slope.shape),
+            whole(length, HD),
+            whole(length, HD),
+            weight(q_width),
+            weight(k_width),
+            weight(k_width),
+        ],
+        out_specs=[
+            whole(length, f_width),
+        ]
+        + [other_spec] * chunks
+        + [own_spec] * chunks
+        + [whole(length, width)] * pieces,
+        scratch_shapes=[
+            pltpu.VMEM((length, q_width), f32),
+            pltpu.VMEM((length, q_width), bf),
+            pltpu.VMEM((length, k_width), f32),
+            pltpu.VMEM((length, k_width), f32),
+        ],
+        ),
+        out_shape=[jax.ShapeDtypeStruct((length, f_width), bf)]
+        + [jax.ShapeDtypeStruct((half, rows, width), bf)] * (2 * chunks)
+        + [jax.ShapeDtypeStruct((length, width), bf)] * pieces,
+        cost_estimate=pl.CostEstimate(
+            flops=4 * length * depth * (q_width + k_width), transcendentals=0, bytes_accessed=20 << 20
+        ),
+    )(side, rank, *upstream, w_out, q, k, v, att, prob, slope, cosine, sine, w_query, w_key, w_value)
+
+
+def norm_kernel(layer, flat, keep, steps, side, rank, own_ref, other_ref, x_ref, recip_ref, *refs):
+    pieces = 1 if flat else steps
+    g_refs, gain_ref, rest = (refs[:pieces], refs[pieces], refs[pieces + 1 :])
+    outs = rest[-(1 if keep else steps) - 1 : -1]
+    gain_out = rest[-1]
+    halves, _, width = own_ref.shape
+    depth = steps * width
+    recip = recip_ref[:, :1]
+
+    @pl.when(pl.program_id(0) == 0)
+    def _():
+        if len(rest) > len(outs) + 1:
+            gain_out[...] = rest[len(outs)][...]
+        else:
+            gain_out[...] = jnp.zeros_like(gain_out)
+
+    def grad_of(block):
+        own, other = (own_ref[block % halves], other_ref[block % halves])
+        pick = block // halves == side[0]
+        return jnp.where(pick, own.astype(jnp.float32), other.astype(jnp.float32))
+
+    total = jnp.zeros_like(recip)
+    for mask in range(steps):
+        block = mask ^ rank[0]
+        columns = pl.ds(pl.multiple_of(block * width, 128), width)
+        unit = x_ref[0, :, columns].astype(jnp.float32) * recip
+        product = grad_of(block) * unit
+        gain_out[:, columns] += jnp.sum(product.reshape(-1, 8, width), axis=0)
+        total += jnp.sum(product * gain_ref[layer : layer + 1, columns], axis=-1, keepdims=True)
+    mean = total / depth
+    for mask in range(steps):
+        block = mask ^ rank[0]
+        columns = pl.ds(pl.multiple_of(block * width, 128), width)
+        unit = x_ref[0, :, columns].astype(jnp.float32) * recip
+        grad = grad_of(block) * gain_ref[layer : layer + 1, columns]
+        g = (g_refs[0][:, columns] if flat else g_refs[mask][...]).astype(jnp.float32)
+        value = (g + recip * (grad - unit * mean)).astype(jnp.bfloat16)
+        if keep:
+            outs[0][:, columns] = value
+        else:
+            outs[mask][...] = value
+
+
+def norm_call(layer, chunk, side, rank, own, other, layer_inputs, recip, upstream, gain, keep, earlier):
+    halves, rows, width = own.shape
+    steps = 2 * halves
+    length, depth = layer_inputs.shape[1:]
+    flat = len(upstream) == 1
+    parts = 3
+    tile = rows // parts
+    half_spec = pl.BlockSpec((halves, tile, width), lambda r: (0, r, 0))
+    flat_spec = pl.BlockSpec((tile, depth), lambda r: (chunk * parts + r, 0))
+    piece_spec = pl.BlockSpec((tile, width), lambda r: (chunk * parts + r, 0))
+    gain_spec = pl.BlockSpec((8, depth), lambda r: (0, 0))
+    smem = pl.BlockSpec(memory_space=pltpu.SMEM)
+    extra = [] if earlier is None else list(earlier)
+    outs = 1 if keep else steps
+    first = 7 + len(upstream)
+    return pl.pallas_call(
+        functools.partial(norm_kernel, layer, flat, keep, steps),
+        grid=(parts,),
+        in_specs=[
+            smem,
+            smem,
+            half_spec,
+            half_spec,
+            pl.BlockSpec((1, tile, depth), lambda r: (layer, chunk * parts + r, 0)),
+            pl.BlockSpec((tile, HD), lambda r: (chunk * parts + r, 0)),
+        ]
+        + [flat_spec if flat else piece_spec] * len(upstream)
+        + [pl.BlockSpec(gain.shape, lambda r: (0, 0))]
+        + ([pl.BlockSpec(memory_space=pl.ANY)] * outs + [gain_spec])[: len(extra)],
+        out_specs=[flat_spec if keep else piece_spec] * outs + [gain_spec],
+        out_shape=[
+            jax.ShapeDtypeStruct((length, depth) if keep else (length, width), jnp.bfloat16)
+        ]
+        * outs
+        + [jax.ShapeDtypeStruct((8, depth), jnp.float32)],
+        input_output_aliases={first + i: i for i in range(outs)} if extra else {},
+        cost_estimate=pl.CostEstimate(
+            flops=30 * rows * depth, transcendentals=0, bytes_accessed=4 << 20
+        ),
+    )(side, rank, own, other, layer_inputs, recip, *upstream, gain, *extra)
+
+
+def weights_kernel(count, groups, *refs):
+    normed = refs[:count]
+    upstream = refs[count : 2 * count]
+    factors = refs[2 * count : 3 * count]
+    wq_ref, wk_ref, wv_ref, wo_ref = refs[-4:]
+    q_width, k_width = (wq_ref.shape[2], wk_ref.shape[2])
+    widths = (q_width, k_width, k_width)
+    start = 0
+    for out_ref, width in zip((wq_ref, wk_ref, wv_ref), widths):
+        total = 0.0
+        for member in range(count):
+            total += contract_rows(normed[member][...], factors[member][:, start : start + width])
+        out_ref[0] = total / groups
+        start += width
+    total = 0.0
+    for member in range(count):
+        total += contract_rows(factors[member][:, start:], upstream[member][...])
+    wo_ref[0] = total / groups
+
+
+def weights_call(layer, layers, normed, upstream, factors, q_width, k_width, earlier):
+    count = len(normed)
+    length, width = normed[0].shape
+    tile = width // 3
+    piece = pl.BlockSpec((length, tile), lambda n: (0, n))
+    factor = pl.BlockSpec(factors[0].shape, lambda n: (0, 0))
+    any_spec = pl.BlockSpec(memory_space=pl.ANY)
+    extra = [] if earlier is None else list(earlier)
+    f32 = jnp.float32
+
+    def tall(columns):
+        return pl.BlockSpec((1, tile, columns), lambda n: (layer, n, 0))
+
+    return pl.pallas_call(
+        functools.partial(weights_kernel, count, count),
+        grid=(width // tile,),
+        in_specs=[piece] * (2 * count) + [factor] * count + [any_spec] * len(extra),
+        out_specs=[
+            tall(q_width),
+            tall(k_width),
+            tall(k_width),
+            pl.BlockSpec((1, q_width, tile), lambda n: (layer, 0, n)),
+        ],
+        out_shape=[
+            jax.ShapeDtypeStruct((layers, width, q_width), f32),
+            jax.ShapeDtypeStruct((layers, width, k_width), f32),
+            jax.ShapeDtypeStruct((layers, width, k_width), f32),
+            jax.ShapeDtypeStruct((layers, q_width, width), f32),
+        ],
+        input_output_aliases={3 * count + i: i for i in range(len(extra))},
+        cost_estimate=pl.CostEstimate(
+            flops=4 * count * length * width * (q_width + k_width),
+            transcendentals=0,
+            bytes_accessed=24 << 20,
+        ),
+    )(*normed, *upstream, *factors, *extra)
+
+
+def xor_send(x, axis, mask):
+    return lax.ppermute(x, axis, [(i, i ^ mask) for i in range(lax.axis_size(axis))])
+
+
+def spread_pieces(pieces):
+    return [pieces[0]] + [
+        xor_send(piece, "dp", mask)
+        for mask, piece in enumerate(pieces)
+        if mask
+    ]
+
+
+def share_factor(factor):
+    beside = xor_send(factor, "dp", 1)
+    across = xor_send(factor, "dp", 2)
+    return [factor, beside, across, xor_send(across, "dp", 1)]
+
+
+def along_line(x, pairs):
+    return lax.ppermute(
+        x, "tp", [(2 * a + side, 2 * b + side) for a, b in pairs for side in range(2)]
+    )
+
+
+def rounded_sum(left, right):
+    return (left.astype(jnp.float32) + right.astype(jnp.float32)).astype(jnp.bfloat16)
+
+
+def after(value, *earlier):
+    return lax.optimization_barrier((value, *earlier))[0]
+
+
+class Wave:
+    def __init__(self, sent, kept, outer):
+        self.outer = outer
+        self.value = list(kept)
+        self.moved = [xor_send(part, "tp", 1) for part in sent]
+        self.last = None
+
+    def tie(self, value):
+        return value if self.last is None else after(value, self.last)
+
+    def step(self, chunk, stage):
+        value, moved = (self.value[chunk], self.tie(self.moved[chunk]))
+        if stage == 3:
+            value = jnp.where(self.outer, moved, value)
+        else:
+            value = rounded_sum(value, moved)
+        self.value[chunk] = self.last = value
+        if stage == 0:
+            self.moved[chunk] = along_line(value, [(0, 1), (3, 2)])
+        elif stage == 1:
+            self.moved[chunk] = along_line(value, [(1, 2), (2, 1)])
+        elif stage == 2:
+            self.moved[chunk] = along_line(value, [(1, 0), (2, 3)])
+        else:
+            self.moved[chunk] = xor_send(value, "tp", 1)
+
+
+def local(layer_inputs, out_grad, gain, w_query, w_key, w_value, w_out, doc_lengths, window_reach):
+    if w_query.shape[2] == HD or lax.axis_size("dp") != 4 or lax.axis_size("tp") != 8:
+        return local_general(
+            layer_inputs, out_grad, gain, w_query, w_key, w_value, w_out, doc_lengths, window_reach
+        )
+    count = lax.axis_size("dp")
+    rank = lax.axis_index("dp").astype(jnp.int32).reshape(1)
+    chunks = 4
+    layers = layer_inputs.shape[0]
+    length = layer_inputs.shape[1]
+    q_width, k_width = (w_query.shape[2], w_key.shape[2])
+    cosine, sine = rope_wide(length, HD)
+    forwards, normed = ([None] * layers, [None] * layers)
+    place = lax.axis_index("tp")
+    side = (place % 2).astype(jnp.int32).reshape(1)
+    line = place // 2
+    outer = (line == 0) | (line == 3)
+
+    def forward(layer, inputs):
+        result = forward_call(
+            layer, count, rank, inputs, gain, w_query, w_key, w_value, doc_lengths, window_reach,
+            cosine, sine,
+        )
+        forwards[layer] = result
+        normed[layer] = spread_pieces(result[:count])
+        return result[0]
+
+    def weights(layer, factors, sent, earlier):
+        return weights_call(
+            layer, layers, normed[layer], sent, factors, q_width, k_width, earlier
+        )
+
+    upstream = [out_grad]
+    waiting = None
+    grads = None
+    gains = [None] * layers
+    top = layers - 1
+    for layer in reversed(range(layers)):
+        if layer == top:
+            forward(top, layer_inputs)
+        factor, *partial = attention_call(
+            layer, count, chunks, side, rank, upstream, w_out, forwards[layer], cosine, sine, w_query,
+            w_key, w_value,
+        )
+        factors = share_factor(factor)
+        sent = spread_pieces(partial[2 * chunks :] or upstream)
+        wave = Wave(partial[:chunks], partial[chunks : 2 * chunks], outer)
+        if layer:
+            wave.last = forward(layer - 1, after(layer_inputs, factor))
+        if waiting is not None:
+            grads = weights(waiting[0], waiting[1], [after(waiting[2][0], factor)] + waiting[2][1:], grads)
+            wave.last = grads[1]
+        result = None
+        for slot in range(chunks + 5):
+            for stage in range(5):
+                chunk = slot - stage
+                if not 0 <= chunk < chunks:
+                    continue
+                if stage < 4:
+                    wave.step(chunk, stage)
+                    continue
+                result = norm_call(
+                    layer, chunk, side, rank, wave.value[chunk], wave.tie(wave.moved[chunk]),
+                    layer_inputs, forwards[layer][-1], upstream, gain, layer == 0, result,
+                )
+                wave.last = result[-1]
+        *upstream, gain_part = result
+        waiting = (layer, factors, sent)
+        gain_row = jnp.sum(gain_part, axis=0, keepdims=True)
+        beside = xor_send(gain_row, "dp", 1)
+        across, corner = (xor_send(gain_row, "dp", 2), xor_send(gain_row, "dp", 3))
+        gains[layer] = ((gain_row + beside) + (across + corner)) / count
+    grads = weights(waiting[0], waiting[1], waiting[2], grads)
+    return (upstream[0], *grads, jnp.concatenate(gains, axis=0))
+
+
 def solution(mesh):
     in_specs = (
         P(None, "dp", None),
@@ -295,4 +912,5 @@
         P(None, "tp", "dp"),
         P(),
     )
+
     return jax.shard_map(local, mesh=mesh, in_specs=in_specs, out_specs=out_specs, check_vma=False)

time: 688 us -> 424 us (0.62)
  waiting for transfers between devices: 340 us -> 156 us
  Pallas kernels: 0 us -> 133 us
  starting transfers between devices: 1.18 us -> 112 us
  matrix products: 110 us -> 0 us
  local copies, waits for them, and re-layouts: 100 us -> 2.91 us
  other arithmetic: 72.7 us -> 9.31 us
  blocking collectives: 40.8 us -> 0 us
  between operations: 15.6 us -> 1.88 us
    ppermute x0 -> x64, waiting for transfers between devices: none -> 156 us  [the longest x24 97.7 us: along_line(): lax.ppermute(x, 'tp', [(2 * a + side, 2 * b + side) for a, b in pairs for...]
    psum x2 -> x0, waiting for transfers between devices: 156 us -> none  [local(): whole_grad = lax.psum(totals.astype(jnp.bfloat16), 'tp').astype(jnp.float32)]
    pallas_call x0 -> x14, Pallas kernels: none -> 133 us  [the longest x2 38.8 us: attention_call(): pl.pallas_call(functools.partial(attention_kernel, flat, chunks), grid_sp...]
    ppermute x0 -> x64, starting transfers between devices: none -> 112 us  [the longest x24 73.4 us: along_line(): lax.ppermute(x, 'tp', [(2 * a + side, 2 * b + side) for a, b in pairs for...]
    dot_general x42 -> x0, matrix products: 110 us -> none  [the longest x12 49.3 us: contract_rows(): lax.dot_general(left_side, right_side, (((0,), (0,)), ((), ())), preferre...]
    reduce_scatter x3 -> x0, waiting for transfers between devices: 107 us -> none  [the longest x1 64.4 us: local(): lax.psum_scatter(stacks[0].astype(jnp.bfloat16), 'dp', scatter_dimension=...]
    unnamed x7 -> x0, waiting for transfers between devices: 77.7 us -> none
    unnamed x152 -> x62, local copies, waits for them, and re-layouts: 52.1 us -> 1.56 us
  transfers between devices with their start and end apart: 6 -> 64, of which waited for: 5 -> 25; matrix products, arithmetic and copies ran while one was open for 23% -> 2% of each run, Pallas kernels for 0% -> 23%
where the time goes in v1:
time: 424 us; the launch traced here: 416 us
  waiting for transfers between devices  156 us (37%)
  Pallas kernels  133 us (31%)
  starting transfers between devices  112 us (26%)
  other arithmetic  9.31 us (2%)
    ppermute x24, waiting for transfers between devices, along_line(): lax.ppermute(x, 'tp', [(2 * a + side, 2 * b + side) for a, b in pairs for...  97.7 us
    ppermute x24, starting transfers between devices, along_line(): lax.ppermute(x, 'tp', [(2 * a + side, 2 * b + side) for a, b in pairs for...  73.4 us
    ppermute x40, waiting for transfers between devices, xor_send(): lax.ppermute(x, axis, [(i, i ^ mask) for i in range(lax.axis_size(axis))])  58.5 us
    pallas_call x2, Pallas kernels, attention_call(): pl.pallas_call(functools.partial(attention_kernel, flat, chunks), grid_sp...  38.8 us
    ppermute x40, starting transfers between devices, xor_send(): lax.ppermute(x, axis, [(i, i ^ mask) for i in range(lax.axis_size(axis))])  38.4 us
    pallas_call x8, Pallas kernels, norm_call(): pl.pallas_call(functools.partial(norm_kernel, layer, flat, keep, steps),...  34.9 us
    pallas_call x2, Pallas kernels, forward_call(): pl.pallas_call(functools.partial(forward_kernel, layer, scale), grid_spec...  34.1 us
    pallas_call x2, Pallas kernels, weights_call(): pl.pallas_call(functools.partial(weights_kernel, count, count), grid=(wid...  25.7 us
  transfers between devices with their start and end apart: 64, of which 25 were waited for; matrix products, arithmetic and copies ran while one was open for 2% of the time, Pallas kernels for 23%

profile of v1, /device:TPU:0, one launch (start us, length us, event | category | flops | bytes accessed | tf_op | source)
XLA Modules:
  0.0 415.6 jit_solution(12142424199235023765)
XLA Ops:
  0.6 16.8 %shard_map.154 = (bf16[384,1152]{1,0:T(8,128)(2,1)}, bf16[384,1152]{1,0:T(8,128)(2,1)}, bf16[384,1152]{1,0:T(8,128)(2,1)}, bf16[384,1152]{1,0:T(8,128)(2,1)}, bf...) custom-call(s32[1]{0:T(128)} %bitcast.1.rank, ...), custom_call_target="tpu_custom_call" | custom-call | flops 3623878656 | bytes 20971520 | tf_op jit(solution)/shard_map/pallas_call | solution.py:407
  17.5 20.1 %shard_map.155 = (bf16[384,1536]{1,0:T(8,128)(2,1)}, bf16[2,96,1152]{2,1,0:T(8,128)(2,1)}, bf16[2,96,1152]{2,1,0:T(8,128)(2,1)}, bf16[2,96,1152]{2,1,0:T(8,128)(...) custom-call(s32[1]{0:T(128)} %bitcast.side, ...), custom_call_target="tpu_custom_call" | custom-call | flops 5435817984 | bytes 20971520 | tf_op jit(solution)/shard_map/pallas_call | solution.py:575
  37.6 3.2 collective-permute-start.1
  40.8 1.9 collective-permute-start.6
  42.9 1.8 collective-permute-start.29
  44.7 17.2 %shard_map.156 = (bf16[384,1152]{1,0:T(8,128)(2,1)}, bf16[384,1152]{1,0:T(8,128)(2,1)}, bf16[384,1152]{1,0:T(8,128)(2,1)}, bf16[384,1152]{1,0:T(8,128)(2,1)}, bf...) custom-call(s32[1]{0:T(128)} %bitcast.1.rank, ...), custom_call_target="tpu_custom_call" | custom-call | flops 3623878656 | bytes 20971520 | tf_op jit(solution)/shard_map/pallas_call | solution.py:407
  62.2 3.5 collective-permute-start.2
  65.8 9.9 %collective-permute-done.2 = bf16[2,96,1152]{2,1,0:T(8,128)(2,1)S(1)} collective-permute-done((bf16[2,96,1152]{2,1,0:T(8,128)(2,1)S(1)}, bf16[2,96,1152]{2,1,0:T(8,128)(2,1)S(1)}, u32[]{:S(2)}, u32[]{:S(2)}) %collective-permute-start.2) | collective-permute-done | bytes 442400 | tf_op jit(solution)/shard_map/ppermute | solution.py:779
  76.3 4.4 %collective-permute-start.5 = (bf16[2,96,1152]{2,1,0:T(8,128)(2,1)S(1)}, bf16[2,96,1152]{2,1,0:T(8,128)(2,1)S(1)}, u32[]{:S(2)}, u32[]{:S(2)}) collective-permute-start(bf16[2,96,1152]{2,1,0:T(8,128)(2,1)S(1)} %add_convert_fusion.22), channel_id=1, source_target_pairs={{0,2},{1,3},{6,4},{7,5},{8,10},{9,11},{14,12},{15,13},{16,18},{17,... | collective-permute-start | bytes 1327112 | tf_op jit(solution)/shard_map/ppermute | solution.py:779
  80.9 8.5 %collective-permute-done.5 = bf16[2,96,1152]{2,1,0:T(8,128)(2,1)S(1)} collective-permute-done((bf16[2,96,1152]{2,1,0:T(8,128)(2,1)S(1)}, bf16[2,96,1152]{2,1,0:T(8,128)(2,1)S(1)}, u32[]{:S(2)}, u32[]{:S(2)}) %collective-permute-start.5) | collective-permute-done | bytes 442400 | tf_op jit(solution)/shard_map/ppermute | solution.py:779
  90.3 15.9 %collective-permute-start.10 = (bf16[2,96,1152]{2,1,0:T(8,128)(2,1)S(1)}, bf16[2,96,1152]{2,1,0:T(8,128)(2,1)S(1)}, u32[]{:S(2)}, u32[]{:S(2)}) collective-permute-start(bf16[2,96,1152]{2,1,0:T(8,128)(2,1)S(1)} %add_convert_fusion.20), channel_id=1, source_target_pairs={{0,2},{1,3},{6,4},{7,5},{8,10},{9,11},{14,12},{15,13},{16,18},{17,... | collective-permute-start | bytes 1327112 | tf_op jit(solution)/shard_map/ppermute | solution.py:779
  107.1 6.1 %collective-permute-done.10 = bf16[2,96,1152]{2,1,0:T(8,128)(2,1)S(1)} collective-permute-done((bf16[2,96,1152]{2,1,0:T(8,128)(2,1)S(1)}, bf16[2,96,1152]{2,1,0:T(8,128)(2,1)S(1)}, u32[]{:S(2)}, u32[]{:S(2)}) %collective-permute-start.10) | collective-permute-done | bytes 442400 | tf_op jit(solution)/shard_map/ppermute | solution.py:779
  114.7 4.6 %collective-permute-start.7 = (bf16[2,96,1152]{2,1,0:T(8,128)(2,1)S(1)}, bf16[2,96,1152]{2,1,0:T(8,128)(2,1)S(1)}, u32[]{:S(2)}, u32[]{:S(2)}) collective-permute-start(bf16[2,96,1152]{2,1,0:T(8,128)(2,1)S(1)} %add_convert_fusion.17), channel_id=1, source_target_pairs={{0,2},{1,3},{6,4},{7,5},{8,10},{9,11},{14,12},{15,13},{16,18},{17,... | collective-permute-start | bytes 1327112 | tf_op jit(solution)/shard_map/ppermute | solution.py:779
  119.4 4.6 %collective-permute-done.8 = bf16[2,96,1152]{2,1,0:T(8,128)(2,1)S(1)} collective-permute-done((bf16[2,96,1152]{2,1,0:T(8,128)(2,1)S(1)}, bf16[2,96,1152]{2,1,0:T(8,128)(2,1)S(1)}, u32[]{:S(2)}, u32[]{:S(2)}) %collective-permute-start.8) | collective-permute-done | bytes 442400 | tf_op jit(solution)/shard_map/ppermute | solution.py:779
  126.7 1.4 collective-permute-start.12
  128.3 7.2 %collective-permute-done.13 = bf16[2,96,1152]{2,1,0:T(8,128)(2,1)S(1)} collective-permute-done((bf16[2,96,1152]{2,1,0:T(8,128)(2,1)S(1)}, bf16[2,96,1152]{2,1,0:T(8,128)(2,1)S(1)}, u32[]{:S(2)}, u32[]{:S(2)}) %collective-permute-start.13) | collective-permute-done | bytes 442400 | tf_op jit(solution)/shard_map/ppermute | solution.py:779
  136.3 1.3 collective-permute-start.17
  137.6 4.2 %shard_map.157 = (bf16[384,1152]{1,0:T(8,128)(2,1)}, bf16[384,1152]{1,0:T(8,128)(2,1)}, bf16[384,1152]{1,0:T(8,128)(2,1)}, bf16[384,1152]{1,0:T(8,128)(2,1)}, f32[8,4608]{1,0:T(8,128)}) custom-call(s32[1]{0:T(128)} %bitcast.side, s32[1]{0:T(128)} %bitcast.1.rank, bf16[2,96,1152]{2,1,0:T(8,128)(2,1)} %copy-done.8, bf16[2,96,1152]{2,1,0:T(8,128)(2,1)} %copy-done.23, ...), custom_call_target="tpu_custom_call" | custom-call | flops 13271040 | bytes 4194304 | tf_op jit(solution)/shard_map/pallas_call | solution.py:675
  141.9 1.4 collective-permute-start.16
  143.4 8.9 %collective-permute-done.17 = bf16[2,96,1152]{2,1,0:T(8,128)(2,1)S(1)} collective-permute-done((bf16[2,96,1152]{2,1,0:T(8,128)(2,1)S(1)}, bf16[2,96,1152]{2,1,0:T(8,128)(2,1)S(1)}, u32[]{:S(2)}, u32[]{:S(2)}) %collective-permute-start.17) | collective-permute-done | bytes 442400 | tf_op jit(solution)/shard_map/ppermute | solution.py:779
  154.5 4.5 %shard_map.158 = (bf16[384,1152]{1,0:T(8,128)(2,1)}, bf16[384,1152]{1,0:T(8,128)(2,1)}, bf16[384,1152]{1,0:T(8,128)(2,1)}, bf16[384,1152]{1,0:T(8,128)(2,1)}, f32[8,4608]{1,0:T(8,128)}) custom-call(s32[1]{0:T(128)} %bitcast.side, s32[1]{0:T(128)} %bitcast.1.rank, ...), custom_call_target="tpu_custom_call", output_to_operand_aliasing={{0}: (8, {}), {1}: (9, {}), {2}: (10, {}), {3}: (11, {})} | custom-call | flops 13271040 | bytes 4194304 | tf_op jit(solution)/shard_map/pallas_call | solution.py:675
  159.0 3.5 collective-permute-done.15
  162.5 1.4 collective-permute-start.19
  165.2 10.1 %collective-permute-done.27.refs_7_ = bf16[384,1152]{1,0:T(8,128)(2,1)} collective-permute-done((bf16[384,1152]{1,0:T(8,128)(2,1)}, bf16[384,1152]{1,0:T(8,128)(2,1)}, u32[]{:S(2)}, u32[]{:S(2)}) %collective-permute-start.27) | collective-permute-done | bytes 884768 | tf_op jit(solution)/shard_map/ppermute | solution.py:761
  177.3 4.9 %collective-permute-done.18.other_ref = bf16[2,96,1152]{2,1,0:T(8,128)(2,1)S(1)} collective-permute-done((bf16[2,96,1152]{2,1,0:T(8,128)(2,1)S(1)}, bf16[2,96,1152]{2,1,0:T(8,128)(2,1)S(1)}, u32[]{:S(2)}, u32[]{:S(2)}) %collective-permute-start.18) | collective-permute-done | bytes 442400 | tf_op jit(solution)/shard_map/ppermute | solution.py:761
  182.2 4.4 %shard_map.159 = (bf16[384,1152]{1,0:T(8,128)(2,1)}, bf16[384,1152]{1,0:T(8,128)(2,1)}, bf16[384,1152]{1,0:T(8,128)(2,1)}, bf16[384,1152]{1,0:T(8,128)(2,1)}, f32[8,4608]{1,0:T(8,128)}) custom-call(s32[1]{0:T(128)} %bitcast.side, s32[1]{0:T(128)} %bitcast.1.rank, ...), custom_call_target="tpu_custom_call", output_to_operand_aliasing={{0}: (8, {}), {1}: (9, {}), {2}: (10, {}), {3}: (11, {})} | custom-call | flops 13271040 | bytes 4194304 | tf_op jit(solution)/shard_map/pallas_call | solution.py:675
  186.6 4.2 %shard_map.160 = (bf16[384,1152]{1,0:T(8,128)(2,1)}, bf16[384,1152]{1,0:T(8,128)(2,1)}, bf16[384,1152]{1,0:T(8,128)(2,1)}, bf16[384,1152]{1,0:T(8,128)(2,1)}, f32[8,4608]{1,0:T(8,128)}) custom-call(s32[1]{0:T(128)} %bitcast.side, s32[1]{0:T(128)} %bitcast.1.rank, ...), custom_call_target="tpu_custom_call", output_to_operand_aliasing={{0}: (8, {}), {1}: (9, {}), {2}: (10, {}), {3}: (11, {})} | custom-call | flops 13271040 | bytes 4194304 | tf_op jit(solution)/shard_map/pallas_call | solution.py:675
  190.8 18.8 %shard_map.161 = (bf16[384,1536]{1,0:T(8,128)(2,1)}, bf16[2,96,1152]{2,1,0:T(8,128)(2,1)}, bf16[2,96,1152]{2,1,0:T(8,128)(2,1)}, bf16[2,96,1152]{2,1,0:T(8,128)(...) custom-call(s32[1]{0:T(128)} %bitcast.side, ...), custom_call_target="tpu_custom_call" | custom-call | flops 5435817984 | bytes 20971520 | tf_op jit(solution)/shard_map/pallas_call | solution.py:575
  209.7 2.0 collective-permute-start.50
  211.7 5.0 %collective-permute-done.24.refs_3_ = bf16[384,1152]{1,0:T(8,128)(2,1)} collective-permute-done((bf16[384,1152]{1,0:T(8,128)(2,1)}, bf16[384,1152]{1,0:T(8,128)(2,1)}, u32[]{:S(2)}, u32[]{:S(2)}) %collective-permute-start.24) | collective-permute-done | bytes 884768 | tf_op jit(solution)/shard_map/ppermute | solution.py:761
  217.4 1.4 collective-permute-start.21
  219.4 12.8 %shard_map.162 = (f32[2,1152,512]{2,1,0:T(8,128)}, f32[2,1152,256]{2,1,0:T(8,128)}, f32[2,1152,256]{2,1,0:T(8,128)}, f32[2,512,1152]{2,1,0:T(8,128)}) custom-call(bf16[384,1152]{1,0:T(8,128)(2,1)} %get-tuple-element.195.refs_0_, bf16[384,1152]{1,0:T(8,128)(2,1)} %collective-permute-done.22.refs_1_, bf16[384,1152]{1,0:T(8,128)(2,1)} %collective-permute-done.23.refs_2_, ...), custom_call_target="tpu_custom_call" | custom-call | flops 5435817984 | bytes 25165824 | tf_op jit(solution)/shard_map/pallas_call | solution.py:735
  232.2 1.5 collective-permute-start.35
  233.9 6.0 %collective-permute-done.32 = bf16[2,96,1152]{2,1,0:T(8,128)(2,1)S(1)} collective-permute-done((bf16[2,96,1152]{2,1,0:T(8,128)(2,1)}, bf16[2,96,1152]{2,1,0:T(8,128)(2,1)S(1)}, u32[]{:S(2)}, u32[]{:S(2)}) %collective-permute-start.32) | collective-permute-done | bytes 442400 | tf_op jit(solution)/shard_map/ppermute | solution.py:761
  239.9 4.9 %collective-permute-start.31 = (bf16[2,96,1152]{2,1,0:T(8,128)(2,1)S(1)}, bf16[2,96,1152]{2,1,0:T(8,128)(2,1)S(1)}, u32[]{:S(2)}, u32[]{:S(2)}) collective-permute-start(bf16[2,96,1152]{2,1,0:T(8,128)(2,1)S(1)} %add_convert_fusion.11), channel_id=1, source_target_pairs={{0,2},{1,3},{6,4},{7,5},{8,10},{9,11},{14,12},{15,13},{16,18},{17,... | collective-permute-start | bytes 1327112 | tf_op jit(solution)/shard_map/ppermute | solution.py:779
  244.9 8.9 %collective-permute-done.31 = bf16[2,96,1152]{2,1,0:T(8,128)(2,1)S(1)} collective-permute-done((bf16[2,96,1152]{2,1,0:T(8,128)(2,1)S(1)}, bf16[2,96,1152]{2,1,0:T(8,128)(2,1)S(1)}, u32[]{:S(2)}, u32[]{:S(2)}) %collective-permute-start.31) | collective-permute-done | bytes 442400 | tf_op jit(solution)/shard_map/ppermute | solution.py:779
  253.8 1.4 collective-permute-start.20
  255.4 4.4 %collective-permute-start.34 = (bf16[2,96,1152]{2,1,0:T(8,128)(2,1)S(1)}, bf16[2,96,1152]{2,1,0:T(8,128)(2,1)S(1)}, u32[]{:S(2)}, u32[]{:S(2)}) collective-permute-start(bf16[2,96,1152]{2,1,0:T(8,128)(2,1)S(1)} %add_convert_fusion.10), channel_id=1, source_target_pairs={{0,2},{1,3},{6,4},{7,5},{8,10},{9,11},{14,12},{15,13},{16,18},{17,... | collective-permute-start | bytes 1327112 | tf_op jit(solution)/shard_map/ppermute | solution.py:779
  259.9 7.9 %collective-permute-done.34 = bf16[2,96,1152]{2,1,0:T(8,128)(2,1)S(1)} collective-permute-done((bf16[2,96,1152]{2,1,0:T(8,128)(2,1)S(1)}, bf16[2,96,1152]{2,1,0:T(8,128)(2,1)S(1)}, u32[]{:S(2)}, u32[]{:S(2)}) %collective-permute-start.34) | collective-permute-done | bytes 442400 | tf_op jit(solution)/shard_map/ppermute | solution.py:779
  268.6 15.1 %collective-permute-start.39 = (bf16[2,96,1152]{2,1,0:T(8,128)(2,1)S(1)}, bf16[2,96,1152]{2,1,0:T(8,128)(2,1)S(1)}, u32[]{:S(2)}, u32[]{:S(2)}) collective-permute-start(bf16[2,96,1152]{2,1,0:T(8,128)(2,1)S(1)} %add_convert_fusion.8), channel_id=1, source_target_pairs={{0,2},{1,3},{6,4},{7,5},{8,10},{9,11},{14,12},{15,13},{16,18},{17,... | collective-permute-start | bytes 1327112 | tf_op jit(solution)/shard_map/ppermute | solution.py:779
  284.7 5.3 %collective-permute-done.39 = bf16[2,96,1152]{2,1,0:T(8,128)(2,1)S(1)} collective-permute-done((bf16[2,96,1152]{2,1,0:T(8,128)(2,1)S(1)}, bf16[2,96,1152]{2,1,0:T(8,128)(2,1)S(1)}, u32[]{:S(2)}, u32[]{:S(2)}) %collective-permute-start.39) | collective-permute-done | bytes 442400 | tf_op jit(solution)/shard_map/ppermute | solution.py:779
  291.4 4.8 %collective-permute-start.36 = (bf16[2,96,1152]{2,1,0:T(8,128)(2,1)S(1)}, bf16[2,96,1152]{2,1,0:T(8,128)(2,1)S(1)}, u32[]{:S(2)}, u32[]{:S(2)}) collective-permute-start(bf16[2,96,1152]{2,1,0:T(8,128)(2,1)S(1)} %add_convert_fusion.5), channel_id=1, source_target_pairs={{0,2},{1,3},{6,4},{7,5},{8,10},{9,11},{14,12},{15,13},{16,18},{17,... | collective-permute-start | bytes 1327112 | tf_op jit(solution)/shard_map/ppermute | solution.py:779
  296.4 3.8 collective-permute-done.37
  304.0 8.0 %collective-permute-done.42 = bf16[2,96,1152]{2,1,0:T(8,128)(2,1)S(1)} collective-permute-done((bf16[2,96,1152]{2,1,0:T(8,128)(2,1)S(1)}, bf16[2,96,1152]{2,1,0:T(8,128)(2,1)S(1)}, u32[]{:S(2)}, u32[]{:S(2)}) %collective-permute-start.42) | collective-permute-done | bytes 442400 | tf_op jit(solution)/shard_map/ppermute | solution.py:779
  312.8 1.3 collective-permute-start.46
  314.1 4.3 %shard_map.163 = (bf16[384,4608]{1,0:T(8,128)(2,1)}, f32[8,4608]{1,0:T(8,128)}) custom-call(s32[1]{0:T(128)} %bitcast.side, s32[1]{0:T(128)} %bitcast.1.rank, bf16[2,96,1152]{2,1,0:T(8,128)(2,1)} %copy-done.9, bf16[2,96,1152]{2,1,0:T(8,128)(2,1)} %copy-done.24, bf16[2,384,4608]{2,1,0:T(8,128)(2,1)} %x_ref.18, f32[384,128]{1,0:T(8,128)} %get-tuple-element.224.recip_ref, ...), custom_call_target="tpu_custom_call" | custom-call | flops 13271040 | bytes 4194304 | tf_op jit(solution)/shard_map/pallas_call | solution.py:675
  319.2 9.9 %collective-permute-done.46 = bf16[2,96,1152]{2,1,0:T(8,128)(2,1)S(1)} collective-permute-done((bf16[2,96,1152]{2,1,0:T(8,128)(2,1)S(1)}, bf16[2,96,1152]{2,1,0:T(8,128)(2,1)S(1)}, u32[]{:S(2)}, u32[]{:S(2)}) %collective-permute-start.46) | collective-permute-done | bytes 442400 | tf_op jit(solution)/shard_map/ppermute | solution.py:779
  331.2 4.5 %shard_map.164 = (bf16[384,4608]{1,0:T(8,128)(2,1)}, f32[8,4608]{1,0:T(8,128)}) custom-call(s32[1]{0:T(128)} %bitcast.side, s32[1]{0:T(128)} %bitcast.1.rank, bf16[2,96,1152]{2,1,0:T(8,128)(2,1)} %copy-done.7, bf16[2,96,1152]{2,1,0:T(8,128)(2,1)} %copy-done.22, bf16[2,384,4608]{2,1,0:T(8,128)(2,1)} %x_ref.18, ...), custom_call_target="tpu_custom_call", output_to_operand_aliasing={{0}: (11, {})} | custom-call | flops 13271040 | bytes 4194304 | tf_op jit(solution)/shard_map/pallas_call | solution.py:675
  335.7 3.6 collective-permute-done.44
  339.9 1.8 broadcast_select_fusion.own_ref
  341.7 1.4 collective-permute-start.47
  344.2 1.8 collective-permute-start.61
  346.0 1.8 collective-permute-done.51.refs_3_
  347.8 5.1 %collective-permute-start.55 = (bf16[384,1536]{1,0:T(8,128)(2,1)}, bf16[384,1536]{1,0:T(8,128)(2,1)}, u32[]{:S(2)}, u32[]{:S(2)}) collective-permute-start(bf16[384,1536]{1,0:T(8,128)(2,1)} %get-tuple-element.200.refs_8_), channel_id=1, source_target_pairs={{0,8},{8,0},{16,24},{24,16},{1,9},{9,1},{17,25},{25,17},{2,10},{10... | collective-permute-start | bytes 3538952 | tf_op jit(solution)/shard_map/ppermute | solution.py:761
  353.8 2.9 collective-permute-done.62
  356.7 3.3 collective-permute-done.63
  361.9 1.4 add_multiply_fusion
  363.3 4.4 %shard_map.165 = (bf16[384,4608]{1,0:T(8,128)(2,1)}, f32[8,4608]{1,0:T(8,128)}) custom-call(s32[1]{0:T(128)} %bitcast.side, s32[1]{0:T(128)} %bitcast.1.rank, bf16[2,96,1152]{2,1,0:T(8,128)(2,1)} %copy-done.3, bf16[2,96,1152]{2,1,0:T(8,128)(2,1)} %collective-permute-done.48.other_ref, ...), custom_call_target="tpu_custom_call", output_to_operand_aliasing={{0}: (11, {})} | custom-call | flops 13271040 | bytes 4194304 | tf_op jit(solution)/shard_map/pallas_call | solution.py:675
  367.6 4.4 %shard_map.166 = (bf16[384,4608]{1,0:T(8,128)(2,1)}, f32[8,4608]{1,0:T(8,128)}) custom-call(s32[1]{0:T(128)} %bitcast.side, s32[1]{0:T(128)} %bitcast.1.rank, bf16[2,96,1152]{2,1,0:T(8,128)(2,1)} %broadcast_select_fusion.own_ref, bf16[2,96,1152]{2,1,0:T(8,128)(2,1)} %collective-permute-done.47.other_ref, ...), custom_call_target="tpu_custom_call", output_to_operand_aliasing={{0}: (11, {})} | custom-call | flops 13271040 | bytes 4194304 | tf_op jit(solution)/shard_map/pallas_call | solution.py:675
  372.0 1.6 reduce_sum.18
  373.6 1.3 broadcast_in_dim.6
  375.3 7.4 %collective-permute-done.53.refs_6_ = bf16[384,1152]{1,0:T(8,128)(2,1)S(1)} collective-permute-done((bf16[384,1152]{1,0:T(8,128)(2,1)S(1)}, bf16[384,1152]{1,0:T(8,128)(2,1)S(1)}, u32[]{:S(2)}, u32[]{:S(2)}) %collective-permute-start.53) | collective-permute-done | bytes 884768 | tf_op jit(solution)/shard_map/ppermute | solution.py:761
  383.4 17.2 %collective-permute-done.54.refs_7_ = bf16[384,1152]{1,0:T(8,128)(2,1)} collective-permute-done((bf16[384,1152]{1,0:T(8,128)(2,1)S(1)}, bf16[384,1152]{1,0:T(8,128)(2,1)}, u32[]{:S(2)}, u32[]{:S(2)}) %collective-permute-start.54) | collective-permute-done | bytes 884768 | tf_op jit(solution)/shard_map/ppermute | solution.py:761
  401.7 12.9 %shard_map.167 = (f32[2,1152,512]{2,1,0:T(8,128)}, f32[2,1152,256]{2,1,0:T(8,128)}, f32[2,1152,256]{2,1,0:T(8,128)}, f32[2,512,1152]{2,1,0:T(8,128)}) custom-call(bf16[384,1152]{1,0:T(8,128)(2,1)} %get-tuple-element.140.refs_0_, ...), custom_call_target="tpu_custom_call", output_to_operand_aliasing={{0}: (12, {}), {1}: (13, {}), {2}: (14, {}), {3}: (15, {})} | custom-call | flops 5435817984 | bytes 25165824 | tf_op jit(solution)/shard_map/pallas_call | solution.py:735
  (179 shorter events, 33.1 us)
Async XLA Ops:
  37.6 24.4 %collective-permute-start.1 = (bf16[2,96,1152]{2,1,0:T(8,128)(2,1)}, bf16[2,96,1152]{2,1,0:T(8,128)(2,1)S(1)}, u32[]{:S(2)}, u32[]{:S(2)}) collective-permute-start(bf16[2,96,1152]{2,1,0:T(8,128)(2,1)} %get-tuple-element.137), channel_id=1, source_target_pairs={{0,1},{1,0},{2,3},{3,2},{4,5},{5,4},{6,7},{7,6},{8,9},{9,8},{10,11... | collective-permute-start | bytes 1327112 | tf_op jit(solution)/shard_map/ppermute | solution.py:761
  40.8 21.4 %collective-permute-start.3 = (bf16[2,96,1152]{2,1,0:T(8,128)(2,1)}, bf16[2,96,1152]{2,1,0:T(8,128)(2,1)S(1)}, u32[]{:S(2)}, u32[]{:S(2)}) collective-permute-start(bf16[2,96,1152]{2,1,0:T(8,128)(2,1)} %get-tuple-element.143), channel_id=1, source_target_pairs={{0,1},{1,0},{2,3},{3,2},{4,5},{5,4},{6,7},{7,6},{8,9},{9,8},{10,11... | collective-permute-start | bytes 1327112 | tf_op jit(solution)/shard_map/ppermute | solution.py:761
  40.8 35.5 %collective-permute-start.6 = (bf16[2,96,1152]{2,1,0:T(8,128)(2,1)}, bf16[2,96,1152]{2,1,0:T(8,128)(2,1)S(1)}, u32[]{:S(2)}, u32[]{:S(2)}) collective-permute-start(bf16[2,96,1152]{2,1,0:T(8,128)(2,1)} %get-tuple-element.147), channel_id=1, source_target_pairs={{0,1},{1,0},{2,3},{3,2},{4,5},{5,4},{6,7},{7,6},{8,9},{9,8},{10,11... | collective-permute-start | bytes 1327112 | tf_op jit(solution)/shard_map/ppermute | solution.py:761
  42.8 63.5 %collective-permute-start = (bf16[2,96,1152]{2,1,0:T(8,128)(2,1)}, bf16[2,96,1152]{2,1,0:T(8,128)(2,1)S(1)}, u32[]{:S(2)}, u32[]{:S(2)}) collective-permute-start(bf16[2,96,1152]{2,1,0:T(8,128)(2,1)} %get-tuple-element.135), channel_id=1, source_target_pairs={{0,1},{1,0},{2,3},{3,2},{4,5},{5,4},{6,7},{7,6},{8,9},{9,8},{10,11... | collective-permute-start | bytes 1327112 | tf_op jit(solution)/shard_map/ppermute | solution.py:761
  42.9 121.8 %collective-permute-start.29 = (bf16[384,1536]{1,0:T(8,128)(2,1)}, bf16[384,1536]{1,0:T(8,128)(2,1)}, u32[]{:S(2)}, u32[]{:S(2)}) collective-permute-start(bf16[384,1536]{1,0:T(8,128)(2,1)} %get-tuple-element.138.refs_8_), channel_id=1, source_target_pairs={{0,16},{8,24},{16,0},{24,8},{1,17},{9,25},{17,1},{25,9},{2,18},{10... | collective-permute-start | bytes 3538952 | tf_op jit(solution)/shard_map/ppermute | solution.py:761
  62.0 102.1 %collective-permute-start.25 = (bf16[384,1152]{1,0:T(8,128)(2,1)}, bf16[384,1152]{1,0:T(8,128)(2,1)}, u32[]{:S(2)}, u32[]{:S(2)}) collective-permute-start(bf16[384,1152]{1,0:T(8,128)(2,1)} %get-tuple-element.202), channel_id=1, source_target_pairs={{0,8},{8,0},{16,24},{24,16},{1,9},{9,1},{17,25},{25,17},{2,10},{10... | collective-permute-start | bytes 2654216 | tf_op jit(solution)/shard_map/ppermute | solution.py:761
  62.2 13.5 %collective-permute-start.2 = (bf16[2,96,1152]{2,1,0:T(8,128)(2,1)S(1)}, bf16[2,96,1152]{2,1,0:T(8,128)(2,1)S(1)}, u32[]{:S(2)}, u32[]{:S(2)}) collective-permute-start(bf16[2,96,1152]{2,1,0:T(8,128)(2,1)S(1)} %add_convert_fusion.23), channel_id=1, source_target_pairs={{0,2},{1,3},{6,4},{7,5},{8,10},{9,11},{14,12},{15,13},{16,18},{17,... | collective-permute-start | bytes 1327112 | tf_op jit(solution)/shard_map/ppermute | solution.py:779
  75.7 89.0 %collective-permute-start.26 = (bf16[384,1152]{1,0:T(8,128)(2,1)}, bf16[384,1152]{1,0:T(8,128)(2,1)}, u32[]{:S(2)}, u32[]{:S(2)}) collective-permute-start(bf16[384,1152]{1,0:T(8,128)(2,1)} %get-tuple-element.203), channel_id=1, source_target_pairs={{0,16},{8,24},{16,0},{24,8},{1,17},{9,25},{17,1},{25,9},{2,18},{10... | collective-permute-start | bytes 2654216 | tf_op jit(solution)/shard_map/ppermute | solution.py:761
  76.3 13.1 %collective-permute-start.5 = (bf16[2,96,1152]{2,1,0:T(8,128)(2,1)S(1)}, bf16[2,96,1152]{2,1,0:T(8,128)(2,1)S(1)}, u32[]{:S(2)}, u32[]{:S(2)}) collective-permute-start(bf16[2,96,1152]{2,1,0:T(8,128)(2,1)S(1)} %add_convert_fusion.22), channel_id=1, source_target_pairs={{0,2},{1,3},{6,4},{7,5},{8,10},{9,11},{14,12},{15,13},{16,18},{17,... | collective-permute-start | bytes 1327112 | tf_op jit(solution)/shard_map/ppermute | solution.py:779
  89.4 0.8 collective-permute-start.4
  90.3 23.0 %collective-permute-start.10 = (bf16[2,96,1152]{2,1,0:T(8,128)(2,1)S(1)}, bf16[2,96,1152]{2,1,0:T(8,128)(2,1)S(1)}, u32[]{:S(2)}, u32[]{:S(2)}) collective-permute-start(bf16[2,96,1152]{2,1,0:T(8,128)(2,1)S(1)} %add_convert_fusion.20), channel_id=1, source_target_pairs={{0,2},{1,3},{6,4},{7,5},{8,10},{9,11},{14,12},{15,13},{16,18},{17,... | collective-permute-start | bytes 1327112 | tf_op jit(solution)/shard_map/ppermute | solution.py:779
  106.3 8.3 %collective-permute-start.9 = (bf16[2,96,1152]{2,1,0:T(8,128)(2,1)S(1)}, bf16[2,96,1152]{2,1,0:T(8,128)(2,1)S(1)}, u32[]{:S(2)}, u32[]{:S(2)}) collective-permute-start(bf16[2,96,1152]{2,1,0:T(8,128)(2,1)S(1)} %add_convert_fusion.19), channel_id=1, source_target_pairs={{2,4},{3,5},{4,2},{5,3},{10,12},{11,13},{12,10},{13,11},{18,20},{1... | collective-permute-start | bytes 1327112 | tf_op jit(solution)/shard_map/ppermute | solution.py:779
  113.3 10.7 %collective-permute-start.8 = (bf16[2,96,1152]{2,1,0:T(8,128)(2,1)S(1)}, bf16[2,96,1152]{2,1,0:T(8,128)(2,1)S(1)}, u32[]{:S(2)}, u32[]{:S(2)}) collective-permute-start(bf16[2,96,1152]{2,1,0:T(8,128)(2,1)S(1)} %add_convert_fusion.18), channel_id=1, source_target_pairs={{2,0},{3,1},{4,6},{5,7},{10,8},{11,9},{12,14},{13,15},{18,16},{19,... | collective-permute-start | bytes 1327112 | tf_op jit(solution)/shard_map/ppermute | solution.py:779
  114.7 10.7 %collective-permute-start.7 = (bf16[2,96,1152]{2,1,0:T(8,128)(2,1)S(1)}, bf16[2,96,1152]{2,1,0:T(8,128)(2,1)S(1)}, u32[]{:S(2)}, u32[]{:S(2)}) collective-permute-start(bf16[2,96,1152]{2,1,0:T(8,128)(2,1)S(1)} %add_convert_fusion.17), channel_id=1, source_target_pairs={{0,2},{1,3},{6,4},{7,5},{8,10},{9,11},{14,12},{15,13},{16,18},{17,... | collective-permute-start | bytes 1327112 | tf_op jit(solution)/shard_map/ppermute | solution.py:779
  124.0 2.7 collective-permute-start.14
  125.3 10.2 %collective-permute-start.13 = (bf16[2,96,1152]{2,1,0:T(8,128)(2,1)S(1)}, bf16[2,96,1152]{2,1,0:T(8,128)(2,1)S(1)}, u32[]{:S(2)}, u32[]{:S(2)}) collective-permute-start(bf16[2,96,1152]{2,1,0:T(8,128)(2,1)S(1)} %add_convert_fusion.15), channel_id=1, source_target_pairs={{2,0},{3,1},{4,6},{5,7},{10,8},{11,9},{12,14},{13,15},{18,16},{19,... | collective-permute-start | bytes 1327112 | tf_op jit(solution)/shard_map/ppermute | solution.py:779
  126.7 9.5 %collective-permute-start.12 = (bf16[2,96,1152]{2,1,0:T(8,128)(2,1)S(1)}, bf16[2,96,1152]{2,1,0:T(8,128)(2,1)S(1)}, u32[]{:S(2)}, u32[]{:S(2)}) collective-permute-start(bf16[2,96,1152]{2,1,0:T(8,128)(2,1)S(1)} %broadcast_select_fusion.7.own_ref), channel_id=1, source_target_pairs={{0,1},{1,0},{2,3},{3,2},{4,5},{5,4},{6,7},{7,6},{8,9},{9,8},{10,11... | collective-permute-start | bytes 1327112 | tf_op jit(solution)/shard_map/ppermute | solution.py:761
  135.5 6.3 %collective-permute-start.11 = (bf16[2,96,1152]{2,1,0:T(8,128)(2,1)S(1)}, bf16[2,96,1152]{2,1,0:T(8,128)(2,1)S(1)}, u32[]{:S(2)}, u32[]{:S(2)}) collective-permute-start(bf16[2,96,1152]{2,1,0:T(8,128)(2,1)S(1)} %add_convert_fusion.14), channel_id=1, source_target_pairs={{2,4},{3,5},{4,2},{5,3},{10,12},{11,13},{12,10},{13,11},{18,20},{1... | collective-permute-start | bytes 1327112 | tf_op jit(solution)/shard_map/ppermute | solution.py:779
  136.3 16.0 %collective-permute-start.17 = (bf16[2,96,1152]{2,1,0:T(8,128)(2,1)S(1)}, bf16[2,96,1152]{2,1,0:T(8,128)(2,1)S(1)}, u32[]{:S(2)}, u32[]{:S(2)}) collective-permute-start(bf16[2,96,1152]{2,1,0:T(8,128)(2,1)S(1)} %add_convert_fusion.13), channel_id=1, source_target_pairs={{2,0},{3,1},{4,6},{5,7},{10,8},{11,9},{12,14},{13,15},{18,16},{19,... | collective-permute-start | bytes 1327112 | tf_op jit(solution)/shard_map/ppermute | solution.py:779
  141.9 11.8 %collective-permute-start.16 = (bf16[2,96,1152]{2,1,0:T(8,128)(2,1)S(1)}, bf16[2,96,1152]{2,1,0:T(8,128)(2,1)S(1)}, u32[]{:S(2)}, u32[]{:S(2)}) collective-permute-start(bf16[2,96,1152]{2,1,0:T(8,128)(2,1)S(1)} %broadcast_select_fusion.6.own_ref), channel_id=1, source_target_pairs={{0,1},{1,0},{2,3},{3,2},{4,5},{5,4},{6,7},{7,6},{8,9},{9,8},{10,11... | collective-permute-start | bytes 1327112 | tf_op jit(solution)/shard_map/ppermute | solution.py:761
  152.3 10.2 %collective-permute-start.15 = (bf16[2,96,1152]{2,1,0:T(8,128)(2,1)S(1)}, bf16[2,96,1152]{2,1,0:T(8,128)(2,1)S(1)}, u32[]{:S(2)}, u32[]{:S(2)}) collective-permute-start(bf16[2,96,1152]{2,1,0:T(8,128)(2,1)S(1)} %add_convert_fusion.12), channel_id=1, source_target_pairs={{2,0},{3,1},{4,6},{5,7},{10,8},{11,9},{12,14},{13,15},{18,16},{19,... | collective-permute-start | bytes 1327112 | tf_op jit(solution)/shard_map/ppermute | solution.py:779
  153.7 21.6 %collective-permute-start.27 = (bf16[384,1152]{1,0:T(8,128)(2,1)}, bf16[384,1152]{1,0:T(8,128)(2,1)}, u32[]{:S(2)}, u32[]{:S(2)}) collective-permute-start(bf16[384,1152]{1,0:T(8,128)(2,1)} %get-tuple-element.204), channel_id=1, source_target_pairs={{0,24},{8,16},{16,8},{24,0},{1,25},{9,17},{17,9},{25,1},{2,26},{10... | collective-permute-start | bytes 2654216 | tf_op jit(solution)/shard_map/ppermute | solution.py:761
  162.5 13.5 %collective-permute-start.19 = (bf16[2,96,1152]{2,1,0:T(8,128)(2,1)S(1)}, bf16[2,96,1152]{2,1,0:T(8,128)(2,1)S(1)}, u32[]{:S(2)}, u32[]{:S(2)}) collective-permute-start(bf16[2,96,1152]{2,1,0:T(8,128)(2,1)S(1)} %broadcast_select_fusion.5.own_ref), channel_id=1, source_target_pairs={{0,1},{1,0},{2,3},{3,2},{4,5},{5,4},{6,7},{7,6},{8,9},{9,8},{10,11... | collective-permute-start | bytes 1327112 | tf_op jit(solution)/shard_map/ppermute | solution.py:761
  164.0 18.2 %collective-permute-start.18 = (bf16[2,96,1152]{2,1,0:T(8,128)(2,1)S(1)}, bf16[2,96,1152]{2,1,0:T(8,128)(2,1)S(1)}, u32[]{:S(2)}, u32[]{:S(2)}) collective-permute-start(bf16[2,96,1152]{2,1,0:T(8,128)(2,1)S(1)} %broadcast_select_fusion.4.own_ref), channel_id=1, source_target_pairs={{0,1},{1,0},{2,3},{3,2},{4,5},{5,4},{6,7},{7,6},{8,9},{9,8},{10,11... | collective-permute-start | bytes 1327112 | tf_op jit(solution)/shard_map/ppermute | solution.py:761
  164.7 52.7 %collective-permute-start.28 = (bf16[384,1536]{1,0:T(8,128)(2,1)S(1)}, bf16[384,1536]{1,0:T(8,128)(2,1)}, u32[]{:S(2)}, u32[]{:S(2)}) collective-permute-start(bf16[384,1536]{1,0:T(8,128)(2,1)S(1)} %copy-done.28), channel_id=1, source_target_pairs={{0,8},{8,0},{16,24},{24,16},{1,9},{9,1},{17,25},{25,17},{2,10},{10... | collective-permute-start | bytes 3538952 | tf_op jit(solution)/shard_map/ppermute | solution.py:761
  164.7 54.1 %collective-permute-start.30 = (bf16[384,1536]{1,0:T(8,128)(2,1)}, bf16[384,1536]{1,0:T(8,128)(2,1)}, u32[]{:S(2)}, u32[]{:S(2)}) collective-permute-start(bf16[384,1536]{1,0:T(8,128)(2,1)} %collective-permute-done.29.refs_10_), channel_id=1, source_target_pairs={{0,8},{8,0},{16,24},{24,16},{1,9},{9,1},{17,25},{25,17},{2,10},{10... | collective-permute-start | bytes 3538952 | tf_op jit(solution)/shard_map/ppermute | solution.py:761
  175.3 34.3 %collective-permute-start.22 = (bf16[384,1152]{1,0:T(8,128)(2,1)}, bf16[384,1152]{1,0:T(8,128)(2,1)}, u32[]{:S(2)}, u32[]{:S(2)}) collective-permute-start(bf16[384,1152]{1,0:T(8,128)(2,1)} %get-tuple-element.196), channel_id=1, source_target_pairs={{0,8},{8,0},{16,24},{24,16},{1,9},{9,1},{17,25},{25,17},{2,10},{10... | collective-permute-start | bytes 2654216 | tf_op jit(solution)/shard_map/ppermute | solution.py:761
  176.1 33.6 %collective-permute-start.23 = (bf16[384,1152]{1,0:T(8,128)(2,1)}, bf16[384,1152]{1,0:T(8,128)(2,1)}, u32[]{:S(2)}, u32[]{:S(2)}) collective-permute-start(bf16[384,1152]{1,0:T(8,128)(2,1)} %get-tuple-element.197), channel_id=1, source_target_pairs={{0,16},{8,24},{16,0},{24,8},{1,17},{9,25},{17,1},{25,9},{2,18},{10... | collective-permute-start | bytes 2654216 | tf_op jit(solution)/shard_map/ppermute | solution.py:761
  182.2 34.4 %collective-permute-start.24 = (bf16[384,1152]{1,0:T(8,128)(2,1)}, bf16[384,1152]{1,0:T(8,128)(2,1)}, u32[]{:S(2)}, u32[]{:S(2)}) collective-permute-start(bf16[384,1152]{1,0:T(8,128)(2,1)} %get-tuple-element.198), channel_id=1, source_target_pairs={{0,24},{8,16},{16,8},{24,0},{1,25},{9,17},{17,9},{25,1},{2,26},{10... | collective-permute-start | bytes 2654216 | tf_op jit(solution)/shard_map/ppermute | solution.py:761
  209.6 132.1 %collective-permute-start.49 = (bf16[384,1152]{1,0:T(8,128)(2,1)}, bf16[384,1152]{1,0:T(8,128)(2,1)}, u32[]{:S(2)}, u32[]{:S(2)}) collective-permute-start(bf16[384,1152]{1,0:T(8,128)(2,1)} %get-tuple-element.238), channel_id=1, source_target_pairs={{0,8},{8,0},{16,24},{24,16},{1,9},{9,1},{17,25},{25,17},{2,10},{10... | collective-permute-start | bytes 2654216 | tf_op jit(solution)/shard_map/ppermute | solution.py:761
  209.7 134.5 %collective-permute-start.50 = (bf16[384,1152]{1,0:T(8,128)(2,1)}, bf16[384,1152]{1,0:T(8,128)(2,1)}, u32[]{:S(2)}, u32[]{:S(2)}) collective-permute-start(bf16[384,1152]{1,0:T(8,128)(2,1)} %get-tuple-element.239), channel_id=1, source_target_pairs={{0,16},{8,24},{16,0},{24,8},{1,17},{9,25},{17,1},{25,9},{2,18},{10... | collective-permute-start | bytes 2654216 | tf_op jit(solution)/shard_map/ppermute | solution.py:761
  216.6 136.2 %collective-permute-start.56 = (bf16[384,1536]{1,0:T(8,128)(2,1)}, bf16[384,1536]{1,0:T(8,128)(2,1)}, u32[]{:S(2)}, u32[]{:S(2)}) collective-permute-start(bf16[384,1536]{1,0:T(8,128)(2,1)} %get-tuple-element.200.refs_8_), channel_id=1, source_target_pairs={{0,16},{8,24},{16,0},{24,8},{1,17},{9,25},{17,1},{25,9},{2,18},{10... | collective-permute-start | bytes 3538952 | tf_op jit(solution)/shard_map/ppermute | solution.py:761
  217.4 14.8 %collective-permute-start.21 = (bf16[2,96,1152]{2,1,0:T(8,128)(2,1)}, bf16[2,96,1152]{2,1,0:T(8,128)(2,1)S(1)}, u32[]{:S(2)}, u32[]{:S(2)}) collective-permute-start(bf16[2,96,1152]{2,1,0:T(8,128)(2,1)} %get-tuple-element.194), channel_id=1, source_target_pairs={{0,1},{1,0},{2,3},{3,2},{4,5},{5,4},{6,7},{7,6},{8,9},{9,8},{10,11... | collective-permute-start | bytes 1327112 | tf_op jit(solution)/shard_map/ppermute | solution.py:761
  218.9 21.0 %collective-permute-start.32 = (bf16[2,96,1152]{2,1,0:T(8,128)(2,1)}, bf16[2,96,1152]{2,1,0:T(8,128)(2,1)S(1)}, u32[]{:S(2)}, u32[]{:S(2)}) collective-permute-start(bf16[2,96,1152]{2,1,0:T(8,128)(2,1)} %get-tuple-element.208), channel_id=1, source_target_pairs={{0,1},{1,0},{2,3},{3,2},{4,5},{5,4},{6,7},{7,6},{8,9},{9,8},{10,11... | collective-permute-start | bytes 1327112 | tf_op jit(solution)/shard_map/ppermute | solution.py:761
  232.2 23.1 %collective-permute-start.35 = (bf16[2,96,1152]{2,1,0:T(8,128)(2,1)S(1)}, bf16[2,96,1152]{2,1,0:T(8,128)(2,1)S(1)}, u32[]{:S(2)}, u32[]{:S(2)}) collective-permute-start(bf16[2,96,1152]{2,1,0:T(8,128)(2,1)S(1)} %copy-done.30), channel_id=1, source_target_pairs={{0,1},{1,0},{2,3},{3,2},{4,5},{5,4},{6,7},{7,6},{8,9},{9,8},{10,11... | collective-permute-start | bytes 1327112 | tf_op jit(solution)/shard_map/ppermute | solution.py:761
  239.9 13.9 %collective-permute-start.31 = (bf16[2,96,1152]{2,1,0:T(8,128)(2,1)S(1)}, bf16[2,96,1152]{2,1,0:T(8,128)(2,1)S(1)}, u32[]{:S(2)}, u32[]{:S(2)}) collective-permute-start(bf16[2,96,1152]{2,1,0:T(8,128)(2,1)S(1)} %add_convert_fusion.11), channel_id=1, source_target_pairs={{0,2},{1,3},{6,4},{7,5},{8,10},{9,11},{14,12},{15,13},{16,18},{17,... | collective-permute-start | bytes 1327112 | tf_op jit(solution)/shard_map/ppermute | solution.py:779
  253.8 30.1 %collective-permute-start.20 = (bf16[2,96,1152]{2,1,0:T(8,128)(2,1)S(1)}, bf16[2,96,1152]{2,1,0:T(8,128)(2,1)S(1)}, u32[]{:S(2)}, u32[]{:S(2)}) collective-permute-start(bf16[2,96,1152]{2,1,0:T(8,128)(2,1)S(1)} %copy-done.29), channel_id=1, source_target_pairs={{0,1},{1,0},{2,3},{3,2},{4,5},{5,4},{6,7},{7,6},{8,9},{9,8},{10,11... | collective-permute-start | bytes 1327112 | tf_op jit(solution)/shard_map/ppermute | solution.py:761
  255.4 12.4 %collective-permute-start.34 = (bf16[2,96,1152]{2,1,0:T(8,128)(2,1)S(1)}, bf16[2,96,1152]{2,1,0:T(8,128)(2,1)S(1)}, u32[]{:S(2)}, u32[]{:S(2)}) collective-permute-start(bf16[2,96,1152]{2,1,0:T(8,128)(2,1)S(1)} %add_convert_fusion.10), channel_id=1, source_target_pairs={{0,2},{1,3},{6,4},{7,5},{8,10},{9,11},{14,12},{15,13},{16,18},{17,... | collective-permute-start | bytes 1327112 | tf_op jit(solution)/shard_map/ppermute | solution.py:779
  267.8 0.8 collective-permute-start.33
  268.6 21.4 %collective-permute-start.39 = (bf16[2,96,1152]{2,1,0:T(8,128)(2,1)S(1)}, bf16[2,96,1152]{2,1,0:T(8,128)(2,1)S(1)}, u32[]{:S(2)}, u32[]{:S(2)}) collective-permute-start(bf16[2,96,1152]{2,1,0:T(8,128)(2,1)S(1)} %add_convert_fusion.8), channel_id=1, source_target_pairs={{0,2},{1,3},{6,4},{7,5},{8,10},{9,11},{14,12},{15,13},{16,18},{17,... | collective-permute-start | bytes 1327112 | tf_op jit(solution)/shard_map/ppermute | solution.py:779
  283.9 7.6 %collective-permute-start.38 = (bf16[2,96,1152]{2,1,0:T(8,128)(2,1)S(1)}, bf16[2,96,1152]{2,1,0:T(8,128)(2,1)S(1)}, u32[]{:S(2)}, u32[]{:S(2)}) collective-permute-start(bf16[2,96,1152]{2,1,0:T(8,128)(2,1)S(1)} %add_convert_fusion.7), channel_id=1, source_target_pairs={{2,4},{3,5},{4,2},{5,3},{10,12},{11,13},{12,10},{13,11},{18,20},{1... | collective-permute-start | bytes 1327112 | tf_op jit(solution)/shard_map/ppermute | solution.py:779
  290.0 10.2 %collective-permute-start.37 = (bf16[2,96,1152]{2,1,0:T(8,128)(2,1)S(1)}, bf16[2,96,1152]{2,1,0:T(8,128)(2,1)S(1)}, u32[]{:S(2)}, u32[]{:S(2)}) collective-permute-start(bf16[2,96,1152]{2,1,0:T(8,128)(2,1)S(1)} %add_convert_fusion.6), channel_id=1, source_target_pairs={{2,0},{3,1},{4,6},{5,7},{10,8},{11,9},{12,14},{13,15},{18,16},{19,... | collective-permute-start | bytes 1327112 | tf_op jit(solution)/shard_map/ppermute | solution.py:779
  291.4 10.4 %collective-permute-start.36 = (bf16[2,96,1152]{2,1,0:T(8,128)(2,1)S(1)}, bf16[2,96,1152]{2,1,0:T(8,128)(2,1)S(1)}, u32[]{:S(2)}, u32[]{:S(2)}) collective-permute-start(bf16[2,96,1152]{2,1,0:T(8,128)(2,1)S(1)} %add_convert_fusion.5), channel_id=1, source_target_pairs={{0,2},{1,3},{6,4},{7,5},{8,10},{9,11},{14,12},{15,13},{16,18},{17,... | collective-permute-start | bytes 1327112 | tf_op jit(solution)/shard_map/ppermute | solution.py:779
  300.2 3.0 collective-permute-start.43
  301.8 10.2 %collective-permute-start.42 = (bf16[2,96,1152]{2,1,0:T(8,128)(2,1)S(1)}, bf16[2,96,1152]{2,1,0:T(8,128)(2,1)S(1)}, u32[]{:S(2)}, u32[]{:S(2)}) collective-permute-start(bf16[2,96,1152]{2,1,0:T(8,128)(2,1)S(1)} %add_convert_fusion.3), channel_id=1, source_target_pairs={{2,0},{3,1},{4,6},{5,7},{10,8},{11,9},{12,14},{13,15},{18,16},{19,... | collective-permute-start | bytes 1327112 | tf_op jit(solution)/shard_map/ppermute | solution.py:779
  303.2 9.5 %collective-permute-start.41 = (bf16[2,96,1152]{2,1,0:T(8,128)(2,1)S(1)}, bf16[2,96,1152]{2,1,0:T(8,128)(2,1)S(1)}, u32[]{:S(2)}, u32[]{:S(2)}) collective-permute-start(bf16[2,96,1152]{2,1,0:T(8,128)(2,1)S(1)} %broadcast_select_fusion.3.own_ref), channel_id=1, source_target_pairs={{0,1},{1,0},{2,3},{3,2},{4,5},{5,4},{6,7},{7,6},{8,9},{9,8},{10,11... | collective-permute-start | bytes 1327112 | tf_op jit(solution)/shard_map/ppermute | solution.py:761
  312.0 6.4 %collective-permute-start.40 = (bf16[2,96,1152]{2,1,0:T(8,128)(2,1)S(1)}, bf16[2,96,1152]{2,1,0:T(8,128)(2,1)S(1)}, u32[]{:S(2)}, u32[]{:S(2)}) collective-permute-start(bf16[2,96,1152]{2,1,0:T(8,128)(2,1)S(1)} %add_convert_fusion.2), channel_id=1, source_target_pairs={{2,4},{3,5},{4,2},{5,3},{10,12},{11,13},{12,10},{13,11},{18,20},{1... | collective-permute-start | bytes 1327112 | tf_op jit(solution)/shard_map/ppermute | solution.py:779
  312.8 16.3 %collective-permute-start.46 = (bf16[2,96,1152]{2,1,0:T(8,128)(2,1)S(1)}, bf16[2,96,1152]{2,1,0:T(8,128)(2,1)S(1)}, u32[]{:S(2)}, u32[]{:S(2)}) collective-permute-start(bf16[2,96,1152]{2,1,0:T(8,128)(2,1)S(1)} %add_convert_fusion.1), channel_id=1, source_target_pairs={{2,0},{3,1},{4,6},{5,7},{10,8},{11,9},{12,14},{13,15},{18,16},{19,... | collective-permute-start | bytes 1327112 | tf_op jit(solution)/shard_map/ppermute | solution.py:779
  318.4 12.0 %collective-permute-start.45 = (bf16[2,96,1152]{2,1,0:T(8,128)(2,1)S(1)}, bf16[2,96,1152]{2,1,0:T(8,128)(2,1)S(1)}, u32[]{:S(2)}, u32[]{:S(2)}) collective-permute-start(bf16[2,96,1152]{2,1,0:T(8,128)(2,1)S(1)} %broadcast_select_fusion.2.own_ref), channel_id=1, source_target_pairs={{0,1},{1,0},{2,3},{3,2},{4,5},{5,4},{6,7},{7,6},{8,9},{9,8},{10,11... | collective-permute-start | bytes 1327112 | tf_op jit(solution)/shard_map/ppermute | solution.py:761
  329.0 10.3 %collective-permute-start.44 = (bf16[2,96,1152]{2,1,0:T(8,128)(2,1)S(1)}, bf16[2,96,1152]{2,1,0:T(8,128)(2,1)}, u32[]{:S(2)}, u32[]{:S(2)}) collective-permute-start(bf16[2,96,1152]{2,1,0:T(8,128)(2,1)S(1)} %add_convert_fusion), channel_id=1, source_target_pairs={{2,0},{3,1},{4,6},{5,7},{10,8},{11,9},{12,14},{13,15},{18,16},{19,... | collective-permute-start | bytes 1327112 | tf_op jit(solution)/shard_map/ppermute | solution.py:779
  330.4 17.3 %collective-permute-start.51 = (bf16[384,1152]{1,0:T(8,128)(2,1)}, bf16[384,1152]{1,0:T(8,128)(2,1)}, u32[]{:S(2)}, u32[]{:S(2)}) collective-permute-start(bf16[384,1152]{1,0:T(8,128)(2,1)} %get-tuple-element.240), channel_id=1, source_target_pairs={{0,24},{8,16},{16,8},{24,0},{1,25},{9,17},{17,9},{25,1},{2,26},{10... | collective-permute-start | bytes 2654216 | tf_op jit(solution)/shard_map/ppermute | solution.py:761
  339.3 20.7 %collective-permute-start.48 = (bf16[2,96,1152]{2,1,0:T(8,128)(2,1)S(1)}, bf16[2,96,1152]{2,1,0:T(8,128)(2,1)}, u32[]{:S(2)}, u32[]{:S(2)}) collective-permute-start(bf16[2,96,1152]{2,1,0:T(8,128)(2,1)S(1)} %broadcast_select_fusion.1.own_ref), channel_id=1, source_target_pairs={{0,1},{1,0},{2,3},{3,2},{4,5},{5,4},{6,7},{7,6},{8,9},{9,8},{10,11... | collective-permute-start | bytes 1327112 | tf_op jit(solution)/shard_map/ppermute | solution.py:761
  341.7 19.2 %collective-permute-start.47 = (bf16[2,96,1152]{2,1,0:T(8,128)(2,1)}, bf16[2,96,1152]{2,1,0:T(8,128)(2,1)}, u32[]{:S(2)}, u32[]{:S(2)}) collective-permute-start(bf16[2,96,1152]{2,1,0:T(8,128)(2,1)} %broadcast_select_fusion.own_ref), channel_id=1, source_target_pairs={{0,1},{1,0},{2,3},{3,2},{4,5},{5,4},{6,7},{7,6},{8,9},{9,8},{10,11... | collective-permute-start | bytes 1327112 | tf_op jit(solution)/shard_map/ppermute | solution.py:761
  344.2 8.7 %collective-permute-start.61 = (f32[1,4608]{1,0:T(1,128)S(1)}, f32[1,4608]{1,0:T(1,128)S(1)}, u32[]{:S(2)}, u32[]{:S(2)}) collective-permute-start(f32[1,4608]{1,0:T(1,128)S(1)} %broadcast_in_dim.7), channel_id=1, source_target_pairs={{0,8},{8,0},{16,24},{24,16},{1,9},{9,1},{17,25},{25,17},{2,10},{10... | collective-permute-start | bytes 55304 | tf_op jit(solution)/shard_map/ppermute | solution.py:761
  347.8 53.9 %collective-permute-start.55 = (bf16[384,1536]{1,0:T(8,128)(2,1)}, bf16[384,1536]{1,0:T(8,128)(2,1)}, u32[]{:S(2)}, u32[]{:S(2)}) collective-permute-start(bf16[384,1536]{1,0:T(8,128)(2,1)} %get-tuple-element.200.refs_8_), channel_id=1, source_target_pairs={{0,8},{8,0},{16,24},{24,16},{1,9},{9,1},{17,25},{25,17},{2,10},{10... | collective-permute-start | bytes 3538952 | tf_op jit(solution)/shard_map/ppermute | solution.py:761
  352.9 48.8 %collective-permute-start.57 = (bf16[384,1536]{1,0:T(8,128)(2,1)}, bf16[384,1536]{1,0:T(8,128)(2,1)}, u32[]{:S(2)}, u32[]{:S(2)}) collective-permute-start(bf16[384,1536]{1,0:T(8,128)(2,1)} %collective-permute-done.56.refs_10_), channel_id=1, source_target_pairs={{0,8},{8,0},{16,24},{24,16},{1,9},{9,1},{17,25},{25,17},{2,10},{10... | collective-permute-start | bytes 3538952 | tf_op jit(solution)/shard_map/ppermute | solution.py:761
  352.9 3.8 collective-permute-start.62
  356.7 3.3 collective-permute-start.63
  360.0 15.0 %collective-permute-start.52 = (bf16[384,1152]{1,0:T(8,128)(2,1)S(1)}, bf16[384,1152]{1,0:T(8,128)(2,1)}, u32[]{:S(2)}, u32[]{:S(2)}) collective-permute-start(bf16[384,1152]{1,0:T(8,128)(2,1)S(1)} %copy-done), channel_id=1, source_target_pairs={{0,8},{8,0},{16,24},{24,16},{1,9},{9,1},{17,25},{25,17},{2,10},{10... | collective-permute-start | bytes 2654216 | tf_op jit(solution)/shard_map/ppermute | solution.py:761
  360.1 22.6 %collective-permute-start.53 = (bf16[384,1152]{1,0:T(8,128)(2,1)S(1)}, bf16[384,1152]{1,0:T(8,128)(2,1)S(1)}, u32[]{:S(2)}, u32[]{:S(2)}) collective-permute-start(bf16[384,1152]{1,0:T(8,128)(2,1)S(1)} %copy-done.1), channel_id=1, source_target_pairs={{0,16},{8,24},{16,0},{24,8},{1,17},{9,25},{17,1},{25,9},{2,18},{10... | collective-permute-start | bytes 2654216 | tf_op jit(solution)/shard_map/ppermute | solution.py:761
  360.9 39.7 %collective-permute-start.54 = (bf16[384,1152]{1,0:T(8,128)(2,1)S(1)}, bf16[384,1152]{1,0:T(8,128)(2,1)}, u32[]{:S(2)}, u32[]{:S(2)}) collective-permute-start(bf16[384,1152]{1,0:T(8,128)(2,1)S(1)} %copy-done.2), channel_id=1, source_target_pairs={{0,24},{8,16},{16,8},{24,0},{1,25},{9,17},{17,9},{25,1},{2,26},{10... | collective-permute-start | bytes 2654216 | tf_op jit(solution)/shard_map/ppermute | solution.py:761
  374.9 39.7 %collective-permute-start.58 = (f32[1,4608]{1,0:T(1,128)}, f32[1,4608]{1,0:T(1,128)S(1)}, u32[]{:S(2)}, u32[]{:S(2)}) collective-permute-start(f32[1,4608]{1,0:T(1,128)} %broadcast_in_dim.6), channel_id=1, source_target_pairs={{0,8},{8,0},{16,24},{24,16},{1,9},{9,1},{17,25},{25,17},{2,10},{10... | collective-permute-start | bytes 55304 | tf_op jit(solution)/shard_map/ppermute | solution.py:761
  382.6 32.0 %collective-permute-start.59 = (f32[1,4608]{1,0:T(1,128)}, f32[1,4608]{1,0:T(1,128)S(1)}, u32[]{:S(2)}, u32[]{:S(2)}) collective-permute-start(f32[1,4608]{1,0:T(1,128)} %broadcast_in_dim.6), channel_id=1, source_target_pairs={{0,16},{8,24},{16,0},{24,8},{1,17},{9,25},{17,1},{25,9},{2,18},{10... | collective-permute-start | bytes 55304 | tf_op jit(solution)/shard_map/ppermute | solution.py:761
  400.6 14.0 %collective-permute-start.60 = (f32[1,4608]{1,0:T(1,128)}, f32[1,4608]{1,0:T(1,128)S(1)}, u32[]{:S(2)}, u32[]{:S(2)}) collective-permute-start(f32[1,4608]{1,0:T(1,128)} %broadcast_in_dim.6), channel_id=1, source_target_pairs={{0,24},{8,16},{16,8},{24,0},{1,25},{9,17},{17,9},{25,1},{2,26},{10... | collective-permute-start | bytes 55304 | tf_op jit(solution)/shard_map/ppermute | solution.py:761
  (31 other events, 471.6 us)

commit v2 on v1

--- a/solution.py
+++ b/solution.py
@@ -283,11 +283,13 @@
     half_width = head_width // 2
     frequencies = np.exp(-np.arange(half_width) * (2.0 * math.log(10000.0) / head_width))
     angles = np.arange(length)[:, None] * frequencies[None, :]
-    cosine, sine_table = (np.cos(angles), np.sin(angles))
-    return (
-        jnp.asarray(np.concatenate([cosine, cosine], axis=-1), jnp.float32),
-        jnp.asarray(np.concatenate([-sine_table, sine_table], axis=-1), jnp.float32),
-    )
+    return jnp.asarray(np.concatenate([np.cos(angles), np.sin(angles)], axis=-1), jnp.float32)
+
+
+def rope_factors(table):
+    flipped = pltpu.roll(table, HD // 2, 1)
+    low = lax.broadcasted_iota(jnp.int32, table.shape, 1) < HD // 2
+    return (jnp.where(low, table, flipped), jnp.where(low, -flipped, table))
 
 
 def dot_nt(left_side, right_side):
@@ -302,90 +304,59 @@
     )
 
 
-def forward_kernel(
-    layer, scale, rank, lengths, reach, x_ref, gain_ref, wq_ref, wk_ref, wv_ref, cos_ref, sin_ref,
-    *rest,
-):
-    normed_refs = rest[: -10]
-    q_ref, k_ref, v_ref, att_ref, prob_ref, slope_ref, recip_ref, accq, acck, accv = rest[-10:]
+def project_kernel(layer, depth, rank, x_ref, gain_ref, wq_ref, wk_ref, wv_ref, rope_ref, *rest):
+    scaled_refs = rest[:-8]
+    q_ref, k_ref, v_ref, recip_ref, accq, acck, accv, squares = rest[-8:]
     step = pl.program_id(0)
-    length = x_ref.shape[1]
     width = wq_ref.shape[1]
-    row_block = 128
 
     @pl.when(step == 0)
     def _():
-        x = x_ref[0].astype(jnp.float32)
-        mean = jnp.mean(x * x, axis=-1, keepdims=True)
-        recip_ref[...] = jnp.broadcast_to(lax.rsqrt(mean + epsilon), recip_ref.shape)
         accq[...] = jnp.zeros_like(accq)
         acck[...] = jnp.zeros_like(acck)
         accv[...] = jnp.zeros_like(accv)
+        squares[...] = jnp.zeros_like(squares)
 
     columns = pl.ds(pl.multiple_of((step ^ rank[0]) * width, 128), width)
-    x = x_ref[0, :, columns].astype(jnp.float32)
-    normed = (x * recip_ref[:, :1] * gain_ref[layer : layer + 1, columns]).astype(jnp.bfloat16)
-    for mask, normed_ref in enumerate(normed_refs):
+    x = x_ref[0].astype(jnp.float32)
+    scaled = (x * gain_ref[layer : layer + 1, columns]).astype(jnp.bfloat16)
+    square = x * x
+    total = squares[...]
+    for start in range(0, width, HD):
+        total += square[:, start : start + HD]
+    squares[...] = total
+    for mask, scaled_ref in enumerate(scaled_refs):
 
         @pl.when(step == mask)
         def _():
-            normed_ref[...] = normed
-
-    accq[...] += dot_nn(normed, wq_ref[0])
-    acck[...] += dot_nn(normed, wk_ref[0])
-    accv[...] += dot_nn(normed, wv_ref[0])
+            scaled_ref[...] = scaled
+
+    accq[...] += dot_nn(scaled, wq_ref[0])
+    acck[...] += dot_nn(scaled, wk_ref[0])
+    accv[...] += dot_nn(scaled, wv_ref[0])
 
     @pl.when(step == pl.num_programs(0) - 1)
     def _():
-        cosine, sine = (cos_ref[...], sin_ref[...])
+        mean = jnp.sum(squares[...], axis=-1, keepdims=True) / depth
+        recip = lax.rsqrt(mean + epsilon)
+        recip_ref[...] = jnp.broadcast_to(recip, recip_ref.shape)
+        cosine, sine = rope_factors(rope_ref[...])
+        cosine, sine = (cosine * recip, sine * recip)
 
         def turn(part):
             return part * cosine + pltpu.roll(part, HD // 2, 1) * sine
 
-        v_ref[...] = accv[...].astype(jnp.bfloat16)
-        for head in range(acck.shape[1] // HD):
-            part = slice(head * HD, (head + 1) * HD)
-            k_ref[:, part] = turn(acck[:, part]).astype(jnp.bfloat16)
-        ends = [lengths[0, 0]]
-        for doc in range(1, lengths.shape[1] - 1):
-            ends.append(ends[-1] + lengths[0, doc])
-        window = reach[layer]
-        heads = accq.shape[1] // HD
-        share = heads // (acck.shape[1] // HD)
-        for head in range(heads):
-            part = slice(head * HD, (head + 1) * HD)
-            q_ref[:, part] = turn(accq[:, part]).astype(jnp.bfloat16)
-        for block in range(length // row_block):
-            rows = slice(block * row_block, (block + 1) * row_block)
-            seen = (block + 1) * row_block
-            row = block * row_block + lax.broadcasted_iota(jnp.int32, (row_block, seen), 0)
-            col = lax.broadcasted_iota(jnp.int32, (row_block, seen), 1)
-            first = row - window + 1
-            for end in ends:
-                first = jnp.maximum(first, jnp.where(row >= end, end, 0))
-            allowed = (col <= row) & (col >= first)
-            for head in range(heads):
+        v_ref[...] = (accv[...] * recip).astype(jnp.bfloat16)
+        for out_ref, acc in ((q_ref, accq), (k_ref, acck)):
+            for head in range(acc.shape[1] // HD):
                 part = slice(head * HD, (head + 1) * HD)
-                kv = head // share
-                kv_part = slice(kv * HD, (kv + 1) * HD)
-                scores = dot_nt(q_ref[rows, part], k_ref[:seen, kv_part]) * scale
-                squashed = jnp.tanh(scores / softcap)
-                raised = jnp.where(allowed, jnp.exp(softcap * squashed), 0.0)
-                total = jnp.sum(raised, axis=-1, keepdims=True)
-                probability = raised * (1.0 / total)
-                rounded = probability.astype(jnp.bfloat16)
-                prob_ref[head, rows, :seen] = rounded
-                slope_ref[head, rows, :seen] = probability * ((1.0 - squashed * squashed) * scale)
-                att_ref[rows, part] = dot_nn(rounded, v_ref[:seen, kv_part]).astype(jnp.bfloat16)
-
-
-def forward_call(layer, steps, rank, layer_inputs, gain, w_query, w_key, w_value, lengths, reach, cosine, sine):
+                out_ref[:, part] = turn(acc[:, part]).astype(jnp.bfloat16)
+
+
+def project_call(layer, steps, rank, layer_inputs, gain, w_query, w_key, w_value, rope):
     _, length, depth = layer_inputs.shape
     width = depth // steps
     q_width, k_width = (w_query.shape[2], w_key.shape[2])
-    heads = q_width // HD
-    scale = (D // HEADS) ** (-0.5)
-    smem = pl.BlockSpec(memory_space=pltpu.SMEM)
 
     def weight(columns):
         return pl.BlockSpec((1, width, columns), lambda k, rank: (layer, k ^ rank[0], 0))
@@ -398,26 +369,19 @@
         ((length, q_width), bf),
         ((length, k_width), bf),
         ((length, k_width), bf),
-        ((length, q_width), bf),
-        ((heads, length, length), bf),
-        ((heads, length, length), f32),
         ((length, HD), f32),
     ]
-    flops = 2 * length * depth * (q_width + 2 * k_width)
     return pl.pallas_call(
-        functools.partial(forward_kernel, layer, scale),
+        functools.partial(project_kernel, layer, depth),
         grid_spec=pltpu.PrefetchScalarGridSpec(
             num_scalar_prefetch=1,
             grid=(steps,),
             in_specs=[
-                smem,
-                smem,
-                pl.BlockSpec((1, length, depth), lambda k, rank: (layer, 0, 0)),
+                pl.BlockSpec((1, length, width), lambda k, rank: (layer, 0, k ^ rank[0])),
                 whole(*gain.shape),
                 weight(q_width),
                 weight(k_width),
                 weight(k_width),
-                whole(length, HD),
                 whole(length, HD),
             ],
             out_specs=[whole(*shape) for shape, _ in shapes],
@@ -425,31 +389,97 @@
                 pltpu.VMEM((length, q_width), f32),
                 pltpu.VMEM((length, k_width), f32),
                 pltpu.VMEM((length, k_width), f32),
+                pltpu.VMEM((length, HD), f32),
             ],
         ),
         out_shape=[jax.ShapeDtypeStruct(shape, kind) for shape, kind in shapes],
         cost_estimate=pl.CostEstimate(
-            flops=flops, transcendentals=heads * length * length, bytes_accessed=20 << 20
+            flops=2 * length * depth * (q_width + 2 * k_width),
+            transcendentals=0,
+            bytes_accessed=17 << 20,
         ),
-    )(rank, lengths, reach, layer_inputs, gain, w_query, w_key, w_value, cosine, sine)
-
-
-def attention_kernel(
-    flat, chunks, side, rank, *refs,
-):
-    g_refs = refs[: 1 if flat else 4]
-    wo_ref, q_ref, k_ref, v_ref, att_ref, prob_ref, slope_ref, cos_ref, sin_ref = refs[
-        len(g_refs) : len(g_refs) + 9
-    ]
-    wq_ref, wk_ref, wv_ref, factor_ref, *rest = refs[len(g_refs) + 9 :]
-    pieces = rest[2 * chunks : -4]
-    acc, heads_ref, dk, dv = rest[-4:]
+    )(rank, layer_inputs, gain, w_query, w_key, w_value, rope)
+
+
+def allowed_block(lengths, window, first_row, rows, seen):
+    ends = [lengths[0, 0]]
+    for doc in range(1, lengths.shape[1] - 1):
+        ends.append(ends[-1] + lengths[0, doc])
+    row = first_row + lax.broadcasted_iota(jnp.int32, (rows, seen), 0)
+    col = lax.broadcasted_iota(jnp.int32, (rows, seen), 1)
+    first = row - window + 1
+    for end in ends:
+        first = jnp.maximum(first, jnp.where(row >= end, end, 0))
+    return (col <= row) & (col >= first)
+
+
+def weigh(q, k, allowed):
+    scale = (D // HEADS) ** (-0.5)
+    squashed = jnp.tanh(dot_nt(q, k) * (scale / softcap))
+    raised = jnp.where(allowed, jnp.exp(softcap * squashed), 0.0)
+    probability = raised * (1.0 / jnp.sum(raised, axis=-1, keepdims=True))
+    return (
+        probability.astype(jnp.bfloat16),
+        probability * (scale - squashed * squashed * scale),
+    )
+
+
+ROW_BLOCK = 128
+CHUNKS = 4
+
+
+def attend_kernel(layer, lengths, reach, q_ref, k_ref, v_ref, att_ref, prob_ref, slope_ref):
+    length = q_ref.shape[0]
+    for start in range(0, length, ROW_BLOCK):
+        rows, seen = (slice(start, start + ROW_BLOCK), start + ROW_BLOCK)
+        allowed = allowed_block(lengths, reach[layer], start, ROW_BLOCK, seen)
+        rounded, slope = weigh(q_ref[rows], k_ref[:seen], allowed)
+        prob_ref[0, rows, :seen] = rounded
+        slope_ref[0, rows, :seen] = slope
+        att_ref[rows] = dot_nn(rounded, v_ref[:seen]).astype(jnp.bfloat16)
+
+
+def attend_call(layer, lengths, reach, q, k, v):
+    length, q_width = q.shape
+    heads = q_width // HD
+    share = heads // (k.shape[1] // HD)
+    smem = pl.BlockSpec(memory_space=pltpu.SMEM)
+    own = pl.BlockSpec((length, HD), lambda h: (0, h))
+    shared = pl.BlockSpec((length, HD), lambda h: (0, h // share))
+    square = pl.BlockSpec((1, length, length), lambda h: (h, 0, 0))
+    return pl.pallas_call(
+        functools.partial(attend_kernel, layer),
+        grid=(heads,),
+        in_specs=[smem, smem, own, shared, shared],
+        out_specs=[own, square, square],
+        out_shape=[
+            jax.ShapeDtypeStruct((length, q_width), jnp.bfloat16),
+            jax.ShapeDtypeStruct((heads, length, length), jnp.bfloat16),
+            jax.ShapeDtypeStruct((heads, length, length), jnp.float32),
+        ],
+        cost_estimate=pl.CostEstimate(
+            flops=4 * heads * length * length * HD,
+            transcendentals=2 * heads * length * length,
+            bytes_accessed=6 << 20,
+        ),
+    )(lengths, reach, q, k, v)
+
+
+def attention_kernel(layer, flat, fused, chunks, side, rank, *refs):
+    g_refs, refs = (refs[: 1 if flat else 4], refs[1 if flat else 4 :])
+    wo_ref, q_ref, k_ref, v_ref, rope_ref, recip_ref, wq_ref, wk_ref, wv_ref, *refs = refs
+    if fused:
+        lengths, reach, *refs = refs
+    else:
+        att_ref, prob_ref, slope_ref, *refs = refs
+    shared_ref, *rest = refs
+    acc, heads_ref, factor_ref, dk, dv = rest[-5:]
     others, owns = (rest[:chunks], rest[chunks : 2 * chunks])
+    pieces = rest[2 * chunks : -5]
     step = pl.program_id(0)
     steps = pl.num_programs(0) // 2
     length, q_width = acc.shape
     k_width = dk.shape[1]
-    row_block = 128
 
     @pl.when(step == 0)
     def _():
@@ -476,7 +506,8 @@
 
     @pl.when(step == steps - 1)
     def _():
-        cosine, sine = (cos_ref[...], sin_ref[...])
+        cosine, sine = rope_factors(rope_ref[...])
+        recip = recip_ref[:, :1]
 
         def unturn(part, rows):
             return part * cosine[rows] - pltpu.roll(part, HD // 2, 1) * sine[rows]
@@ -486,62 +517,92 @@
         dv[...] = jnp.zeros_like(dv)
         heads = q_width // HD
         share = heads // (k_width // HD)
-        for head in range(heads):
-            part = slice(head * HD, (head + 1) * HD)
-            kv = head // share
-            kv_part = slice(kv * HD, (kv + 1) * HD)
-            for block in range(length // row_block):
-                rows = slice(block * row_block, (block + 1) * row_block)
-                seen = (block + 1) * row_block
-                ga = heads_ref[rows, part]
-                delta = jnp.sum(
-                    ga.astype(jnp.float32) * att_ref[rows, part].astype(jnp.float32),
-                    axis=-1,
-                    keepdims=True,
-                )
-                grad_probs = dot_nt(ga, v_ref[:seen, kv_part])
-                grad_scores = (slope_ref[head, rows, :seen] * (grad_probs - delta)).astype(
-                    jnp.bfloat16
-                )
-                gq = dot_nn(grad_scores, k_ref[:seen, kv_part])
-                factor_ref[rows, part] = unturn(gq, rows).astype(jnp.bfloat16)
-                dk[:seen, kv_part] += contract_rows(grad_scores, q_ref[rows, part])
-                dv[:seen, kv_part] += contract_rows(prob_ref[head, rows, :seen], ga)
+
+        def group_step(group, carry):
+            kv_part = pl.ds(pl.multiple_of(group * HD, HD), HD)
+            for member in range(share):
+                head = group * share + member
+                part = pl.ds(pl.multiple_of(head * HD, HD), HD)
+                att_part = pl.ds(pl.multiple_of(q_width + 2 * k_width + head * HD, HD), HD)
+                for start in range(0, length, ROW_BLOCK):
+                    rows, seen = (slice(start, start + ROW_BLOCK), start + ROW_BLOCK)
+                    ga = heads_ref[rows, part]
+                    if fused:
+                        allowed = allowed_block(lengths, reach[layer], start, ROW_BLOCK, seen)
+                        rounded, slope = weigh(q_ref[rows, part], k_ref[:seen, kv_part], allowed)
+                        att = dot_nn(rounded, v_ref[:seen, kv_part]).astype(jnp.bfloat16)
+                    else:
+                        rounded = prob_ref[head, rows, :seen]
+                        slope = slope_ref[head, rows, :seen]
+                        att = att_ref[rows, part]
+                    shared_ref[rows, att_part] = att
+                    delta = jnp.sum(
+                        ga.astype(jnp.float32) * att.astype(jnp.float32), axis=-1, keepdims=True
+                    )
+                    grad_probs = dot_nt(ga, v_ref[:seen, kv_part])
+                    grad_scores = (slope * (grad_probs - delta)).astype(jnp.bfloat16)
+                    gq = unturn(dot_nn(grad_scores, k_ref[:seen, kv_part]), rows)
+                    factor_ref[rows, part] = gq.astype(jnp.bfloat16)
+                    shared_ref[rows, part] = (gq * recip[rows]).astype(jnp.bfloat16)
+                    dk[:seen, kv_part] += contract_rows(grad_scores, q_ref[rows, part])
+                    dv[:seen, kv_part] += contract_rows(rounded, ga)
+            return carry
+
+        lax.fori_loop(0, k_width // HD, group_step, 0)
         every = slice(0, length)
         for kv in range(k_width // HD):
             kv_part = slice(kv * HD, (kv + 1) * HD)
-            factor_ref[:, q_width + kv * HD : q_width + (kv + 1) * HD] = unturn(
-                dk[:, kv_part], every
-            ).astype(jnp.bfloat16)
-        factor_ref[:, q_width + k_width : q_width + 2 * k_width] = dv[...].astype(jnp.bfloat16)
-        factor_ref[:, q_width + 2 * k_width :] = att_ref[...]
+            part = slice(q_width + kv * HD, q_width + (kv + 1) * HD)
+            gk = unturn(dk[:, kv_part], every)
+            factor_ref[:, part] = gk.astype(jnp.bfloat16)
+            shared_ref[:, part] = (gk * recip).astype(jnp.bfloat16)
+        part = slice(q_width + k_width, q_width + 2 * k_width)
+        factor_ref[:, part] = dv[...].astype(jnp.bfloat16)
+        shared_ref[:, part] = (dv[...] * recip).astype(jnp.bfloat16)
 
     @pl.when(step >= steps)
     def _():
-        total = dot_nt(factor_ref[:, :q_width], wq_ref[0])
-        total += dot_nt(factor_ref[:, q_width : q_width + k_width], wk_ref[0])
-        total += dot_nt(factor_ref[:, q_width + k_width : q_width + 2 * k_width], wv_ref[0])
         rows = length // chunks
-
-        @pl.when(step < steps + steps // 2)
-        def _():
-            for chunk in range(chunks):
-                others[chunk][0] = total[chunk * rows : (chunk + 1) * rows].astype(jnp.bfloat16)
-
-        @pl.when(step >= steps + steps // 2)
-        def _():
-            for chunk in range(chunks):
-                owns[chunk][0] = total[chunk * rows : (chunk + 1) * rows].astype(jnp.bfloat16)
-
-
-def attention_call(layer, steps, chunks, side, rank, upstream, w_out, forward, cosine, sine, w_query, w_key, w_value):
-    q, k, v, att, prob, slope = forward[steps:-1]
+        width = wq_ref.shape[1]
+        tile = width // 3
+
+        def tile_step(turn, carry):
+            here = pl.ds(pl.multiple_of(turn * tile, 128), tile)
+            total = dot_nt(factor_ref[:, :q_width], wq_ref[0, here])
+            total += dot_nt(factor_ref[:, q_width : q_width + k_width], wk_ref[0, here])
+            total += dot_nt(
+                factor_ref[:, q_width + k_width : q_width + 2 * k_width], wv_ref[0, here]
+            )
+
+            @pl.when(step < steps + steps // 2)
+            def _():
+                for chunk in range(chunks):
+                    others[chunk][0, :, here] = total[chunk * rows : (chunk + 1) * rows].astype(
+                        jnp.bfloat16
+                    )
+
+            @pl.when(step >= steps + steps // 2)
+            def _():
+                for chunk in range(chunks):
+                    owns[chunk][0, :, here] = total[chunk * rows : (chunk + 1) * rows].astype(
+                        jnp.bfloat16
+                    )
+
+            return carry
+
+        lax.fori_loop(0, 3, tile_step, 0)
+
+
+def attention_call(
+    layer, steps, chunks, side, rank, upstream, w_out, q, k, v, rope, recip, w_query, w_key,
+    w_value, lengths, reach, saved,
+):
     length, q_width = q.shape
     k_width = k.shape[1]
     depth = w_out.shape[2]
     width = depth // steps
     flat = len(upstream) == 1
-
+    fused = saved is None
     half = steps // 2
 
     def whole(*shape):
@@ -570,118 +631,152 @@
     own_spec = pl.BlockSpec(
         (1, rows, width), lambda k, side, rank: (jnp.clip(k - steps - half, 0, half - 1), 0, 0)
     )
+    smem = pl.BlockSpec(memory_space=pltpu.SMEM)
+    extra = [lengths, reach] if fused else list(saved)
     bf, f32 = (jnp.bfloat16, jnp.float32)
     f_width = 2 * (q_width + k_width)
     return pl.pallas_call(
-        functools.partial(attention_kernel, flat, chunks),
+        functools.partial(attention_kernel, layer, flat, fused, chunks),
         grid_spec=pltpu.PrefetchScalarGridSpec(
-        num_scalar_prefetch=2,
-        grid=(2 * steps,),
-        in_specs=g_specs
-        + [
-            pl.BlockSpec((1, q_width, width), lambda k, side, rank: (layer, 0, first(k) ^ rank[0])),
-            whole(*q.shape),
-            whole(*k.shape),
-            whole(*v.shape),
-            whole(*att.shape),
-            whole(*prob.shape),
-            whole(*slope.shape),
-            whole(length, HD),
-            whole(length, HD),
-            weight(q_width),
-            weight(k_width),
-            weight(k_width),
-        ],
-        out_specs=[
-            whole(length, f_width),
-        ]
-        + [other_spec] * chunks
-        + [own_spec] * chunks
-        + [whole(length, width)] * pieces,
-        scratch_shapes=[
-            pltpu.VMEM((length, q_width), f32),
-            pltpu.VMEM((length, q_width), bf),
-            pltpu.VMEM((length, k_width), f32),
-            pltpu.VMEM((length, k_width), f32),
-        ],
+            num_scalar_prefetch=2,
+            grid=(2 * steps,),
+            in_specs=g_specs
+            + [
+                pl.BlockSpec(
+                    (1, q_width, width), lambda k, side, rank: (layer, 0, first(k) ^ rank[0])
+                ),
+                whole(*q.shape),
+                whole(*k.shape),
+                whole(*v.shape),
+                whole(length, HD),
+                whole(length, HD),
+                weight(q_width),
+                weight(k_width),
+                weight(k_width),
+            ]
+            + ([smem, smem] if fused else [whole(*part.shape) for part in extra]),
+            out_specs=[whole(length, f_width)]
+            + [other_spec] * chunks
+            + [own_spec] * chunks
+            + [whole(length, width)] * pieces,
+            scratch_shapes=[
+                pltpu.VMEM((length, q_width), f32),
+                pltpu.VMEM((length, q_width), bf),
+                pltpu.VMEM((length, q_width + 2 * k_width), bf),
+                pltpu.VMEM((length, k_width), f32),
+                pltpu.VMEM((length, k_width), f32),
+            ],
         ),
         out_shape=[jax.ShapeDtypeStruct((length, f_width), bf)]
         + [jax.ShapeDtypeStruct((half, rows, width), bf)] * (2 * chunks)
         + [jax.ShapeDtypeStruct((length, width), bf)] * pieces,
         cost_estimate=pl.CostEstimate(
-            flops=4 * length * depth * (q_width + k_width), transcendentals=0, bytes_accessed=20 << 20
+            flops=4 * length * depth * (q_width + k_width),
+            transcendentals=0,
+            bytes_accessed=20 << 20,
         ),
-    )(side, rank, *upstream, w_out, q, k, v, att, prob, slope, cosine, sine, w_query, w_key, w_value)
-
-
-def norm_kernel(layer, flat, keep, steps, side, rank, own_ref, other_ref, x_ref, recip_ref, *refs):
+    )(side, rank, *upstream, w_out, q, k, v, rope, recip, w_query, w_key, w_value, *extra)
+
+
+NORM_ROWS = 16
+
+
+def norm_kernel(layer, flat, keep, steps, count, parts, side, rank, *refs):
+    owns, others, refs = (refs[:count], refs[count : 2 * count], refs[2 * count :])
+    x_ref, recip_ref, *refs = refs
     pieces = 1 if flat else steps
     g_refs, gain_ref, rest = (refs[:pieces], refs[pieces], refs[pieces + 1 :])
     outs = rest[-(1 if keep else steps) - 1 : -1]
     gain_out = rest[-1]
-    halves, _, width = own_ref.shape
+    halves, tile, width = owns[0].shape
     depth = steps * width
-    recip = recip_ref[:, :1]
-
-    @pl.when(pl.program_id(0) == 0)
+    step = pl.program_id(0)
+
+    @pl.when(step == 0)
     def _():
         if len(rest) > len(outs) + 1:
             gain_out[...] = rest[len(outs)][...]
         else:
             gain_out[...] = jnp.zeros_like(gain_out)
 
-    def grad_of(block):
-        own, other = (own_ref[block % halves], other_ref[block % halves])
-        pick = block // halves == side[0]
-        return jnp.where(pick, own.astype(jnp.float32), other.astype(jnp.float32))
-
-    total = jnp.zeros_like(recip)
-    for mask in range(steps):
-        block = mask ^ rank[0]
-        columns = pl.ds(pl.multiple_of(block * width, 128), width)
-        unit = x_ref[0, :, columns].astype(jnp.float32) * recip
-        product = grad_of(block) * unit
-        gain_out[:, columns] += jnp.sum(product.reshape(-1, 8, width), axis=0)
-        total += jnp.sum(product * gain_ref[layer : layer + 1, columns], axis=-1, keepdims=True)
-    mean = total / depth
-    for mask in range(steps):
-        block = mask ^ rank[0]
-        columns = pl.ds(pl.multiple_of(block * width, 128), width)
-        unit = x_ref[0, :, columns].astype(jnp.float32) * recip
-        grad = grad_of(block) * gain_ref[layer : layer + 1, columns]
-        g = (g_refs[0][:, columns] if flat else g_refs[mask][...]).astype(jnp.float32)
-        value = (g + recip * (grad - unit * mean)).astype(jnp.bfloat16)
-        if keep:
-            outs[0][:, columns] = value
-        else:
-            outs[mask][...] = value
-
-
-def norm_call(layer, chunk, side, rank, own, other, layer_inputs, recip, upstream, gain, keep, earlier):
-    halves, rows, width = own.shape
+    def row_step(own_ref, other_ref, turn, carry):
+        rows = pl.ds(pl.multiple_of(turn * NORM_ROWS, NORM_ROWS), NORM_ROWS)
+        recip = recip_ref[rows, :1]
+
+        def grad_of(block):
+            pick = jnp.broadcast_to(block // halves == side[0], (NORM_ROWS, width))
+            half = block % halves
+            return jnp.where(pick, own_ref[half, rows], other_ref[half, rows]).astype(jnp.float32)
+
+        total = jnp.zeros((NORM_ROWS, HD), jnp.float32)
+        for mask in range(steps):
+            block = mask ^ rank[0]
+            columns = pl.ds(pl.multiple_of(block * width, 128), width)
+            product = grad_of(block) * x_ref[0, rows, columns].astype(jnp.float32) * recip
+            gain_out[:, columns] += product[:8] + product[8:]
+            weighted = product * gain_ref[layer : layer + 1, columns]
+            for start in range(0, width, HD):
+                total += weighted[:, start : start + HD]
+        slope = recip * recip * (jnp.sum(total, axis=-1, keepdims=True) / depth)
+        for mask in range(steps):
+            block = mask ^ rank[0]
+            columns = pl.ds(pl.multiple_of(block * width, 128), width)
+            g = g_refs[0][rows, columns] if flat else g_refs[mask][rows]
+            value = (
+                g.astype(jnp.float32)
+                + grad_of(block) * gain_ref[layer : layer + 1, columns] * recip
+                - x_ref[0, rows, columns].astype(jnp.float32) * slope
+            ).astype(jnp.bfloat16)
+            if keep:
+                outs[0][rows, columns] = value
+            else:
+                outs[mask][rows] = value
+        return carry
+
+    for member in range(count):
+
+        @pl.when(step // parts == member)
+        def _():
+            lax.fori_loop(
+                0,
+                tile // NORM_ROWS,
+                functools.partial(row_step, owns[member], others[member]),
+                0,
+            )
+
+
+def norm_call(
+    layer, first, side, rank, owns, others, layer_inputs, recip, upstream, gain, keep, earlier
+):
+    count = len(owns)
+    halves, rows, width = owns[0].shape
     steps = 2 * halves
     length, depth = layer_inputs.shape[1:]
     flat = len(upstream) == 1
-    parts = 3
-    tile = rows // parts
-    half_spec = pl.BlockSpec((halves, tile, width), lambda r: (0, r, 0))
-    flat_spec = pl.BlockSpec((tile, depth), lambda r: (chunk * parts + r, 0))
-    piece_spec = pl.BlockSpec((tile, width), lambda r: (chunk * parts + r, 0))
+    tile = 32
+    parts = rows // tile
+    start = first * parts
+
+    def half_spec(member):
+        return pl.BlockSpec(
+            (halves, tile, width), lambda r: (0, jnp.clip(r - member * parts, 0, parts - 1), 0)
+        )
+
+    flat_spec = pl.BlockSpec((tile, depth), lambda r: (start + r, 0))
+    piece_spec = pl.BlockSpec((tile, width), lambda r: (start + r, 0))
     gain_spec = pl.BlockSpec((8, depth), lambda r: (0, 0))
     smem = pl.BlockSpec(memory_space=pltpu.SMEM)
     extra = [] if earlier is None else list(earlier)
     outs = 1 if keep else steps
-    first = 7 + len(upstream)
+    before = 5 + 2 * count + len(upstream)
     return pl.pallas_call(
-        functools.partial(norm_kernel, layer, flat, keep, steps),
-        grid=(parts,),
-        in_specs=[
-            smem,
-            smem,
-            half_spec,
-            half_spec,
-            pl.BlockSpec((1, tile, depth), lambda r: (layer, chunk * parts + r, 0)),
-            pl.BlockSpec((tile, HD), lambda r: (chunk * parts + r, 0)),
+        functools.partial(norm_kernel, layer, flat, keep, steps, count, parts),
+        grid=(count * parts,),
+        in_specs=[smem, smem]
+        + [half_spec(member) for member in range(count)] * 2
+        + [
+            pl.BlockSpec((1, tile, depth), lambda r: (layer, start + r, 0)),
+            pl.BlockSpec((tile, HD), lambda r: (start + r, 0)),
         ]
         + [flat_spec if flat else piece_spec] * len(upstream)
         + [pl.BlockSpec(gain.shape, lambda r: (0, 0))]
@@ -692,11 +787,11 @@
         ]
         * outs
         + [jax.ShapeDtypeStruct((8, depth), jnp.float32)],
-        input_output_aliases={first + i: i for i in range(outs)} if extra else {},
+        input_output_aliases={before + i: i for i in range(outs)} if extra else {},
         cost_estimate=pl.CostEstimate(
-            flops=30 * rows * depth, transcendentals=0, bytes_accessed=4 << 20
+            flops=30 * count * rows * depth, transcendentals=0, bytes_accessed=4 * count << 20
         ),
-    )(side, rank, own, other, layer_inputs, recip, *upstream, gain, *extra)
+    )(side, rank, *owns, *others, layer_inputs, recip, *upstream, gain, *extra)
 
 
 def weights_kernel(count, groups, *refs):
@@ -719,28 +814,30 @@
     wo_ref[0] = total / groups
 
 
-def weights_call(layer, layers, normed, upstream, factors, q_width, k_width, earlier):
+def weights_call(
+    layer, layers, normed, upstream, factors, q_width, k_width, earlier, first_tile, tiles
+):
     count = len(normed)
     length, width = normed[0].shape
     tile = width // 3
-    piece = pl.BlockSpec((length, tile), lambda n: (0, n))
+    piece = pl.BlockSpec((length, tile), lambda n: (0, n + first_tile))
     factor = pl.BlockSpec(factors[0].shape, lambda n: (0, 0))
     any_spec = pl.BlockSpec(memory_space=pl.ANY)
     extra = [] if earlier is None else list(earlier)
     f32 = jnp.float32
 
     def tall(columns):
-        return pl.BlockSpec((1, tile, columns), lambda n: (layer, n, 0))
+        return pl.BlockSpec((1, tile, columns), lambda n: (layer, n + first_tile, 0))
 
     return pl.pallas_call(
         functools.partial(weights_kernel, count, count),
-        grid=(width // tile,),
+        grid=(tiles,),
         in_specs=[piece] * (2 * count) + [factor] * count + [any_spec] * len(extra),
         out_specs=[
             tall(q_width),
             tall(k_width),
             tall(k_width),
-            pl.BlockSpec((1, q_width, tile), lambda n: (layer, 0, n)),
+            pl.BlockSpec((1, q_width, tile), lambda n: (layer, 0, n + first_tile)),
         ],
         out_shape=[
             jax.ShapeDtypeStruct((layers, width, q_width), f32),
@@ -750,9 +847,9 @@
         ],
         input_output_aliases={3 * count + i: i for i in range(len(extra))},
         cost_estimate=pl.CostEstimate(
-            flops=4 * count * length * width * (q_width + k_width),
+            flops=4 * count * length * tile * tiles * (q_width + k_width),
             transcendentals=0,
-            bytes_accessed=24 << 20,
+            bytes_accessed=8 * tiles << 20,
         ),
     )(*normed, *upstream, *factors, *extra)
 
@@ -772,7 +869,7 @@
 def share_factor(factor):
     beside = xor_send(factor, "dp", 1)
     across = xor_send(factor, "dp", 2)
-    return [factor, beside, across, xor_send(across, "dp", 1)]
+    return [beside, across]
 
 
 def along_line(x, pairs):
@@ -787,6 +884,13 @@
 
 def after(value, *earlier):
     return lax.optimization_barrier((value, *earlier))[0]
+
+
+def wave_order(chunks):
+    order = []
+    for slot in range(chunks + 3):
+        order += [(stage, slot - stage) for stage in range(4) if 0 <= slot - stage < chunks]
+    return order + [(4, 0), (4, chunks - 1)]
 
 
 class Wave:
@@ -823,73 +927,102 @@
         )
     count = lax.axis_size("dp")
     rank = lax.axis_index("dp").astype(jnp.int32).reshape(1)
-    chunks = 4
+    chunks = CHUNKS
     layers = layer_inputs.shape[0]
     length = layer_inputs.shape[1]
     q_width, k_width = (w_query.shape[2], w_key.shape[2])
-    cosine, sine = rope_wide(length, HD)
-    forwards, normed = ([None] * layers, [None] * layers)
+    rope = rope_wide(length, HD)
+    normed = [None] * layers
     place = lax.axis_index("tp")
     side = (place % 2).astype(jnp.int32).reshape(1)
     line = place // 2
     outer = (line == 0) | (line == 3)
 
-    def forward(layer, inputs):
-        result = forward_call(
-            layer, count, rank, inputs, gain, w_query, w_key, w_value, doc_lengths, window_reach,
-            cosine, sine,
-        )
-        forwards[layer] = result
-        normed[layer] = spread_pieces(result[:count])
-        return result[0]
-
-    def weights(layer, factors, sent, earlier):
-        return weights_call(
-            layer, layers, normed[layer], sent, factors, q_width, k_width, earlier
-        )
-
-    upstream = [out_grad]
-    waiting = None
     grads = None
     gains = [None] * layers
     top = layers - 1
+    waiting = None
+    upstream = [out_grad]
+
+    def project(layer, inputs):
+        result = project_call(
+            layer, count, rank, inputs, gain, w_query, w_key, w_value, rope
+        )
+        return (result[:count], result[count : count + 3], result[-1])
+
+    def weights(layer, factors, sent, tie):
+        sent = [after(sent[0], tie)] + sent[1:]
+        return weights_call(
+            layer, layers, normed[layer], sent, factors, q_width, k_width, grads, 0, 3
+        )
+
+    pieces, heads, recip = project(top, layer_inputs)
+    normed[top] = spread_pieces(pieces)
+    saved = None
     for layer in reversed(range(layers)):
-        if layer == top:
-            forward(top, layer_inputs)
         factor, *partial = attention_call(
-            layer, count, chunks, side, rank, upstream, w_out, forwards[layer], cosine, sine, w_query,
-            w_key, w_value,
+            layer, count, chunks, side, rank, upstream, w_out, *heads, rope, recip, w_query,
+            w_key, w_value, doc_lengths, window_reach, saved,
         )
-        factors = share_factor(factor)
-        sent = spread_pieces(partial[2 * chunks :] or upstream)
         wave = Wave(partial[:chunks], partial[chunks : 2 * chunks], outer)
+        owned = partial[2 * chunks :] or upstream
         if layer:
-            wave.last = forward(layer - 1, after(layer_inputs, factor))
+            wave.last = after(layer_inputs, factor)
+            next_pieces, next_heads, next_recip = project(layer - 1, wave.last)
+            wave.last = next_heads[0]
         if waiting is not None:
-            grads = weights(waiting[0], waiting[1], [after(waiting[2][0], factor)] + waiting[2][1:], grads)
+            grads = weights(*waiting, factor)
             wave.last = grads[1]
         result = None
-        for slot in range(chunks + 5):
-            for stage in range(5):
-                chunk = slot - stage
-                if not 0 <= chunk < chunks:
-                    continue
-                if stage < 4:
-                    wave.step(chunk, stage)
-                    continue
+        for stage, chunk in wave_order(chunks):
+            if stage < 4:
+                wave.step(chunk, stage)
+            else:
+                members = range(chunk, chunks - 1) if chunk < chunks - 1 else range(chunk, chunks)
                 result = norm_call(
-                    layer, chunk, side, rank, wave.value[chunk], wave.tie(wave.moved[chunk]),
-                    layer_inputs, forwards[layer][-1], upstream, gain, layer == 0, result,
+                    layer, chunk, side, rank, [wave.value[member] for member in members],
+                    [wave.tie(wave.moved[member]) for member in members], layer_inputs, recip,
+                    upstream, gain, layer == 0, result,
                 )
                 wave.last = result[-1]
+            if (stage, chunk) == (0, 0):
+                tied = owned
+                if layer == top:
+                    tied = [
+                        after(piece, wave.last) if mask else piece
+                        for mask, piece in enumerate(owned)
+                    ]
+                factors = [factor] + share_factor(after(factor, wave.last))
+                sent = spread_pieces(tied)
+            if layer and (stage, chunk) == (0, 1):
+                tied = [
+                    after(piece, wave.last) if mask else piece
+                    for mask, piece in enumerate(next_pieces)
+                ]
+                normed[layer - 1] = spread_pieces(tied)
+            if (stage, chunk) == (2, chunks - 1):
+                factors.append(xor_send(after(factors[2], wave.last), "dp", 1))
+            if (stage, chunk) == (3, chunks - 2):
+                if layer:
+                    saved = attend_call(
+                        layer - 1, doc_lengths, window_reach, wave.tie(next_heads[0]),
+                        *next_heads[1:],
+                    )
+                    wave.last = saved[0]
+                else:
+                    grads = weights(layer, factors, sent, wave.last)
+                    wave.last = grads[1]
         *upstream, gain_part = result
         waiting = (layer, factors, sent)
-        gain_row = jnp.sum(gain_part, axis=0, keepdims=True)
-        beside = xor_send(gain_row, "dp", 1)
-        across, corner = (xor_send(gain_row, "dp", 2), xor_send(gain_row, "dp", 3))
-        gains[layer] = ((gain_row + beside) + (across + corner)) / count
-    grads = weights(waiting[0], waiting[1], waiting[2], grads)
-    return (upstream[0], *grads, jnp.concatenate(gains, axis=0))
+        if layer:
+            heads, recip = (next_heads, next_recip)
+        gains[layer] = gain_part
+    gain_rows = jnp.stack([jnp.sum(part, axis=0) for part in lax.optimization_barrier(gains)])
+    beside, across, corner = (
+        xor_send(gain_rows, "dp", mask) for mask in range(1, 4)
+    )
+    gain_total = ((gain_rows + beside) + (across + corner)) / count
+    return (upstream[0], *grads, gain_total)
 
 
 def solution(mesh):

time: 424 us -> 486 us (1.15); the launches traced: 416 us -> 483 us
  waiting for transfers between devices: 156 us -> 237 us
  starting transfers between devices: 112 us -> 102 us
    ppermute x24, waiting for transfers between devices: 97.7 us -> 174 us  [along_line(): lax.ppermute(x, 'tp', [(2 * a + side, 2 * b + side) for a, b in pairs for...]
    ppermute x24, starting transfers between devices: 73.4 us -> 66.3 us  [along_line(): lax.ppermute(x, 'tp', [(2 * a + side, 2 * b + side) for a, b in pairs for...]
    ppermute x40 -> x37, waiting for transfers between devices: 58.5 us -> 63 us  [xor_send(): lax.ppermute(x, axis, [(i, i ^ mask) for i in range(lax.axis_size(axis))])]
    ppermute x40 -> x37, starting transfers between devices: 38.4 us -> 35.3 us  [xor_send(): lax.ppermute(x, axis, [(i, i ^ mask) for i in range(lax.axis_size(axis))])]
    pallas_call x14 -> x11, Pallas kernels: 133 us -> 133 us  [the longest x2 47.3 us: attention_call(): pl.pallas_call(functools.partial(attention_kernel, layer, flat, fused, ch...]
  transfers between devices with their start and end apart: 64 -> 61, of which waited for: 25 -> 26; matrix products, arithmetic and copies ran while one was open for 2% -> 1% of each run, Pallas kernels for 23% -> 19%
where the time goes in v2:
time: 486 us; the launch traced here: 483 us
  waiting for transfers between devices  237 us (49%)
  Pallas kernels  133 us (27%)
  starting transfers between devices  102 us (21%)
  other arithmetic  6.24 us (1%)
    ppermute x24, waiting for transfers between devices, along_line(): lax.ppermute(x, 'tp', [(2 * a + side, 2 * b + side) for a, b in pairs for...  174 us
    ppermute x24, starting transfers between devices, along_line(): lax.ppermute(x, 'tp', [(2 * a + side, 2 * b + side) for a, b in pairs for...  66.3 us
    ppermute x37, waiting for transfers between devices, xor_send(): lax.ppermute(x, axis, [(i, i ^ mask) for i in range(lax.axis_size(axis))])  63 us
    pallas_call x2, Pallas kernels, attention_call(): pl.pallas_call(functools.partial(attention_kernel, layer, flat, fused, ch...  47.3 us
    ppermute x37, starting transfers between devices, xor_send(): lax.ppermute(x, axis, [(i, i ^ mask) for i in range(lax.axis_size(axis))])  35.3 us
    pallas_call x4, Pallas kernels, norm_call(): pl.pallas_call(functools.partial(norm_kernel, layer, flat, keep, steps, c...  30.6 us
    pallas_call x2, Pallas kernels, weights_call(): pl.pallas_call(functools.partial(weights_kernel, count, count), grid=(til...  25.7 us
    pallas_call x2, Pallas kernels, project_call(): pl.pallas_call(functools.partial(project_kernel, layer, depth), grid_spec...  23.5 us
  transfers between devices with their start and end apart: 61, of which 26 were waited for; matrix products, arithmetic and copies ran while one was open for 1% of the time, Pallas kernels for 19%

profile of v2, /device:TPU:0, one launch (start us, length us, event | category | flops | bytes accessed | tf_op | source)
XLA Modules:
  0.0 482.6 jit_solution(14299169322461880247)
XLA Ops:
  0.6 11.7 %shard_map.145 = (bf16[384,1152]{1,0:T(8,128)(2,1)}, bf16[384,1152]{1,0:T(8,128)(2,1)}, bf16[384,1152]{1,0:T(8,128)(2,1)}, bf16[384,1152]{1,0:T(8,128)(2,1)}, bf...) custom-call(s32[1]{0:T(128)} %bitcast.1.rank, ...), custom_call_target="tpu_custom_call" | custom-call | flops 3623878656 | bytes 17825792 | tf_op jit(solution)/shard_map/pallas_call | solution.py:374
  12.4 25.8 %shard_map.146 = (bf16[384,1536]{1,0:T(8,128)(2,1)}, bf16[2,96,1152]{2,1,0:T(8,128)(2,1)}, bf16[2,96,1152]{2,1,0:T(8,128)(2,1)}, bf16[2,96,1152]{2,1,0:T(8,128)(...) custom-call(s32[1]{0:T(128)} %bitcast.side, ...), custom_call_target="tpu_custom_call" | custom-call | flops 5435817984 | bytes 20971520 | tf_op jit(solution)/shard_map/pallas_call | solution.py:638
  38.2 3.1 collective-permute-start.1
  41.3 1.9 collective-permute-start.6
  43.4 11.8 %shard_map.147 = (bf16[384,1152]{1,0:T(8,128)(2,1)}, bf16[384,1152]{1,0:T(8,128)(2,1)}, bf16[384,1152]{1,0:T(8,128)(2,1)}, bf16[384,1152]{1,0:T(8,128)(2,1)}, bf...) custom-call(s32[1]{0:T(128)} %bitcast.1.rank, ...), custom_call_target="tpu_custom_call" | custom-call | flops 3623878656 | bytes 17825792 | tf_op jit(solution)/shard_map/pallas_call | solution.py:374
  55.2 2.0 collective-permute-start.23
  57.3 4.7 collective-permute-done.3
  62.0 4.0 collective-permute-start.2
  66.1 7.4 %collective-permute-done.2 = bf16[2,96,1152]{2,1,0:T(8,128)(2,1)S(1)} collective-permute-done((bf16[2,96,1152]{2,1,0:T(8,128)(2,1)S(1)}, bf16[2,96,1152]{2,1,0:T(8,128)(2,1)S(1)}, u32[]{:S(2)}, u32[]{:S(2)}) %collective-permute-start.2) | collective-permute-done | bytes 442400 | tf_op jit(solution)/shard_map/ppermute | solution.py:876
  73.6 4.4 collective-permute-start.5
  78.1 9.8 %collective-permute-done.5 = bf16[2,96,1152]{2,1,0:T(8,128)(2,1)S(1)} collective-permute-done((bf16[2,96,1152]{2,1,0:T(8,128)(2,1)S(1)}, bf16[2,96,1152]{2,1,0:T(8,128)(2,1)S(1)}, u32[]{:S(2)}, u32[]{:S(2)}) %collective-permute-start.5) | collective-permute-done | bytes 442400 | tf_op jit(solution)/shard_map/ppermute | solution.py:876
  88.7 1.9 collective-permute-start.29
  90.7 17.4 %collective-permute-start.10 = (bf16[2,96,1152]{2,1,0:T(8,128)(2,1)S(1)}, bf16[2,96,1152]{2,1,0:T(8,128)(2,1)S(1)}, u32[]{:S(2)}, u32[]{:S(2)}) collective-permute-start(bf16[2,96,1152]{2,1,0:T(8,128)(2,1)S(1)} %add_convert_fusion.20), channel_id=1, source_target_pairs={{0,2},{1,3},{6,4},{7,5},{8,10},{9,11},{14,12},{15,13},{16,18},{17,... | collective-permute-start | bytes 1327112 | tf_op jit(solution)/shard_map/ppermute | solution.py:876
  108.2 8.6 %collective-permute-done.10 = bf16[2,96,1152]{2,1,0:T(8,128)(2,1)S(1)} collective-permute-done((bf16[2,96,1152]{2,1,0:T(8,128)(2,1)S(1)}, bf16[2,96,1152]{2,1,0:T(8,128)(2,1)S(1)}, u32[]{:S(2)}, u32[]{:S(2)}) %collective-permute-start.10) | collective-permute-done | bytes 442400 | tf_op jit(solution)/shard_map/ppermute | solution.py:876
  117.6 1.3 collective-permute-start.8
  119.0 21.9 %collective-permute-done.8 = bf16[2,96,1152]{2,1,0:T(8,128)(2,1)S(1)} collective-permute-done((bf16[2,96,1152]{2,1,0:T(8,128)(2,1)S(1)}, bf16[2,96,1152]{2,1,0:T(8,128)(2,1)S(1)}, u32[]{:S(2)}, u32[]{:S(2)}) %collective-permute-start.8) | collective-permute-done | bytes 442400 | tf_op jit(solution)/shard_map/ppermute | solution.py:876
  140.9 1.5 collective-permute-start.7
  142.5 6.7 %collective-permute-done.7 = bf16[2,96,1152]{2,1,0:T(8,128)(2,1)S(1)} collective-permute-done((bf16[2,96,1152]{2,1,0:T(8,128)(2,1)S(1)}, bf16[2,96,1152]{2,1,0:T(8,128)(2,1)S(1)}, u32[]{:S(2)}, u32[]{:S(2)}) %collective-permute-start.7) | collective-permute-done | bytes 442400 | tf_op jit(solution)/shard_map/ppermute | solution.py:876
  150.0 1.3 collective-permute-start.12
  151.4 18.1 %collective-permute-done.12 = bf16[2,96,1152]{2,1,0:T(8,128)(2,1)S(1)} collective-permute-done((bf16[2,96,1152]{2,1,0:T(8,128)(2,1)S(1)}, bf16[2,96,1152]{2,1,0:T(8,128)(2,1)S(1)}, u32[]{:S(2)}, u32[]{:S(2)}) %collective-permute-start.12) | collective-permute-done | bytes 442400 | tf_op jit(solution)/shard_map/ppermute | solution.py:876
  170.3 1.3 collective-permute-start.15
  171.7 17.7 %collective-permute-done.15 = bf16[2,96,1152]{2,1,0:T(8,128)(2,1)S(1)} collective-permute-done((bf16[2,96,1152]{2,1,0:T(8,128)(2,1)S(1)}, bf16[2,96,1152]{2,1,0:T(8,128)(2,1)S(1)}, u32[]{:S(2)}, u32[]{:S(2)}) %collective-permute-start.15) | collective-permute-done | bytes 442400 | tf_op jit(solution)/shard_map/ppermute | solution.py:876
  189.4 1.5 collective-permute-start.14
  190.9 6.1 %shard_map.148 = (bf16[384,512]{1,0:T(8,128)(2,1)}, bf16[4,384,384]{2,1,0:T(8,128)(2,1)}, f32[4,384,384]{2,1,0:T(8,128)}) custom-call(s32[1,4]{1,0:T(1,128)} %lengths.1, s32[2]{0:T(128)} %reach.1, bf16[384,512]{1,0:T(8,128)(2,1)} %get-tuple-element.155.q_ref.refs_5_, bf16[384,256]{1,0:T(8,128)(2,1)} %get-tuple-element.156.k_ref.refs_6_, ...), custom_call_target="tpu_custom_call" | custom-call | flops 301989888 | bytes 6291456 | tf_op jit(solution)/shard_map/pallas_call | solution.py:450
  197.0 2.5 collective-permute-done.14
  203.8 8.8 %collective-permute-done.18.refs_4_ = bf16[2,96,1152]{2,1,0:T(8,128)(2,1)S(1)} collective-permute-done((bf16[2,96,1152]{2,1,0:T(8,128)(2,1)S(1)}, bf16[2,96,1152]{2,1,0:T(8,128)(2,1)S(1)}, u32[]{:S(2)}, u32[]{:S(2)}) %collective-permute-start.18) | collective-permute-done | bytes 442400 | tf_op jit(solution)/shard_map/ppermute | solution.py:858
  212.6 9.5 %collective-permute-done.17.refs_3_ = bf16[2,96,1152]{2,1,0:T(8,128)(2,1)S(1)} collective-permute-done((bf16[2,96,1152]{2,1,0:T(8,128)(2,1)S(1)}, bf16[2,96,1152]{2,1,0:T(8,128)(2,1)S(1)}, u32[]{:S(2)}, u32[]{:S(2)}) %collective-permute-start.17) | collective-permute-done | bytes 442400 | tf_op jit(solution)/shard_map/ppermute | solution.py:858
  222.1 5.0 %collective-permute-done.19.refs_5_ = bf16[2,96,1152]{2,1,0:T(8,128)(2,1)S(1)} collective-permute-done((bf16[2,96,1152]{2,1,0:T(8,128)(2,1)S(1)}, bf16[2,96,1152]{2,1,0:T(8,128)(2,1)S(1)}, u32[]{:S(2)}, u32[]{:S(2)}) %collective-permute-start.19) | collective-permute-done | bytes 442400 | tf_op jit(solution)/shard_map/ppermute | solution.py:858
  227.1 4.0 collective-permute-start.26
  231.9 10.7 %shard_map.149 = (bf16[384,1152]{1,0:T(8,128)(2,1)}, bf16[384,1152]{1,0:T(8,128)(2,1)}, bf16[384,1152]{1,0:T(8,128)(2,1)}, bf16[384,1152]{1,0:T(8,128)(2,1)}, f32[8,4608]{1,0:T(8,128)}) custom-call(s32[1]{0:T(128)} %bitcast.side, s32[1]{0:T(128)} %bitcast.1.rank, bf16[2,96,1152]{2,1,0:T(8,128)(2,1)} %copy-done.4, bf16[2,96,1152]{2,1,0:T(8,128)(2,1)} %copy-done.5, ...), custom_call_target="tpu_custom_call" | custom-call | flops 39813120 | bytes 12582912 | tf_op jit(solution)/shard_map/pallas_call | solution.py:772
  242.6 4.7 shard_map.150
  247.3 21.5 %shard_map.151 = (bf16[384,1536]{1,0:T(8,128)(2,1)}, bf16[2,96,1152]{2,1,0:T(8,128)(2,1)}, bf16[2,96,1152]{2,1,0:T(8,128)(2,1)}, bf16[2,96,1152]{2,1,0:T(8,128)(...) custom-call(s32[1]{0:T(128)} %bitcast.side, ...), custom_call_target="tpu_custom_call" | custom-call | flops 5435817984 | bytes 20971520 | tf_op jit(solution)/shard_map/pallas_call | solution.py:638
  268.8 4.1 collective-permute-start.44
  273.0 1.4 collective-permute-start.46
  274.4 1.1 collective-permute-start.21
  276.4 12.8 %shard_map.152 = (f32[2,1152,512]{2,1,0:T(8,128)}, f32[2,1152,256]{2,1,0:T(8,128)}, f32[2,1152,256]{2,1,0:T(8,128)}, f32[2,512,1152]{2,1,0:T(8,128)}) custom-call(bf16[384,1152]{1,0:T(8,128)(2,1)} %get-tuple-element.180.refs_0_, bf16[384,1152]{1,0:T(8,128)(2,1)} %collective-permute-done.22.refs_1_, bf16[384,1152]{1,0:T(8,128)(2,1)} %collective-permute-done.23.refs_2_, ...), custom_call_target="tpu_custom_call" | custom-call | flops 5435817984 | bytes 25165824 | tf_op jit(solution)/shard_map/pallas_call | solution.py:832
  289.2 1.2 collective-permute-start.35
  290.5 6.6 %collective-permute-done.32 = bf16[2,96,1152]{2,1,0:T(8,128)(2,1)S(1)} collective-permute-done((bf16[2,96,1152]{2,1,0:T(8,128)(2,1)}, bf16[2,96,1152]{2,1,0:T(8,128)(2,1)S(1)}, u32[]{:S(2)}, u32[]{:S(2)}) %collective-permute-start.32) | collective-permute-done | bytes 442400 | tf_op jit(solution)/shard_map/ppermute | solution.py:858
  297.1 1.8 collective-permute-start.31
  299.0 9.1 %collective-permute-done.31 = bf16[2,96,1152]{2,1,0:T(8,128)(2,1)S(1)} collective-permute-done((bf16[2,96,1152]{2,1,0:T(8,128)(2,1)S(1)}, bf16[2,96,1152]{2,1,0:T(8,128)(2,1)S(1)}, u32[]{:S(2)}, u32[]{:S(2)}) %collective-permute-start.31) | collective-permute-done | bytes 442400 | tf_op jit(solution)/shard_map/ppermute | solution.py:876
  308.1 1.1 collective-permute-start.20
  309.3 4.4 collective-permute-start.34
  313.9 8.1 %collective-permute-done.34 = bf16[2,96,1152]{2,1,0:T(8,128)(2,1)S(1)} collective-permute-done((bf16[2,96,1152]{2,1,0:T(8,128)(2,1)S(1)}, bf16[2,96,1152]{2,1,0:T(8,128)(2,1)S(1)}, u32[]{:S(2)}, u32[]{:S(2)}) %collective-permute-start.34) | collective-permute-done | bytes 442400 | tf_op jit(solution)/shard_map/ppermute | solution.py:876
  323.0 15.3 %collective-permute-start.39 = (bf16[2,96,1152]{2,1,0:T(8,128)(2,1)S(1)}, bf16[2,96,1152]{2,1,0:T(8,128)(2,1)S(1)}, u32[]{:S(2)}, u32[]{:S(2)}) collective-permute-start(bf16[2,96,1152]{2,1,0:T(8,128)(2,1)S(1)} %add_convert_fusion.8), channel_id=1, source_target_pairs={{0,2},{1,3},{6,4},{7,5},{8,10},{9,11},{14,12},{15,13},{16,18},{17,... | collective-permute-start | bytes 1327112 | tf_op jit(solution)/shard_map/ppermute | solution.py:876
  338.4 6.4 %collective-permute-done.39 = bf16[2,96,1152]{2,1,0:T(8,128)(2,1)S(1)} collective-permute-done((bf16[2,96,1152]{2,1,0:T(8,128)(2,1)S(1)}, bf16[2,96,1152]{2,1,0:T(8,128)(2,1)S(1)}, u32[]{:S(2)}, u32[]{:S(2)}) %collective-permute-start.39) | collective-permute-done | bytes 442400 | tf_op jit(solution)/shard_map/ppermute | solution.py:876
  345.6 1.3 collective-permute-start.37
  347.0 18.0 %collective-permute-done.37 = bf16[2,96,1152]{2,1,0:T(8,128)(2,1)S(1)} collective-permute-done((bf16[2,96,1152]{2,1,0:T(8,128)(2,1)S(1)}, bf16[2,96,1152]{2,1,0:T(8,128)(2,1)S(1)}, u32[]{:S(2)}, u32[]{:S(2)}) %collective-permute-start.37) | collective-permute-done | bytes 442400 | tf_op jit(solution)/shard_map/ppermute | solution.py:876
  365.0 1.5 collective-permute-start.36
  366.5 5.7 %collective-permute-done.36 = bf16[2,96,1152]{2,1,0:T(8,128)(2,1)S(1)} collective-permute-done((bf16[2,96,1152]{2,1,0:T(8,128)(2,1)S(1)}, bf16[2,96,1152]{2,1,0:T(8,128)(2,1)S(1)}, u32[]{:S(2)}, u32[]{:S(2)}) %collective-permute-start.36) | collective-permute-done | bytes 442400 | tf_op jit(solution)/shard_map/ppermute | solution.py:876
  373.0 1.3 collective-permute-start.41
  374.4 18.0 %collective-permute-done.41 = bf16[2,96,1152]{2,1,0:T(8,128)(2,1)S(1)} collective-permute-done((bf16[2,96,1152]{2,1,0:T(8,128)(2,1)S(1)}, bf16[2,96,1152]{2,1,0:T(8,128)(2,1)S(1)}, u32[]{:S(2)}, u32[]{:S(2)}) %collective-permute-start.41) | collective-permute-done | bytes 442400 | tf_op jit(solution)/shard_map/ppermute | solution.py:876
  394.0 1.5 collective-permute-start.47
  396.3 1.7 collective-permute-start.49
  398.0 11.7 %collective-permute-done.47 = bf16[2,96,1152]{2,1,0:T(8,128)(2,1)S(1)} collective-permute-done((bf16[2,96,1152]{2,1,0:T(8,128)(2,1)S(1)}, bf16[2,96,1152]{2,1,0:T(8,128)(2,1)S(1)}, u32[]{:S(2)}, u32[]{:S(2)}) %collective-permute-start.47) | collective-permute-done | bytes 442400 | tf_op jit(solution)/shard_map/ppermute | solution.py:876
  411.5 7.3 %collective-permute-done.49.refs_6_ = bf16[384,1152]{1,0:T(8,128)(2,1)S(1)} collective-permute-done((bf16[384,1152]{1,0:T(8,128)(2,1)S(1)}, bf16[384,1152]{1,0:T(8,128)(2,1)S(1)}, u32[]{:S(2)}, u32[]{:S(2)}) %collective-permute-start.49) | collective-permute-done | bytes 884768 | tf_op jit(solution)/shard_map/ppermute | solution.py:858
  419.7 16.9 %collective-permute-done.50.refs_7_ = bf16[384,1152]{1,0:T(8,128)(2,1)S(1)} collective-permute-done((bf16[384,1152]{1,0:T(8,128)(2,1)S(1)}, bf16[384,1152]{1,0:T(8,128)(2,1)S(1)}, u32[]{:S(2)}, u32[]{:S(2)}) %collective-permute-start.50) | collective-permute-done | bytes 884768 | tf_op jit(solution)/shard_map/ppermute | solution.py:858
  436.7 1.3 collective-permute-start.43
  440.0 12.9 %shard_map.153 = (f32[2,1152,512]{2,1,0:T(8,128)}, f32[2,1152,256]{2,1,0:T(8,128)}, f32[2,1152,256]{2,1,0:T(8,128)}, f32[2,512,1152]{2,1,0:T(8,128)}) custom-call(bf16[384,1152]{1,0:T(8,128)(2,1)} %get-tuple-element.214.refs_0_, ...), custom_call_target="tpu_custom_call", output_to_operand_aliasing={{0}: (12, {}), {1}: (13, {}), {2}: (14, {}), {3}: (15, {})} | custom-call | flops 5435817984 | bytes 25165824 | tf_op jit(solution)/shard_map/pallas_call | solution.py:832
  453.0 3.9 collective-permute-done.43
  459.5 10.5 %shard_map.154 = (bf16[384,4608]{1,0:T(8,128)(2,1)}, f32[8,4608]{1,0:T(8,128)}) custom-call(s32[1]{0:T(128)} %bitcast.side, s32[1]{0:T(128)} %bitcast.1.rank, bf16[2,96,1152]{2,1,0:T(8,128)(2,1)} %copy-done.3, bf16[2,96,1152]{2,1,0:T(8,128)(2,1)} %broadcast_select_fusion.2.refs_1_, bf16[2,96,1152]{2,1,0:T(8,128)(2,1)} %broadcast_select_fusion.1.refs_2_, ...), custom_call_target="tpu_custom_call" | custom-call | flops 39813120 | bytes 12582912 | tf_op jit(solution)/shard_map/pallas_call | solution.py:772
  470.8 4.7 shard_map.155
  476.7 1.8 collective-permute-start.59
  478.6 2.2 collective-permute-done.59
  480.7 1.2 collective-permute-done.60
  (175 shorter events, 25.9 us)
Async XLA Ops:
  38.2 17.0 %collective-permute-start.1 = (bf16[2,96,1152]{2,1,0:T(8,128)(2,1)}, bf16[2,96,1152]{2,1,0:T(8,128)(2,1)S(1)}, u32[]{:S(2)}, u32[]{:S(2)}) collective-permute-start(bf16[2,96,1152]{2,1,0:T(8,128)(2,1)} %get-tuple-element.132), channel_id=1, source_target_pairs={{0,1},{1,0},{2,3},{3,2},{4,5},{5,4},{6,7},{7,6},{8,9},{9,8},{10,11... | collective-permute-start | bytes 1327112 | tf_op jit(solution)/shard_map/ppermute | solution.py:858
  41.2 20.7 %collective-permute-start.3 = (bf16[2,96,1152]{2,1,0:T(8,128)(2,1)}, bf16[2,96,1152]{2,1,0:T(8,128)(2,1)S(1)}, u32[]{:S(2)}, u32[]{:S(2)}) collective-permute-start(bf16[2,96,1152]{2,1,0:T(8,128)(2,1)} %get-tuple-element.138), channel_id=1, source_target_pairs={{0,1},{1,0},{2,3},{3,2},{4,5},{5,4},{6,7},{7,6},{8,9},{9,8},{10,11... | collective-permute-start | bytes 1327112 | tf_op jit(solution)/shard_map/ppermute | solution.py:858
  41.3 32.2 %collective-permute-start.6 = (bf16[2,96,1152]{2,1,0:T(8,128)(2,1)}, bf16[2,96,1152]{2,1,0:T(8,128)(2,1)S(1)}, u32[]{:S(2)}, u32[]{:S(2)}) collective-permute-start(bf16[2,96,1152]{2,1,0:T(8,128)(2,1)} %get-tuple-element.142), channel_id=1, source_target_pairs={{0,1},{1,0},{2,3},{3,2},{4,5},{5,4},{6,7},{7,6},{8,9},{9,8},{10,11... | collective-permute-start | bytes 1327112 | tf_op jit(solution)/shard_map/ppermute | solution.py:858
  43.3 47.4 %collective-permute-start = (bf16[2,96,1152]{2,1,0:T(8,128)(2,1)}, bf16[2,96,1152]{2,1,0:T(8,128)(2,1)S(1)}, u32[]{:S(2)}, u32[]{:S(2)}) collective-permute-start(bf16[2,96,1152]{2,1,0:T(8,128)(2,1)} %get-tuple-element.130), channel_id=1, source_target_pairs={{0,1},{1,0},{2,3},{3,2},{4,5},{5,4},{6,7},{7,6},{8,9},{9,8},{10,11... | collective-permute-start | bytes 1327112 | tf_op jit(solution)/shard_map/ppermute | solution.py:858
  43.4 157.3 %collective-permute-start.22 = (bf16[384,1152]{1,0:T(8,128)(2,1)}, bf16[384,1152]{1,0:T(8,128)(2,1)}, u32[]{:S(2)}, u32[]{:S(2)}) collective-permute-start(bf16[384,1152]{1,0:T(8,128)(2,1)} %get-tuple-element.181), channel_id=1, source_target_pairs={{0,8},{8,0},{16,24},{24,16},{1,9},{9,1},{17,25},{25,17},{2,10},{10... | collective-permute-start | bytes 2654216 | tf_op jit(solution)/shard_map/ppermute | solution.py:858
  55.2 146.4 %collective-permute-start.23 = (bf16[384,1152]{1,0:T(8,128)(2,1)}, bf16[384,1152]{1,0:T(8,128)(2,1)}, u32[]{:S(2)}, u32[]{:S(2)}) collective-permute-start(bf16[384,1152]{1,0:T(8,128)(2,1)} %get-tuple-element.182), channel_id=1, source_target_pairs={{0,16},{8,24},{16,0},{24,8},{1,17},{9,25},{17,1},{25,9},{2,18},{10... | collective-permute-start | bytes 2654216 | tf_op jit(solution)/shard_map/ppermute | solution.py:858
  62.0 11.5 %collective-permute-start.2 = (bf16[2,96,1152]{2,1,0:T(8,128)(2,1)S(1)}, bf16[2,96,1152]{2,1,0:T(8,128)(2,1)S(1)}, u32[]{:S(2)}, u32[]{:S(2)}) collective-permute-start(bf16[2,96,1152]{2,1,0:T(8,128)(2,1)S(1)} %add_convert_fusion.23), channel_id=1, source_target_pairs={{0,2},{1,3},{6,4},{7,5},{8,10},{9,11},{14,12},{15,13},{16,18},{17,... | collective-permute-start | bytes 1327112 | tf_op jit(solution)/shard_map/ppermute | solution.py:876
  73.5 130.3 %collective-permute-start.24 = (bf16[384,1152]{1,0:T(8,128)(2,1)}, bf16[384,1152]{1,0:T(8,128)(2,1)}, u32[]{:S(2)}, u32[]{:S(2)}) collective-permute-start(bf16[384,1152]{1,0:T(8,128)(2,1)} %get-tuple-element.183), channel_id=1, source_target_pairs={{0,24},{8,16},{16,8},{24,0},{1,25},{9,17},{17,9},{25,1},{2,26},{10... | collective-permute-start | bytes 2654216 | tf_op jit(solution)/shard_map/ppermute | solution.py:858
  73.6 14.3 %collective-permute-start.5 = (bf16[2,96,1152]{2,1,0:T(8,128)(2,1)S(1)}, bf16[2,96,1152]{2,1,0:T(8,128)(2,1)S(1)}, u32[]{:S(2)}, u32[]{:S(2)}) collective-permute-start(bf16[2,96,1152]{2,1,0:T(8,128)(2,1)S(1)} %add_convert_fusion.22), channel_id=1, source_target_pairs={{0,2},{1,3},{6,4},{7,5},{8,10},{9,11},{14,12},{15,13},{16,18},{17,... | collective-permute-start | bytes 1327112 | tf_op jit(solution)/shard_map/ppermute | solution.py:876
  87.9 0.8 collective-permute-start.4
  88.7 114.1 %collective-permute-start.29 = (bf16[384,1536]{1,0:T(8,128)(2,1)}, bf16[384,1536]{1,0:T(8,128)(2,1)}, u32[]{:S(2)}, u32[]{:S(2)}) collective-permute-start(bf16[384,1536]{1,0:T(8,128)(2,1)} %get-tuple-element.193.refs_8_), channel_id=1, source_target_pairs={{0,16},{8,24},{16,0},{24,8},{1,17},{9,25},{17,1},{25,9},{2,18},{10... | collective-permute-start | bytes 3538952 | tf_op jit(solution)/shard_map/ppermute | solution.py:858
  90.7 26.1 %collective-permute-start.10 = (bf16[2,96,1152]{2,1,0:T(8,128)(2,1)S(1)}, bf16[2,96,1152]{2,1,0:T(8,128)(2,1)S(1)}, u32[]{:S(2)}, u32[]{:S(2)}) collective-permute-start(bf16[2,96,1152]{2,1,0:T(8,128)(2,1)S(1)} %add_convert_fusion.20), channel_id=1, source_target_pairs={{0,2},{1,3},{6,4},{7,5},{8,10},{9,11},{14,12},{15,13},{16,18},{17,... | collective-permute-start | bytes 1327112 | tf_op jit(solution)/shard_map/ppermute | solution.py:876
  116.8 0.8 collective-permute-start.9
  117.6 23.3 %collective-permute-start.8 = (bf16[2,96,1152]{2,1,0:T(8,128)(2,1)S(1)}, bf16[2,96,1152]{2,1,0:T(8,128)(2,1)S(1)}, u32[]{:S(2)}, u32[]{:S(2)}) collective-permute-start(bf16[2,96,1152]{2,1,0:T(8,128)(2,1)S(1)} %add_convert_fusion.18), channel_id=1, source_target_pairs={{2,0},{3,1},{4,6},{5,7},{10,8},{11,9},{12,14},{13,15},{18,16},{19,... | collective-permute-start | bytes 1327112 | tf_op jit(solution)/shard_map/ppermute | solution.py:876
  140.9 8.2 %collective-permute-start.7 = (bf16[2,96,1152]{2,1,0:T(8,128)(2,1)S(1)}, bf16[2,96,1152]{2,1,0:T(8,128)(2,1)S(1)}, u32[]{:S(2)}, u32[]{:S(2)}) collective-permute-start(bf16[2,96,1152]{2,1,0:T(8,128)(2,1)S(1)} %add_convert_fusion.17), channel_id=1, source_target_pairs={{0,2},{1,3},{6,4},{7,5},{8,10},{9,11},{14,12},{15,13},{16,18},{17,... | collective-permute-start | bytes 1327112 | tf_op jit(solution)/shard_map/ppermute | solution.py:876
  142.5 58.2 %copy-start.4 = (bf16[2,96,1152]{2,1,0:T(8,128)(2,1)}, bf16[2,96,1152]{2,1,0:T(8,128)(2,1)S(1)}, u32[]{:S(2)}) copy-start(bf16[2,96,1152]{2,1,0:T(8,128)(2,1)S(1)} %broadcast_select_fusion.7.refs_0_) | copy-start | bytes 1327108
  149.2 0.8 collective-permute-start.13
  150.0 19.5 %collective-permute-start.12 = (bf16[2,96,1152]{2,1,0:T(8,128)(2,1)S(1)}, bf16[2,96,1152]{2,1,0:T(8,128)(2,1)S(1)}, u32[]{:S(2)}, u32[]{:S(2)}) collective-permute-start(bf16[2,96,1152]{2,1,0:T(8,128)(2,1)S(1)} %add_convert_fusion.15), channel_id=1, source_target_pairs={{2,0},{3,1},{4,6},{5,7},{10,8},{11,9},{12,14},{13,15},{18,16},{19,... | collective-permute-start | bytes 1327112 | tf_op jit(solution)/shard_map/ppermute | solution.py:876
  169.5 0.8 collective-permute-start.11
  170.3 19.1 %collective-permute-start.15 = (bf16[2,96,1152]{2,1,0:T(8,128)(2,1)S(1)}, bf16[2,96,1152]{2,1,0:T(8,128)(2,1)S(1)}, u32[]{:S(2)}, u32[]{:S(2)}) collective-permute-start(bf16[2,96,1152]{2,1,0:T(8,128)(2,1)S(1)} %add_convert_fusion.13), channel_id=1, source_target_pairs={{2,0},{3,1},{4,6},{5,7},{10,8},{11,9},{12,14},{13,15},{18,16},{19,... | collective-permute-start | bytes 1327112 | tf_op jit(solution)/shard_map/ppermute | solution.py:876
  189.4 10.2 %collective-permute-start.14 = (bf16[2,96,1152]{2,1,0:T(8,128)(2,1)S(1)}, bf16[2,96,1152]{2,1,0:T(8,128)(2,1)S(1)}, u32[]{:S(2)}, u32[]{:S(2)}) collective-permute-start(bf16[2,96,1152]{2,1,0:T(8,128)(2,1)S(1)} %add_convert_fusion.12), channel_id=1, source_target_pairs={{2,0},{3,1},{4,6},{5,7},{10,8},{11,9},{12,14},{13,15},{18,16},{19,... | collective-permute-start | bytes 1327112 | tf_op jit(solution)/shard_map/ppermute | solution.py:876
  199.6 13.0 %collective-permute-start.18 = (bf16[2,96,1152]{2,1,0:T(8,128)(2,1)S(1)}, bf16[2,96,1152]{2,1,0:T(8,128)(2,1)S(1)}, u32[]{:S(2)}, u32[]{:S(2)}) collective-permute-start(bf16[2,96,1152]{2,1,0:T(8,128)(2,1)S(1)} %broadcast_select_fusion.6.refs_1_), channel_id=1, source_target_pairs={{0,1},{1,0},{2,3},{3,2},{4,5},{5,4},{6,7},{7,6},{8,9},{9,8},{10,11... | collective-permute-start | bytes 1327112 | tf_op jit(solution)/shard_map/ppermute | solution.py:858
  200.7 21.4 %collective-permute-start.17 = (bf16[2,96,1152]{2,1,0:T(8,128)(2,1)S(1)}, bf16[2,96,1152]{2,1,0:T(8,128)(2,1)S(1)}, u32[]{:S(2)}, u32[]{:S(2)}) collective-permute-start(bf16[2,96,1152]{2,1,0:T(8,128)(2,1)S(1)} %broadcast_select_fusion.7.refs_0_), channel_id=1, source_target_pairs={{0,1},{1,0},{2,3},{3,2},{4,5},{5,4},{6,7},{7,6},{8,9},{9,8},{10,11... | collective-permute-start | bytes 1327112 | tf_op jit(solution)/shard_map/ppermute | solution.py:858
  201.6 25.5 %collective-permute-start.19 = (bf16[2,96,1152]{2,1,0:T(8,128)(2,1)S(1)}, bf16[2,96,1152]{2,1,0:T(8,128)(2,1)S(1)}, u32[]{:S(2)}, u32[]{:S(2)}) collective-permute-start(bf16[2,96,1152]{2,1,0:T(8,128)(2,1)S(1)} %broadcast_select_fusion.5.refs_2_), channel_id=1, source_target_pairs={{0,1},{1,0},{2,3},{3,2},{4,5},{5,4},{6,7},{7,6},{8,9},{9,8},{10,11... | collective-permute-start | bytes 1327112 | tf_op jit(solution)/shard_map/ppermute | solution.py:858
  202.8 29.1 %collective-permute-start.16 = (bf16[2,96,1152]{2,1,0:T(8,128)(2,1)S(1)}, bf16[2,96,1152]{2,1,0:T(8,128)(2,1)S(1)}, u32[]{:S(2)}, u32[]{:S(2)}) collective-permute-start(bf16[2,96,1152]{2,1,0:T(8,128)(2,1)S(1)} %broadcast_select_fusion.4.refs_0_), channel_id=1, source_target_pairs={{0,1},{1,0},{2,3},{3,2},{4,5},{5,4},{6,7},{7,6},{8,9},{9,8},{10,11... | collective-permute-start | bytes 1327112 | tf_op jit(solution)/shard_map/ppermute | solution.py:858
  203.8 70.6 %collective-permute-start.28 = (bf16[384,1536]{1,0:T(8,128)(2,1)}, bf16[384,1536]{1,0:T(8,128)(2,1)}, u32[]{:S(2)}, u32[]{:S(2)}) collective-permute-start(bf16[384,1536]{1,0:T(8,128)(2,1)} %get-tuple-element.193.refs_8_), channel_id=1, source_target_pairs={{0,8},{8,0},{16,24},{24,16},{1,9},{9,1},{17,25},{25,17},{2,10},{10... | collective-permute-start | bytes 3538952 | tf_op jit(solution)/shard_map/ppermute | solution.py:858
  212.6 62.9 %collective-permute-start.30 = (bf16[384,1536]{1,0:T(8,128)(2,1)}, bf16[384,1536]{1,0:T(8,128)(2,1)}, u32[]{:S(2)}, u32[]{:S(2)}) collective-permute-start(bf16[384,1536]{1,0:T(8,128)(2,1)} %collective-permute-done.29.refs_10_), channel_id=1, source_target_pairs={{0,8},{8,0},{16,24},{24,16},{1,9},{9,1},{17,25},{25,17},{2,10},{10... | collective-permute-start | bytes 3538952 | tf_op jit(solution)/shard_map/ppermute | solution.py:858
  222.1 46.7 %collective-permute-start.25 = (bf16[384,1152]{1,0:T(8,128)(2,1)}, bf16[384,1152]{1,0:T(8,128)(2,1)}, u32[]{:S(2)}, u32[]{:S(2)}) collective-permute-start(bf16[384,1152]{1,0:T(8,128)(2,1)} %get-tuple-element.188), channel_id=1, source_target_pairs={{0,8},{8,0},{16,24},{24,16},{1,9},{9,1},{17,25},{25,17},{2,10},{10... | collective-permute-start | bytes 2654216 | tf_op jit(solution)/shard_map/ppermute | solution.py:858
  227.1 45.8 %collective-permute-start.26 = (bf16[384,1152]{1,0:T(8,128)(2,1)}, bf16[384,1152]{1,0:T(8,128)(2,1)}, u32[]{:S(2)}, u32[]{:S(2)}) collective-permute-start(bf16[384,1152]{1,0:T(8,128)(2,1)} %get-tuple-element.190), channel_id=1, source_target_pairs={{0,16},{8,24},{16,0},{24,8},{1,17},{9,25},{17,1},{25,9},{2,18},{10... | collective-permute-start | bytes 2654216 | tf_op jit(solution)/shard_map/ppermute | solution.py:858
  231.9 41.1 %collective-permute-start.27 = (bf16[384,1152]{1,0:T(8,128)(2,1)}, bf16[384,1152]{1,0:T(8,128)(2,1)}, u32[]{:S(2)}, u32[]{:S(2)}) collective-permute-start(bf16[384,1152]{1,0:T(8,128)(2,1)} %get-tuple-element.192), channel_id=1, source_target_pairs={{0,24},{8,16},{16,8},{24,0},{1,25},{9,17},{17,9},{25,1},{2,26},{10... | collective-permute-start | bytes 2654216 | tf_op jit(solution)/shard_map/ppermute | solution.py:858
  268.8 126.9 %collective-permute-start.44 = (bf16[384,1152]{1,0:T(8,128)(2,1)}, bf16[384,1152]{1,0:T(8,128)(2,1)}, u32[]{:S(2)}, u32[]{:S(2)}) collective-permute-start(bf16[384,1152]{1,0:T(8,128)(2,1)} %get-tuple-element.216), channel_id=1, source_target_pairs={{0,8},{8,0},{16,24},{24,16},{1,9},{9,1},{17,25},{25,17},{2,10},{10... | collective-permute-start | bytes 2654216 | tf_op jit(solution)/shard_map/ppermute | solution.py:858
  272.9 123.3 %collective-permute-start.45 = (bf16[384,1152]{1,0:T(8,128)(2,1)}, bf16[384,1152]{1,0:T(8,128)(2,1)}, u32[]{:S(2)}, u32[]{:S(2)}) collective-permute-start(bf16[384,1152]{1,0:T(8,128)(2,1)} %get-tuple-element.218), channel_id=1, source_target_pairs={{0,16},{8,24},{16,0},{24,8},{1,17},{9,25},{17,1},{25,9},{2,18},{10... | collective-permute-start | bytes 2654216 | tf_op jit(solution)/shard_map/ppermute | solution.py:858
  273.0 123.3 %collective-permute-start.46 = (bf16[384,1152]{1,0:T(8,128)(2,1)}, bf16[384,1152]{1,0:T(8,128)(2,1)}, u32[]{:S(2)}, u32[]{:S(2)}) collective-permute-start(bf16[384,1152]{1,0:T(8,128)(2,1)} %get-tuple-element.220), channel_id=1, source_target_pairs={{0,24},{8,16},{16,8},{24,0},{1,25},{9,17},{17,9},{25,1},{2,26},{10... | collective-permute-start | bytes 2654216 | tf_op jit(solution)/shard_map/ppermute | solution.py:858
  274.4 14.8 %collective-permute-start.21 = (bf16[2,96,1152]{2,1,0:T(8,128)(2,1)}, bf16[2,96,1152]{2,1,0:T(8,128)(2,1)S(1)}, u32[]{:S(2)}, u32[]{:S(2)}) collective-permute-start(bf16[2,96,1152]{2,1,0:T(8,128)(2,1)} %get-tuple-element.179), channel_id=1, source_target_pairs={{0,1},{1,0},{2,3},{3,2},{4,5},{5,4},{6,7},{7,6},{8,9},{9,8},{10,11... | collective-permute-start | bytes 1327112 | tf_op jit(solution)/shard_map/ppermute | solution.py:858
  275.5 21.6 %collective-permute-start.32 = (bf16[2,96,1152]{2,1,0:T(8,128)(2,1)}, bf16[2,96,1152]{2,1,0:T(8,128)(2,1)S(1)}, u32[]{:S(2)}, u32[]{:S(2)}) collective-permute-start(bf16[2,96,1152]{2,1,0:T(8,128)(2,1)} %get-tuple-element.198), channel_id=1, source_target_pairs={{0,1},{1,0},{2,3},{3,2},{4,5},{5,4},{6,7},{7,6},{8,9},{9,8},{10,11... | collective-permute-start | bytes 1327112 | tf_op jit(solution)/shard_map/ppermute | solution.py:858
  289.2 20.1 %collective-permute-start.35 = (bf16[2,96,1152]{2,1,0:T(8,128)(2,1)S(1)}, bf16[2,96,1152]{2,1,0:T(8,128)(2,1)S(1)}, u32[]{:S(2)}, u32[]{:S(2)}) collective-permute-start(bf16[2,96,1152]{2,1,0:T(8,128)(2,1)S(1)} %copy-done.33), channel_id=1, source_target_pairs={{0,1},{1,0},{2,3},{3,2},{4,5},{5,4},{6,7},{7,6},{8,9},{9,8},{10,11... | collective-permute-start | bytes 1327112 | tf_op jit(solution)/shard_map/ppermute | solution.py:858
  297.1 11.0 %collective-permute-start.31 = (bf16[2,96,1152]{2,1,0:T(8,128)(2,1)S(1)}, bf16[2,96,1152]{2,1,0:T(8,128)(2,1)S(1)}, u32[]{:S(2)}, u32[]{:S(2)}) collective-permute-start(bf16[2,96,1152]{2,1,0:T(8,128)(2,1)S(1)} %add_convert_fusion.11), channel_id=1, source_target_pairs={{0,2},{1,3},{6,4},{7,5},{8,10},{9,11},{14,12},{15,13},{16,18},{17,... | collective-permute-start | bytes 1327112 | tf_op jit(solution)/shard_map/ppermute | solution.py:876
  308.1 14.9 %collective-permute-start.20 = (bf16[2,96,1152]{2,1,0:T(8,128)(2,1)S(1)}, bf16[2,96,1152]{2,1,0:T(8,128)(2,1)S(1)}, u32[]{:S(2)}, u32[]{:S(2)}) collective-permute-start(bf16[2,96,1152]{2,1,0:T(8,128)(2,1)S(1)} %copy-done.32), channel_id=1, source_target_pairs={{0,1},{1,0},{2,3},{3,2},{4,5},{5,4},{6,7},{7,6},{8,9},{9,8},{10,11... | collective-permute-start | bytes 1327112 | tf_op jit(solution)/shard_map/ppermute | solution.py:858
  309.3 12.6 %collective-permute-start.34 = (bf16[2,96,1152]{2,1,0:T(8,128)(2,1)S(1)}, bf16[2,96,1152]{2,1,0:T(8,128)(2,1)S(1)}, u32[]{:S(2)}, u32[]{:S(2)}) collective-permute-start(bf16[2,96,1152]{2,1,0:T(8,128)(2,1)S(1)} %add_convert_fusion.10), channel_id=1, source_target_pairs={{0,2},{1,3},{6,4},{7,5},{8,10},{9,11},{14,12},{15,13},{16,18},{17,... | collective-permute-start | bytes 1327112 | tf_op jit(solution)/shard_map/ppermute | solution.py:876
  322.0 0.8 collective-permute-start.33
  322.8 72.8 %collective-permute-start.52 = (bf16[384,1536]{1,0:T(8,128)(2,1)S(1)}, bf16[384,1536]{1,0:T(8,128)(2,1)S(1)}, u32[]{:S(2)}, u32[]{:S(2)}) collective-permute-start(bf16[384,1536]{1,0:T(8,128)(2,1)S(1)} %copy-done.9), channel_id=1, source_target_pairs={{0,16},{8,24},{16,0},{24,8},{1,17},{9,25},{17,1},{25,9},{2,18},{10... | collective-permute-start | bytes 3538952 | tf_op jit(solution)/shard_map/ppermute | solution.py:858
  323.0 21.8 %collective-permute-start.39 = (bf16[2,96,1152]{2,1,0:T(8,128)(2,1)S(1)}, bf16[2,96,1152]{2,1,0:T(8,128)(2,1)S(1)}, u32[]{:S(2)}, u32[]{:S(2)}) collective-permute-start(bf16[2,96,1152]{2,1,0:T(8,128)(2,1)S(1)} %add_convert_fusion.8), channel_id=1, source_target_pairs={{0,2},{1,3},{6,4},{7,5},{8,10},{9,11},{14,12},{15,13},{16,18},{17,... | collective-permute-start | bytes 1327112 | tf_op jit(solution)/shard_map/ppermute | solution.py:876
  344.8 0.8 collective-permute-start.38
  345.6 19.4 %collective-permute-start.37 = (bf16[2,96,1152]{2,1,0:T(8,128)(2,1)S(1)}, bf16[2,96,1152]{2,1,0:T(8,128)(2,1)S(1)}, u32[]{:S(2)}, u32[]{:S(2)}) collective-permute-start(bf16[2,96,1152]{2,1,0:T(8,128)(2,1)S(1)} %add_convert_fusion.6), channel_id=1, source_target_pairs={{2,0},{3,1},{4,6},{5,7},{10,8},{11,9},{12,14},{13,15},{18,16},{19,... | collective-permute-start | bytes 1327112 | tf_op jit(solution)/shard_map/ppermute | solution.py:876
  365.0 7.2 %collective-permute-start.36 = (bf16[2,96,1152]{2,1,0:T(8,128)(2,1)S(1)}, bf16[2,96,1152]{2,1,0:T(8,128)(2,1)S(1)}, u32[]{:S(2)}, u32[]{:S(2)}) collective-permute-start(bf16[2,96,1152]{2,1,0:T(8,128)(2,1)S(1)} %add_convert_fusion.5), channel_id=1, source_target_pairs={{0,2},{1,3},{6,4},{7,5},{8,10},{9,11},{14,12},{15,13},{16,18},{17,... | collective-permute-start | bytes 1327112 | tf_op jit(solution)/shard_map/ppermute | solution.py:876
  366.5 52.3 %copy-start.3 = (bf16[2,96,1152]{2,1,0:T(8,128)(2,1)}, bf16[2,96,1152]{2,1,0:T(8,128)(2,1)S(1)}, u32[]{:S(2)}) copy-start(bf16[2,96,1152]{2,1,0:T(8,128)(2,1)S(1)} %broadcast_select_fusion.3.refs_0_) | copy-start | bytes 1327108
  366.5 43.2 %copy-start.2 = (bf16[384,1152]{1,0:T(8,128)(2,1)S(1)}, bf16[384,1152]{1,0:T(8,128)(2,1)}, u32[]{:S(2)}) copy-start(bf16[384,1152]{1,0:T(8,128)(2,1)} %get-tuple-element.172.refs_3_.refs_11_.refs_7_) | copy-start | bytes 2654212
  372.2 0.8 collective-permute-start.42
  373.0 19.4 %collective-permute-start.41 = (bf16[2,96,1152]{2,1,0:T(8,128)(2,1)S(1)}, bf16[2,96,1152]{2,1,0:T(8,128)(2,1)S(1)}, u32[]{:S(2)}, u32[]{:S(2)}) collective-permute-start(bf16[2,96,1152]{2,1,0:T(8,128)(2,1)S(1)} %add_convert_fusion.3), channel_id=1, source_target_pairs={{2,0},{3,1},{4,6},{5,7},{10,8},{11,9},{12,14},{13,15},{18,16},{19,... | collective-permute-start | bytes 1327112 | tf_op jit(solution)/shard_map/ppermute | solution.py:876
  392.4 1.5 collective-permute-start.40
  394.0 15.7 %collective-permute-start.47 = (bf16[2,96,1152]{2,1,0:T(8,128)(2,1)S(1)}, bf16[2,96,1152]{2,1,0:T(8,128)(2,1)S(1)}, u32[]{:S(2)}, u32[]{:S(2)}) collective-permute-start(bf16[2,96,1152]{2,1,0:T(8,128)(2,1)S(1)} %add_convert_fusion.1), channel_id=1, source_target_pairs={{2,0},{3,1},{4,6},{5,7},{10,8},{11,9},{12,14},{13,15},{18,16},{19,... | collective-permute-start | bytes 1327112 | tf_op jit(solution)/shard_map/ppermute | solution.py:876
  395.6 42.4 %collective-permute-start.51 = (bf16[384,1536]{1,0:T(8,128)(2,1)S(1)}, bf16[384,1536]{1,0:T(8,128)(2,1)S(1)}, u32[]{:S(2)}, u32[]{:S(2)}) collective-permute-start(bf16[384,1536]{1,0:T(8,128)(2,1)S(1)} %copy-done.9), channel_id=1, source_target_pairs={{0,8},{8,0},{16,24},{24,16},{1,9},{9,1},{17,25},{25,17},{2,10},{10... | collective-permute-start | bytes 3538952 | tf_op jit(solution)/shard_map/ppermute | solution.py:858
  395.7 43.3 %collective-permute-start.53 = (bf16[384,1536]{1,0:T(8,128)(2,1)S(1)}, bf16[384,1536]{1,0:T(8,128)(2,1)S(1)}, u32[]{:S(2)}, u32[]{:S(2)}) collective-permute-start(bf16[384,1536]{1,0:T(8,128)(2,1)S(1)} %collective-permute-done.52.refs_10_), channel_id=1, source_target_pairs={{0,8},{8,0},{16,24},{24,16},{1,9},{9,1},{17,25},{25,17},{2,10},{10... | collective-permute-start | bytes 3538952 | tf_op jit(solution)/shard_map/ppermute | solution.py:858
  396.2 14.3 %collective-permute-start.48 = (bf16[384,1152]{1,0:T(8,128)(2,1)S(1)}, bf16[384,1152]{1,0:T(8,128)(2,1)S(1)}, u32[]{:S(2)}, u32[]{:S(2)}) collective-permute-start(bf16[384,1152]{1,0:T(8,128)(2,1)S(1)} %copy-done), channel_id=1, source_target_pairs={{0,8},{8,0},{16,24},{24,16},{1,9},{9,1},{17,25},{25,17},{2,10},{10... | collective-permute-start | bytes 2654216 | tf_op jit(solution)/shard_map/ppermute | solution.py:858
  396.3 22.5 %collective-permute-start.49 = (bf16[384,1152]{1,0:T(8,128)(2,1)S(1)}, bf16[384,1152]{1,0:T(8,128)(2,1)S(1)}, u32[]{:S(2)}, u32[]{:S(2)}) collective-permute-start(bf16[384,1152]{1,0:T(8,128)(2,1)S(1)} %copy-done.1), channel_id=1, source_target_pairs={{0,16},{8,24},{16,0},{24,8},{1,17},{9,25},{17,1},{25,9},{2,18},{10... | collective-permute-start | bytes 2654216 | tf_op jit(solution)/shard_map/ppermute | solution.py:858
  409.7 27.0 %collective-permute-start.50 = (bf16[384,1152]{1,0:T(8,128)(2,1)S(1)}, bf16[384,1152]{1,0:T(8,128)(2,1)S(1)}, u32[]{:S(2)}, u32[]{:S(2)}) collective-permute-start(bf16[384,1152]{1,0:T(8,128)(2,1)S(1)} %copy-done.2), channel_id=1, source_target_pairs={{0,24},{8,16},{16,8},{24,0},{1,25},{9,17},{17,9},{25,1},{2,26},{10... | collective-permute-start | bytes 2654216 | tf_op jit(solution)/shard_map/ppermute | solution.py:858
  410.5 47.4 %collective-permute-start.56 = (bf16[2,96,1152]{2,1,0:T(8,128)(2,1)}, bf16[2,96,1152]{2,1,0:T(8,128)(2,1)}, u32[]{:S(2)}, u32[]{:S(2)}) collective-permute-start(bf16[2,96,1152]{2,1,0:T(8,128)(2,1)} %broadcast_select_fusion.2.refs_1_), channel_id=1, source_target_pairs={{0,1},{1,0},{2,3},{3,2},{4,5},{5,4},{6,7},{7,6},{8,9},{9,8},{10,11... | collective-permute-start | bytes 1327112 | tf_op jit(solution)/shard_map/ppermute | solution.py:858
  418.8 39.1 %collective-permute-start.55 = (bf16[2,96,1152]{2,1,0:T(8,128)(2,1)S(1)}, bf16[2,96,1152]{2,1,0:T(8,128)(2,1)S(1)}, u32[]{:S(2)}, u32[]{:S(2)}) collective-permute-start(bf16[2,96,1152]{2,1,0:T(8,128)(2,1)S(1)} %broadcast_select_fusion.3.refs_0_), channel_id=1, source_target_pairs={{0,1},{1,0},{2,3},{3,2},{4,5},{5,4},{6,7},{7,6},{8,9},{9,8},{10,11... | collective-permute-start | bytes 1327112 | tf_op jit(solution)/shard_map/ppermute | solution.py:858
  436.7 20.2 %collective-permute-start.43 = (bf16[2,96,1152]{2,1,0:T(8,128)(2,1)S(1)}, bf16[2,96,1152]{2,1,0:T(8,128)(2,1)S(1)}, u32[]{:S(2)}, u32[]{:S(2)}) collective-permute-start(bf16[2,96,1152]{2,1,0:T(8,128)(2,1)S(1)} %add_convert_fusion), channel_id=1, source_target_pairs={{2,0},{3,1},{4,6},{5,7},{10,8},{11,9},{12,14},{13,15},{18,16},{19,... | collective-permute-start | bytes 1327112 | tf_op jit(solution)/shard_map/ppermute | solution.py:876
  438.0 19.9 %collective-permute-start.57 = (bf16[2,96,1152]{2,1,0:T(8,128)(2,1)}, bf16[2,96,1152]{2,1,0:T(8,128)(2,1)S(1)}, u32[]{:S(2)}, u32[]{:S(2)}) collective-permute-start(bf16[2,96,1152]{2,1,0:T(8,128)(2,1)} %broadcast_select_fusion.1.refs_2_), channel_id=1, source_target_pairs={{0,1},{1,0},{2,3},{3,2},{4,5},{5,4},{6,7},{7,6},{8,9},{9,8},{10,11... | collective-permute-start | bytes 1327112 | tf_op jit(solution)/shard_map/ppermute | solution.py:858
  456.9 13.1 %collective-permute-start.54 = (bf16[2,96,1152]{2,1,0:T(8,128)(2,1)S(1)}, bf16[2,96,1152]{2,1,0:T(8,128)(2,1)S(1)}, u32[]{:S(2)}, u32[]{:S(2)}) collective-permute-start(bf16[2,96,1152]{2,1,0:T(8,128)(2,1)S(1)} %broadcast_select_fusion.refs_0_), channel_id=1, source_target_pairs={{0,1},{1,0},{2,3},{3,2},{4,5},{5,4},{6,7},{7,6},{8,9},{9,8},{10,11... | collective-permute-start | bytes 1327112 | tf_op jit(solution)/shard_map/ppermute | solution.py:858
  476.6 1.9 collective-permute-start.58
  476.7 4.0 collective-permute-start.59
  478.5 3.4 collective-permute-start.60
  (31 other events, 573.4 us)

commit v3 on v2

--- a/solution.py
+++ b/solution.py
@@ -518,37 +518,35 @@
         heads = q_width // HD
         share = heads // (k_width // HD)
 
-        def group_step(group, carry):
-            kv_part = pl.ds(pl.multiple_of(group * HD, HD), HD)
-            for member in range(share):
-                head = group * share + member
-                part = pl.ds(pl.multiple_of(head * HD, HD), HD)
-                att_part = pl.ds(pl.multiple_of(q_width + 2 * k_width + head * HD, HD), HD)
-                for start in range(0, length, ROW_BLOCK):
-                    rows, seen = (slice(start, start + ROW_BLOCK), start + ROW_BLOCK)
-                    ga = heads_ref[rows, part]
-                    if fused:
-                        allowed = allowed_block(lengths, reach[layer], start, ROW_BLOCK, seen)
-                        rounded, slope = weigh(q_ref[rows, part], k_ref[:seen, kv_part], allowed)
-                        att = dot_nn(rounded, v_ref[:seen, kv_part]).astype(jnp.bfloat16)
-                    else:
-                        rounded = prob_ref[head, rows, :seen]
-                        slope = slope_ref[head, rows, :seen]
-                        att = att_ref[rows, part]
-                    shared_ref[rows, att_part] = att
-                    delta = jnp.sum(
-                        ga.astype(jnp.float32) * att.astype(jnp.float32), axis=-1, keepdims=True
-                    )
-                    grad_probs = dot_nt(ga, v_ref[:seen, kv_part])
-                    grad_scores = (slope * (grad_probs - delta)).astype(jnp.bfloat16)
-                    gq = unturn(dot_nn(grad_scores, k_ref[:seen, kv_part]), rows)
-                    factor_ref[rows, part] = gq.astype(jnp.bfloat16)
-                    shared_ref[rows, part] = (gq * recip[rows]).astype(jnp.bfloat16)
-                    dk[:seen, kv_part] += contract_rows(grad_scores, q_ref[rows, part])
-                    dv[:seen, kv_part] += contract_rows(rounded, ga)
+        def head_step(head, carry):
+            part = pl.ds(pl.multiple_of(head * HD, HD), HD)
+            kv_part = pl.ds(pl.multiple_of((head // share) * HD, HD), HD)
+            att_part = pl.ds(pl.multiple_of(q_width + 2 * k_width + head * HD, HD), HD)
+            for start in range(0, length, ROW_BLOCK):
+                rows, seen = (slice(start, start + ROW_BLOCK), start + ROW_BLOCK)
+                ga = heads_ref[rows, part]
+                if fused:
+                    allowed = allowed_block(lengths, reach[layer], start, ROW_BLOCK, seen)
+                    rounded, slope = weigh(q_ref[rows, part], k_ref[:seen, kv_part], allowed)
+                    att = dot_nn(rounded, v_ref[:seen, kv_part]).astype(jnp.bfloat16)
+                else:
+                    rounded = prob_ref[head, rows, :seen]
+                    slope = slope_ref[head, rows, :seen]
+                    att = att_ref[rows, part]
+                shared_ref[rows, att_part] = att
+                delta = jnp.sum(
+                    ga.astype(jnp.float32) * att.astype(jnp.float32), axis=-1, keepdims=True
+                )
+                grad_probs = dot_nt(ga, v_ref[:seen, kv_part])
+                grad_scores = (slope * (grad_probs - delta)).astype(jnp.bfloat16)
+                gq = unturn(dot_nn(grad_scores, k_ref[:seen, kv_part]), rows)
+                factor_ref[rows, part] = gq.astype(jnp.bfloat16)
+                shared_ref[rows, part] = (gq * recip[rows]).astype(jnp.bfloat16)
+                dk[:seen, kv_part] += contract_rows(grad_scores, q_ref[rows, part])
+                dv[:seen, kv_part] += contract_rows(rounded, ga)
             return carry
 
-        lax.fori_loop(0, k_width // HD, group_step, 0)
+        lax.fori_loop(0, heads, head_step, 0)
         every = slice(0, length)
         for kv in range(k_width // HD):
             kv_part = slice(kv * HD, (kv + 1) * HD)
@@ -950,10 +948,11 @@
         )
         return (result[:count], result[count : count + 3], result[-1])
 
-    def weights(layer, factors, sent, tie):
+    def weights(layer, factors, sent, tie, first_tile=0, tiles=3):
         sent = [after(sent[0], tie)] + sent[1:]
         return weights_call(
-            layer, layers, normed[layer], sent, factors, q_width, k_width, grads, 0, 3
+            layer, layers, normed[layer], sent, factors, q_width, k_width, grads, first_tile,
+            tiles,
         )
 
     pieces, heads, recip = project(top, layer_inputs)
@@ -1010,13 +1009,14 @@
                     )
                     wave.last = saved[0]
                 else:
-                    grads = weights(layer, factors, sent, wave.last)
+                    grads = weights(layer, factors, sent, wave.last, 0, 2)
                     wave.last = grads[1]
         *upstream, gain_part = result
         waiting = (layer, factors, sent)
         if layer:
             heads, recip = (next_heads, next_recip)
         gains[layer] = gain_part
+    grads = weights(*waiting, gain_part, 2, 1)
     gain_rows = jnp.stack([jnp.sum(part, axis=0) for part in lax.optimization_barrier(gains)])
     beside, across, corner = (
         xor_send(gain_rows, "dp", mask) for mask in range(1, 4)

time: 486 us -> 497 us (1.023)
  Pallas kernels: 133 us -> 138 us
    pallas_call x2 -> x3, Pallas kernels: 25.7 us -> 29.6 us  [weights_call(): pl.pallas_call(functools.partial(weights_kernel, count, count), grid=(til...]
  transfers between devices with their start and end apart: 61 -> 61, of which waited for: 26 -> 24; matrix products, arithmetic and copies ran while one was open for 1% -> 1% of each run, Pallas kernels for 19% -> 19%
where the time goes in v3:
time: 497 us; the launch traced here: 489 us
  waiting for transfers between devices  236 us (47%)
  Pallas kernels  138 us (28%)
  starting transfers between devices  103 us (21%)
  other arithmetic  7.02 us (1%)
    ppermute x24, waiting for transfers between devices, along_line(): lax.ppermute(x, 'tp', [(2 * a + side, 2 * b + side) for a, b in pairs for...  173 us
    ppermute x24, starting transfers between devices, along_line(): lax.ppermute(x, 'tp', [(2 * a + side, 2 * b + side) for a, b in pairs for...  66.3 us
    ppermute x37, waiting for transfers between devices, xor_send(): lax.ppermute(x, axis, [(i, i ^ mask) for i in range(lax.axis_size(axis))])  63.3 us
    pallas_call x2, Pallas kernels, attention_call(): pl.pallas_call(functools.partial(attention_kernel, layer, flat, fused, ch...  48 us
    ppermute x37, starting transfers between devices, xor_send(): lax.ppermute(x, axis, [(i, i ^ mask) for i in range(lax.axis_size(axis))])  37 us
    pallas_call x4, Pallas kernels, norm_call(): pl.pallas_call(functools.partial(norm_kernel, layer, flat, keep, steps, c...  30.6 us
    pallas_call x3, Pallas kernels, weights_call(): pl.pallas_call(functools.partial(weights_kernel, count, count), grid=(til...  29.6 us
    pallas_call x2, Pallas kernels, project_call(): pl.pallas_call(functools.partial(project_kernel, layer, depth), grid_spec...  23.5 us
  transfers between devices with their start and end apart: 61, of which 24 were waited for; matrix products, arithmetic and copies ran while one was open for 1% of the time, Pallas kernels for 19%

profile of v3, /device:TPU:0, one launch (start us, length us, event | category | flops | bytes accessed | tf_op | source)
XLA Modules:
  0.0 489.2 jit_solution(15422053637893969651)
XLA Ops:
  0.6 11.7 %shard_map.145 = (bf16[384,1152]{1,0:T(8,128)(2,1)}, bf16[384,1152]{1,0:T(8,128)(2,1)}, bf16[384,1152]{1,0:T(8,128)(2,1)}, bf16[384,1152]{1,0:T(8,128)(2,1)}, bf...) custom-call(s32[1]{0:T(128)} %bitcast.1.rank, ...), custom_call_target="tpu_custom_call" | custom-call | flops 3623878656 | bytes 17825792 | tf_op jit(solution)/shard_map/pallas_call | solution.py:374
  12.4 26.1 %shard_map.146 = (bf16[384,1536]{1,0:T(8,128)(2,1)}, bf16[2,96,1152]{2,1,0:T(8,128)(2,1)}, bf16[2,96,1152]{2,1,0:T(8,128)(2,1)}, bf16[2,96,1152]{2,1,0:T(8,128)(...) custom-call(s32[1]{0:T(128)} %bitcast.side, ...), custom_call_target="tpu_custom_call" | custom-call | flops 5435817984 | bytes 20971520 | tf_op jit(solution)/shard_map/pallas_call | solution.py:636
  38.4 3.1 collective-permute-start.1
  41.6 1.9 collective-permute-start.6
  43.6 11.7 %shard_map.147 = (bf16[384,1152]{1,0:T(8,128)(2,1)}, bf16[384,1152]{1,0:T(8,128)(2,1)}, bf16[384,1152]{1,0:T(8,128)(2,1)}, bf16[384,1152]{1,0:T(8,128)(2,1)}, bf...) custom-call(s32[1]{0:T(128)} %bitcast.1.rank, ...), custom_call_target="tpu_custom_call" | custom-call | flops 3623878656 | bytes 17825792 | tf_op jit(solution)/shard_map/pallas_call | solution.py:374
  55.4 2.0 collective-permute-start.23
  57.5 4.7 collective-permute-done.3
  62.2 4.0 collective-permute-start.2
  66.3 7.4 %collective-permute-done.2 = bf16[2,96,1152]{2,1,0:T(8,128)(2,1)S(1)} collective-permute-done((bf16[2,96,1152]{2,1,0:T(8,128)(2,1)S(1)}, bf16[2,96,1152]{2,1,0:T(8,128)(2,1)S(1)}, u32[]{:S(2)}, u32[]{:S(2)}) %collective-permute-start.2) | collective-permute-done | bytes 442400 | tf_op jit(solution)/shard_map/ppermute | solution.py:874
  73.8 4.4 collective-permute-start.5
  78.4 9.8 %collective-permute-done.5 = bf16[2,96,1152]{2,1,0:T(8,128)(2,1)S(1)} collective-permute-done((bf16[2,96,1152]{2,1,0:T(8,128)(2,1)S(1)}, bf16[2,96,1152]{2,1,0:T(8,128)(2,1)S(1)}, u32[]{:S(2)}, u32[]{:S(2)}) %collective-permute-start.5) | collective-permute-done | bytes 442400 | tf_op jit(solution)/shard_map/ppermute | solution.py:874
  89.0 1.9 collective-permute-start.29
  90.9 17.4 %collective-permute-start.10 = (bf16[2,96,1152]{2,1,0:T(8,128)(2,1)S(1)}, bf16[2,96,1152]{2,1,0:T(8,128)(2,1)S(1)}, u32[]{:S(2)}, u32[]{:S(2)}) collective-permute-start(bf16[2,96,1152]{2,1,0:T(8,128)(2,1)S(1)} %add_convert_fusion.20), channel_id=1, source_target_pairs={{0,2},{1,3},{6,4},{7,5},{8,10},{9,11},{14,12},{15,13},{16,18},{17,... | collective-permute-start | bytes 1327112 | tf_op jit(solution)/shard_map/ppermute | solution.py:874
  108.5 8.6 %collective-permute-done.10 = bf16[2,96,1152]{2,1,0:T(8,128)(2,1)S(1)} collective-permute-done((bf16[2,96,1152]{2,1,0:T(8,128)(2,1)S(1)}, bf16[2,96,1152]{2,1,0:T(8,128)(2,1)S(1)}, u32[]{:S(2)}, u32[]{:S(2)}) %collective-permute-start.10) | collective-permute-done | bytes 442400 | tf_op jit(solution)/shard_map/ppermute | solution.py:874
  117.9 1.3 collective-permute-start.8
  119.3 21.9 %collective-permute-done.8 = bf16[2,96,1152]{2,1,0:T(8,128)(2,1)S(1)} collective-permute-done((bf16[2,96,1152]{2,1,0:T(8,128)(2,1)S(1)}, bf16[2,96,1152]{2,1,0:T(8,128)(2,1)S(1)}, u32[]{:S(2)}, u32[]{:S(2)}) %collective-permute-start.8) | collective-permute-done | bytes 442400 | tf_op jit(solution)/shard_map/ppermute | solution.py:874
  141.1 1.5 collective-permute-start.7
  142.7 6.7 %collective-permute-done.7 = bf16[2,96,1152]{2,1,0:T(8,128)(2,1)S(1)} collective-permute-done((bf16[2,96,1152]{2,1,0:T(8,128)(2,1)S(1)}, bf16[2,96,1152]{2,1,0:T(8,128)(2,1)S(1)}, u32[]{:S(2)}, u32[]{:S(2)}) %collective-permute-start.7) | collective-permute-done | bytes 442400 | tf_op jit(solution)/shard_map/ppermute | solution.py:874
  150.2 1.3 collective-permute-start.12
  151.6 18.1 %collective-permute-done.12 = bf16[2,96,1152]{2,1,0:T(8,128)(2,1)S(1)} collective-permute-done((bf16[2,96,1152]{2,1,0:T(8,128)(2,1)S(1)}, bf16[2,96,1152]{2,1,0:T(8,128)(2,1)S(1)}, u32[]{:S(2)}, u32[]{:S(2)}) %collective-permute-start.12) | collective-permute-done | bytes 442400 | tf_op jit(solution)/shard_map/ppermute | solution.py:874
  170.4 1.3 collective-permute-start.15
  171.9 17.7 %collective-permute-done.15 = bf16[2,96,1152]{2,1,0:T(8,128)(2,1)S(1)} collective-permute-done((bf16[2,96,1152]{2,1,0:T(8,128)(2,1)S(1)}, bf16[2,96,1152]{2,1,0:T(8,128)(2,1)S(1)}, u32[]{:S(2)}, u32[]{:S(2)}) %collective-permute-start.15) | collective-permute-done | bytes 442400 | tf_op jit(solution)/shard_map/ppermute | solution.py:874
  189.6 1.5 collective-permute-start.14
  191.1 6.1 %shard_map.148 = (bf16[384,512]{1,0:T(8,128)(2,1)}, bf16[4,384,384]{2,1,0:T(8,128)(2,1)}, f32[4,384,384]{2,1,0:T(8,128)}) custom-call(s32[1,4]{1,0:T(1,128)} %lengths.1, s32[2]{0:T(128)} %reach.1, bf16[384,512]{1,0:T(8,128)(2,1)} %get-tuple-element.160.q_ref.refs_5_, bf16[384,256]{1,0:T(8,128)(2,1)} %get-tuple-element.161.k_ref.refs_6_, ...), custom_call_target="tpu_custom_call" | custom-call | flops 301989888 | bytes 6291456 | tf_op jit(solution)/shard_map/pallas_call | solution.py:450
  197.2 2.5 collective-permute-done.14
  199.8 1.3 collective-permute-start.18
  201.8 1.3 collective-permute-start.19
  204.0 8.8 %collective-permute-done.18.refs_4_ = bf16[2,96,1152]{2,1,0:T(8,128)(2,1)S(1)} collective-permute-done((bf16[2,96,1152]{2,1,0:T(8,128)(2,1)S(1)}, bf16[2,96,1152]{2,1,0:T(8,128)(2,1)S(1)}, u32[]{:S(2)}, u32[]{:S(2)}) %collective-permute-start.18) | collective-permute-done | bytes 442400 | tf_op jit(solution)/shard_map/ppermute | solution.py:856
  212.8 9.5 %collective-permute-done.17.refs_3_ = bf16[2,96,1152]{2,1,0:T(8,128)(2,1)S(1)} collective-permute-done((bf16[2,96,1152]{2,1,0:T(8,128)(2,1)S(1)}, bf16[2,96,1152]{2,1,0:T(8,128)(2,1)S(1)}, u32[]{:S(2)}, u32[]{:S(2)}) %collective-permute-start.17) | collective-permute-done | bytes 442400 | tf_op jit(solution)/shard_map/ppermute | solution.py:856
  222.3 5.0 %collective-permute-done.19.refs_5_ = bf16[2,96,1152]{2,1,0:T(8,128)(2,1)S(1)} collective-permute-done((bf16[2,96,1152]{2,1,0:T(8,128)(2,1)S(1)}, bf16[2,96,1152]{2,1,0:T(8,128)(2,1)S(1)}, u32[]{:S(2)}, u32[]{:S(2)}) %collective-permute-start.19) | collective-permute-done | bytes 442400 | tf_op jit(solution)/shard_map/ppermute | solution.py:856
  227.3 4.1 collective-permute-start.26
  232.1 10.7 %shard_map.149 = (bf16[384,1152]{1,0:T(8,128)(2,1)}, bf16[384,1152]{1,0:T(8,128)(2,1)}, bf16[384,1152]{1,0:T(8,128)(2,1)}, bf16[384,1152]{1,0:T(8,128)(2,1)}, f32[8,4608]{1,0:T(8,128)}) custom-call(s32[1]{0:T(128)} %bitcast.side, s32[1]{0:T(128)} %bitcast.1.rank, bf16[2,96,1152]{2,1,0:T(8,128)(2,1)} %copy-done.11, bf16[2,96,1152]{2,1,0:T(8,128)(2,1)} %copy-done.12, ...), custom_call_target="tpu_custom_call" | custom-call | flops 39813120 | bytes 12582912 | tf_op jit(solution)/shard_map/pallas_call | solution.py:770
  242.8 4.7 shard_map.150
  247.5 21.9 %shard_map.151 = (bf16[384,1536]{1,0:T(8,128)(2,1)}, bf16[2,96,1152]{2,1,0:T(8,128)(2,1)}, bf16[2,96,1152]{2,1,0:T(8,128)(2,1)}, bf16[2,96,1152]{2,1,0:T(8,128)(...) custom-call(s32[1]{0:T(128)} %bitcast.side, ...), custom_call_target="tpu_custom_call" | custom-call | flops 5435817984 | bytes 20971520 | tf_op jit(solution)/shard_map/pallas_call | solution.py:636
  269.4 4.2 collective-permute-start.44
  273.7 1.4 collective-permute-start.46
  275.0 1.4 collective-permute-start.21
  277.1 12.7 %shard_map.152 = (f32[2,1152,512]{2,1,0:T(8,128)}, f32[2,1152,256]{2,1,0:T(8,128)}, f32[2,1152,256]{2,1,0:T(8,128)}, f32[2,512,1152]{2,1,0:T(8,128)}) custom-call(bf16[384,1152]{1,0:T(8,128)(2,1)} %get-tuple-element.185.refs_0_, bf16[384,1152]{1,0:T(8,128)(2,1)} %collective-permute-done.22.refs_1_, bf16[384,1152]{1,0:T(8,128)(2,1)} %collective-permute-done.23.refs_2_, ...), custom_call_target="tpu_custom_call" | custom-call | flops 5435817984 | bytes 25165824 | tf_op jit(solution)/shard_map/pallas_call | solution.py:830
  289.8 1.4 collective-permute-start.35
  291.4 6.4 %collective-permute-done.32 = bf16[2,96,1152]{2,1,0:T(8,128)(2,1)S(1)} collective-permute-done((bf16[2,96,1152]{2,1,0:T(8,128)(2,1)}, bf16[2,96,1152]{2,1,0:T(8,128)(2,1)S(1)}, u32[]{:S(2)}, u32[]{:S(2)}) %collective-permute-start.32) | collective-permute-done | bytes 442400 | tf_op jit(solution)/shard_map/ppermute | solution.py:856
  297.8 1.8 collective-permute-start.31
  299.7 9.1 %collective-permute-done.31 = bf16[2,96,1152]{2,1,0:T(8,128)(2,1)S(1)} collective-permute-done((bf16[2,96,1152]{2,1,0:T(8,128)(2,1)S(1)}, bf16[2,96,1152]{2,1,0:T(8,128)(2,1)S(1)}, u32[]{:S(2)}, u32[]{:S(2)}) %collective-permute-start.31) | collective-permute-done | bytes 442400 | tf_op jit(solution)/shard_map/ppermute | solution.py:874
  308.8 1.4 collective-permute-start.20
  310.3 4.4 collective-permute-start.34
  314.8 8.1 %collective-permute-done.34 = bf16[2,96,1152]{2,1,0:T(8,128)(2,1)S(1)} collective-permute-done((bf16[2,96,1152]{2,1,0:T(8,128)(2,1)S(1)}, bf16[2,96,1152]{2,1,0:T(8,128)(2,1)S(1)}, u32[]{:S(2)}, u32[]{:S(2)}) %collective-permute-start.34) | collective-permute-done | bytes 442400 | tf_op jit(solution)/shard_map/ppermute | solution.py:874
  323.9 15.3 %collective-permute-start.39 = (bf16[2,96,1152]{2,1,0:T(8,128)(2,1)S(1)}, bf16[2,96,1152]{2,1,0:T(8,128)(2,1)S(1)}, u32[]{:S(2)}, u32[]{:S(2)}) collective-permute-start(bf16[2,96,1152]{2,1,0:T(8,128)(2,1)S(1)} %add_convert_fusion.8), channel_id=1, source_target_pairs={{0,2},{1,3},{6,4},{7,5},{8,10},{9,11},{14,12},{15,13},{16,18},{17,... | collective-permute-start | bytes 1327112 | tf_op jit(solution)/shard_map/ppermute | solution.py:874
  339.3 6.4 %collective-permute-done.39 = bf16[2,96,1152]{2,1,0:T(8,128)(2,1)S(1)} collective-permute-done((bf16[2,96,1152]{2,1,0:T(8,128)(2,1)S(1)}, bf16[2,96,1152]{2,1,0:T(8,128)(2,1)S(1)}, u32[]{:S(2)}, u32[]{:S(2)}) %collective-permute-start.39) | collective-permute-done | bytes 442400 | tf_op jit(solution)/shard_map/ppermute | solution.py:874
  346.5 1.3 collective-permute-start.37
  347.9 18.0 %collective-permute-done.37 = bf16[2,96,1152]{2,1,0:T(8,128)(2,1)S(1)} collective-permute-done((bf16[2,96,1152]{2,1,0:T(8,128)(2,1)S(1)}, bf16[2,96,1152]{2,1,0:T(8,128)(2,1)S(1)}, u32[]{:S(2)}, u32[]{:S(2)}) %collective-permute-start.37) | collective-permute-done | bytes 442400 | tf_op jit(solution)/shard_map/ppermute | solution.py:874
  365.9 1.5 collective-permute-start.36
  368.2 4.9 %collective-permute-done.36 = bf16[2,96,1152]{2,1,0:T(8,128)(2,1)S(1)} collective-permute-done((bf16[2,96,1152]{2,1,0:T(8,128)(2,1)S(1)}, bf16[2,96,1152]{2,1,0:T(8,128)(2,1)S(1)}, u32[]{:S(2)}, u32[]{:S(2)}) %collective-permute-start.36) | collective-permute-done | bytes 442400 | tf_op jit(solution)/shard_map/ppermute | solution.py:874
  375.4 18.0 %collective-permute-done.41 = bf16[2,96,1152]{2,1,0:T(8,128)(2,1)S(1)} collective-permute-done((bf16[2,96,1152]{2,1,0:T(8,128)(2,1)S(1)}, bf16[2,96,1152]{2,1,0:T(8,128)(2,1)S(1)}, u32[]{:S(2)}, u32[]{:S(2)}) %collective-permute-start.41) | collective-permute-done | bytes 442400 | tf_op jit(solution)/shard_map/ppermute | solution.py:874
  394.9 1.5 collective-permute-start.47
  397.8 1.7 collective-permute-start.49
  399.6 15.6 %collective-permute-done.47 = bf16[2,96,1152]{2,1,0:T(8,128)(2,1)S(1)} collective-permute-done((bf16[2,96,1152]{2,1,0:T(8,128)(2,1)S(1)}, bf16[2,96,1152]{2,1,0:T(8,128)(2,1)S(1)}, u32[]{:S(2)}, u32[]{:S(2)}) %collective-permute-start.47) | collective-permute-done | bytes 442400 | tf_op jit(solution)/shard_map/ppermute | solution.py:874
  417.8 2.6 collective-permute-done.49.refs_6_
  421.0 17.2 %collective-permute-done.50.refs_7_ = bf16[384,1152]{1,0:T(8,128)(2,1)S(1)} collective-permute-done((bf16[384,1152]{1,0:T(8,128)(2,1)S(1)}, bf16[384,1152]{1,0:T(8,128)(2,1)S(1)}, u32[]{:S(2)}, u32[]{:S(2)}) %collective-permute-start.50) | collective-permute-done | bytes 884768 | tf_op jit(solution)/shard_map/ppermute | solution.py:856
  438.9 1.4 collective-permute-start.57
  441.4 10.1 %shard_map.153 = (f32[2,1152,512]{2,1,0:T(8,128)}, f32[2,1152,256]{2,1,0:T(8,128)}, f32[2,1152,256]{2,1,0:T(8,128)}, f32[2,512,1152]{2,1,0:T(8,128)}) custom-call(bf16[384,1152]{1,0:T(8,128)(2,1)} %get-tuple-element.219.refs_0_, bf16[384,1152]{1,0:T(8,128)(2,1)} %copy-done.7, ...), custom_call_target="tpu_custom_call", output_to_operand_aliasing={{0}: (12, {}), {1}: (13, {}), {2}: (14, {}), {3}: (15, {})} | custom-call | flops 3623878656 | bytes 16777216 | tf_op jit(solution)/shard_map/pallas_call | solution.py:830
  452.7 8.3 %collective-permute-done.57.refs_5_ = bf16[2,96,1152]{2,1,0:T(8,128)(2,1)S(1)} collective-permute-done((bf16[2,96,1152]{2,1,0:T(8,128)(2,1)S(1)}, bf16[2,96,1152]{2,1,0:T(8,128)(2,1)S(1)}, u32[]{:S(2)}, u32[]{:S(2)}) %collective-permute-start.57) | collective-permute-done | bytes 442400 | tf_op jit(solution)/shard_map/ppermute | solution.py:856
  462.7 10.5 %shard_map.154 = (bf16[384,4608]{1,0:T(8,128)(2,1)}, f32[8,4608]{1,0:T(8,128)}) custom-call(s32[1]{0:T(128)} %bitcast.side, s32[1]{0:T(128)} %bitcast.1.rank, bf16[2,96,1152]{2,1,0:T(8,128)(2,1)} %broadcast_select_fusion.3.refs_0_, bf16[2,96,1152]{2,1,0:T(8,128)(2,1)} %broadcast_select_fusion.2.refs_1_, bf16[2,96,1152]{2,1,0:T(8,128)(2,1)} %copy-done.15, ...), custom_call_target="tpu_custom_call" | custom-call | flops 39813120 | bytes 12582912 | tf_op jit(solution)/shard_map/pallas_call | solution.py:770
  474.0 4.7 shard_map.155
  479.9 1.8 collective-permute-start.59
  481.7 6.7 %shard_map.156 = (f32[2,1152,512]{2,1,0:T(8,128)}, f32[2,1152,256]{2,1,0:T(8,128)}, f32[2,1152,256]{2,1,0:T(8,128)}, f32[2,512,1152]{2,1,0:T(8,128)}) custom-call(bf16[384,1152]{1,0:T(8,128)(2,1)} %get-tuple-element.219.refs_0_, bf16[384,1152]{1,0:T(8,128)(2,1)} %copy-done.7, ...), custom_call_target="tpu_custom_call", output_to_operand_aliasing={{0}: (12, {}), {1}: (13, {}), {2}: (14, {}), {3}: (15, {})} | custom-call | flops 1811939328 | bytes 8388608 | tf_op jit(solution)/shard_map/pallas_call | solution.py:830
  (180 shorter events, 26.2 us)
Async XLA Ops:
  38.4 16.9 %collective-permute-start.1 = (bf16[2,96,1152]{2,1,0:T(8,128)(2,1)}, bf16[2,96,1152]{2,1,0:T(8,128)(2,1)S(1)}, u32[]{:S(2)}, u32[]{:S(2)}) collective-permute-start(bf16[2,96,1152]{2,1,0:T(8,128)(2,1)} %get-tuple-element.137), channel_id=1, source_target_pairs={{0,1},{1,0},{2,3},{3,2},{4,5},{5,4},{6,7},{7,6},{8,9},{9,8},{10,11... | collective-permute-start | bytes 1327112 | tf_op jit(solution)/shard_map/ppermute | solution.py:856
  41.5 20.7 %collective-permute-start.3 = (bf16[2,96,1152]{2,1,0:T(8,128)(2,1)}, bf16[2,96,1152]{2,1,0:T(8,128)(2,1)S(1)}, u32[]{:S(2)}, u32[]{:S(2)}) collective-permute-start(bf16[2,96,1152]{2,1,0:T(8,128)(2,1)} %get-tuple-element.143), channel_id=1, source_target_pairs={{0,1},{1,0},{2,3},{3,2},{4,5},{5,4},{6,7},{7,6},{8,9},{9,8},{10,11... | collective-permute-start | bytes 1327112 | tf_op jit(solution)/shard_map/ppermute | solution.py:856
  41.6 32.3 %collective-permute-start.6 = (bf16[2,96,1152]{2,1,0:T(8,128)(2,1)}, bf16[2,96,1152]{2,1,0:T(8,128)(2,1)S(1)}, u32[]{:S(2)}, u32[]{:S(2)}) collective-permute-start(bf16[2,96,1152]{2,1,0:T(8,128)(2,1)} %get-tuple-element.147), channel_id=1, source_target_pairs={{0,1},{1,0},{2,3},{3,2},{4,5},{5,4},{6,7},{7,6},{8,9},{9,8},{10,11... | collective-permute-start | bytes 1327112 | tf_op jit(solution)/shard_map/ppermute | solution.py:856
  43.5 47.4 %collective-permute-start = (bf16[2,96,1152]{2,1,0:T(8,128)(2,1)}, bf16[2,96,1152]{2,1,0:T(8,128)(2,1)S(1)}, u32[]{:S(2)}, u32[]{:S(2)}) collective-permute-start(bf16[2,96,1152]{2,1,0:T(8,128)(2,1)} %get-tuple-element.135), channel_id=1, source_target_pairs={{0,1},{1,0},{2,3},{3,2},{4,5},{5,4},{6,7},{7,6},{8,9},{9,8},{10,11... | collective-permute-start | bytes 1327112 | tf_op jit(solution)/shard_map/ppermute | solution.py:856
  43.6 157.5 %collective-permute-start.22 = (bf16[384,1152]{1,0:T(8,128)(2,1)}, bf16[384,1152]{1,0:T(8,128)(2,1)}, u32[]{:S(2)}, u32[]{:S(2)}) collective-permute-start(bf16[384,1152]{1,0:T(8,128)(2,1)} %get-tuple-element.186), channel_id=1, source_target_pairs={{0,8},{8,0},{16,24},{24,16},{1,9},{9,1},{17,25},{25,17},{2,10},{10... | collective-permute-start | bytes 2654216 | tf_op jit(solution)/shard_map/ppermute | solution.py:856
  55.4 146.4 %collective-permute-start.23 = (bf16[384,1152]{1,0:T(8,128)(2,1)}, bf16[384,1152]{1,0:T(8,128)(2,1)}, u32[]{:S(2)}, u32[]{:S(2)}) collective-permute-start(bf16[384,1152]{1,0:T(8,128)(2,1)} %get-tuple-element.187), channel_id=1, source_target_pairs={{0,16},{8,24},{16,0},{24,8},{1,17},{9,25},{17,1},{25,9},{2,18},{10... | collective-permute-start | bytes 2654216 | tf_op jit(solution)/shard_map/ppermute | solution.py:856
  62.2 11.5 %collective-permute-start.2 = (bf16[2,96,1152]{2,1,0:T(8,128)(2,1)S(1)}, bf16[2,96,1152]{2,1,0:T(8,128)(2,1)S(1)}, u32[]{:S(2)}, u32[]{:S(2)}) collective-permute-start(bf16[2,96,1152]{2,1,0:T(8,128)(2,1)S(1)} %add_convert_fusion.23), channel_id=1, source_target_pairs={{0,2},{1,3},{6,4},{7,5},{8,10},{9,11},{14,12},{15,13},{16,18},{17,... | collective-permute-start | bytes 1327112 | tf_op jit(solution)/shard_map/ppermute | solution.py:874
  73.7 130.3 %collective-permute-start.24 = (bf16[384,1152]{1,0:T(8,128)(2,1)}, bf16[384,1152]{1,0:T(8,128)(2,1)}, u32[]{:S(2)}, u32[]{:S(2)}) collective-permute-start(bf16[384,1152]{1,0:T(8,128)(2,1)} %get-tuple-element.188), channel_id=1, source_target_pairs={{0,24},{8,16},{16,8},{24,0},{1,25},{9,17},{17,9},{25,1},{2,26},{10... | collective-permute-start | bytes 2654216 | tf_op jit(solution)/shard_map/ppermute | solution.py:856
  73.8 14.3 %collective-permute-start.5 = (bf16[2,96,1152]{2,1,0:T(8,128)(2,1)S(1)}, bf16[2,96,1152]{2,1,0:T(8,128)(2,1)S(1)}, u32[]{:S(2)}, u32[]{:S(2)}) collective-permute-start(bf16[2,96,1152]{2,1,0:T(8,128)(2,1)S(1)} %add_convert_fusion.22), channel_id=1, source_target_pairs={{0,2},{1,3},{6,4},{7,5},{8,10},{9,11},{14,12},{15,13},{16,18},{17,... | collective-permute-start | bytes 1327112 | tf_op jit(solution)/shard_map/ppermute | solution.py:874
  88.2 0.8 collective-permute-start.4
  89.0 114.2 %collective-permute-start.29 = (bf16[384,1536]{1,0:T(8,128)(2,1)}, bf16[384,1536]{1,0:T(8,128)(2,1)}, u32[]{:S(2)}, u32[]{:S(2)}) collective-permute-start(bf16[384,1536]{1,0:T(8,128)(2,1)} %get-tuple-element.198.refs_8_), channel_id=1, source_target_pairs={{0,16},{8,24},{16,0},{24,8},{1,17},{9,25},{17,1},{25,9},{2,18},{10... | collective-permute-start | bytes 3538952 | tf_op jit(solution)/shard_map/ppermute | solution.py:856
  90.9 26.1 %collective-permute-start.10 = (bf16[2,96,1152]{2,1,0:T(8,128)(2,1)S(1)}, bf16[2,96,1152]{2,1,0:T(8,128)(2,1)S(1)}, u32[]{:S(2)}, u32[]{:S(2)}) collective-permute-start(bf16[2,96,1152]{2,1,0:T(8,128)(2,1)S(1)} %add_convert_fusion.20), channel_id=1, source_target_pairs={{0,2},{1,3},{6,4},{7,5},{8,10},{9,11},{14,12},{15,13},{16,18},{17,... | collective-permute-start | bytes 1327112 | tf_op jit(solution)/shard_map/ppermute | solution.py:874
  117.0 0.8 collective-permute-start.9
  117.9 23.3 %collective-permute-start.8 = (bf16[2,96,1152]{2,1,0:T(8,128)(2,1)S(1)}, bf16[2,96,1152]{2,1,0:T(8,128)(2,1)S(1)}, u32[]{:S(2)}, u32[]{:S(2)}) collective-permute-start(bf16[2,96,1152]{2,1,0:T(8,128)(2,1)S(1)} %add_convert_fusion.18), channel_id=1, source_target_pairs={{2,0},{3,1},{4,6},{5,7},{10,8},{11,9},{12,14},{13,15},{18,16},{19,... | collective-permute-start | bytes 1327112 | tf_op jit(solution)/shard_map/ppermute | solution.py:874
  141.1 8.2 %collective-permute-start.7 = (bf16[2,96,1152]{2,1,0:T(8,128)(2,1)S(1)}, bf16[2,96,1152]{2,1,0:T(8,128)(2,1)S(1)}, u32[]{:S(2)}, u32[]{:S(2)}) collective-permute-start(bf16[2,96,1152]{2,1,0:T(8,128)(2,1)S(1)} %add_convert_fusion.17), channel_id=1, source_target_pairs={{0,2},{1,3},{6,4},{7,5},{8,10},{9,11},{14,12},{15,13},{16,18},{17,... | collective-permute-start | bytes 1327112 | tf_op jit(solution)/shard_map/ppermute | solution.py:874
  142.7 58.4 %copy-start.11 = (bf16[2,96,1152]{2,1,0:T(8,128)(2,1)}, bf16[2,96,1152]{2,1,0:T(8,128)(2,1)S(1)}, u32[]{:S(2)}) copy-start(bf16[2,96,1152]{2,1,0:T(8,128)(2,1)S(1)} %broadcast_select_fusion.7.refs_0_) | copy-start | bytes 1327108
  149.4 0.8 collective-permute-start.13
  150.2 19.5 %collective-permute-start.12 = (bf16[2,96,1152]{2,1,0:T(8,128)(2,1)S(1)}, bf16[2,96,1152]{2,1,0:T(8,128)(2,1)S(1)}, u32[]{:S(2)}, u32[]{:S(2)}) collective-permute-start(bf16[2,96,1152]{2,1,0:T(8,128)(2,1)S(1)} %add_convert_fusion.15), channel_id=1, source_target_pairs={{2,0},{3,1},{4,6},{5,7},{10,8},{11,9},{12,14},{13,15},{18,16},{19,... | collective-permute-start | bytes 1327112 | tf_op jit(solution)/shard_map/ppermute | solution.py:874
  169.7 0.8 collective-permute-start.11
  170.4 19.1 %collective-permute-start.15 = (bf16[2,96,1152]{2,1,0:T(8,128)(2,1)S(1)}, bf16[2,96,1152]{2,1,0:T(8,128)(2,1)S(1)}, u32[]{:S(2)}, u32[]{:S(2)}) collective-permute-start(bf16[2,96,1152]{2,1,0:T(8,128)(2,1)S(1)} %add_convert_fusion.13), channel_id=1, source_target_pairs={{2,0},{3,1},{4,6},{5,7},{10,8},{11,9},{12,14},{13,15},{18,16},{19,... | collective-permute-start | bytes 1327112 | tf_op jit(solution)/shard_map/ppermute | solution.py:874
  189.6 10.2 %collective-permute-start.14 = (bf16[2,96,1152]{2,1,0:T(8,128)(2,1)S(1)}, bf16[2,96,1152]{2,1,0:T(8,128)(2,1)S(1)}, u32[]{:S(2)}, u32[]{:S(2)}) collective-permute-start(bf16[2,96,1152]{2,1,0:T(8,128)(2,1)S(1)} %add_convert_fusion.12), channel_id=1, source_target_pairs={{2,0},{3,1},{4,6},{5,7},{10,8},{11,9},{12,14},{13,15},{18,16},{19,... | collective-permute-start | bytes 1327112 | tf_op jit(solution)/shard_map/ppermute | solution.py:874
  199.8 13.0 %collective-permute-start.18 = (bf16[2,96,1152]{2,1,0:T(8,128)(2,1)S(1)}, bf16[2,96,1152]{2,1,0:T(8,128)(2,1)S(1)}, u32[]{:S(2)}, u32[]{:S(2)}) collective-permute-start(bf16[2,96,1152]{2,1,0:T(8,128)(2,1)S(1)} %broadcast_select_fusion.6.refs_1_), channel_id=1, source_target_pairs={{0,1},{1,0},{2,3},{3,2},{4,5},{5,4},{6,7},{7,6},{8,9},{9,8},{10,11... | collective-permute-start | bytes 1327112 | tf_op jit(solution)/shard_map/ppermute | solution.py:856
  201.1 21.2 %collective-permute-start.17 = (bf16[2,96,1152]{2,1,0:T(8,128)(2,1)S(1)}, bf16[2,96,1152]{2,1,0:T(8,128)(2,1)S(1)}, u32[]{:S(2)}, u32[]{:S(2)}) collective-permute-start(bf16[2,96,1152]{2,1,0:T(8,128)(2,1)S(1)} %broadcast_select_fusion.7.refs_0_), channel_id=1, source_target_pairs={{0,1},{1,0},{2,3},{3,2},{4,5},{5,4},{6,7},{7,6},{8,9},{9,8},{10,11... | collective-permute-start | bytes 1327112 | tf_op jit(solution)/shard_map/ppermute | solution.py:856
  201.8 25.5 %collective-permute-start.19 = (bf16[2,96,1152]{2,1,0:T(8,128)(2,1)S(1)}, bf16[2,96,1152]{2,1,0:T(8,128)(2,1)S(1)}, u32[]{:S(2)}, u32[]{:S(2)}) collective-permute-start(bf16[2,96,1152]{2,1,0:T(8,128)(2,1)S(1)} %broadcast_select_fusion.5.refs_2_), channel_id=1, source_target_pairs={{0,1},{1,0},{2,3},{3,2},{4,5},{5,4},{6,7},{7,6},{8,9},{9,8},{10,11... | collective-permute-start | bytes 1327112 | tf_op jit(solution)/shard_map/ppermute | solution.py:856
  203.2 28.8 %collective-permute-start.16 = (bf16[2,96,1152]{2,1,0:T(8,128)(2,1)S(1)}, bf16[2,96,1152]{2,1,0:T(8,128)(2,1)S(1)}, u32[]{:S(2)}, u32[]{:S(2)}) collective-permute-start(bf16[2,96,1152]{2,1,0:T(8,128)(2,1)S(1)} %broadcast_select_fusion.4.refs_0_), channel_id=1, source_target_pairs={{0,1},{1,0},{2,3},{3,2},{4,5},{5,4},{6,7},{7,6},{8,9},{9,8},{10,11... | collective-permute-start | bytes 1327112 | tf_op jit(solution)/shard_map/ppermute | solution.py:856
  204.0 71.1 %collective-permute-start.28 = (bf16[384,1536]{1,0:T(8,128)(2,1)}, bf16[384,1536]{1,0:T(8,128)(2,1)}, u32[]{:S(2)}, u32[]{:S(2)}) collective-permute-start(bf16[384,1536]{1,0:T(8,128)(2,1)} %get-tuple-element.198.refs_8_), channel_id=1, source_target_pairs={{0,8},{8,0},{16,24},{24,16},{1,9},{9,1},{17,25},{25,17},{2,10},{10... | collective-permute-start | bytes 3538952 | tf_op jit(solution)/shard_map/ppermute | solution.py:856
  212.8 63.6 %collective-permute-start.30 = (bf16[384,1536]{1,0:T(8,128)(2,1)}, bf16[384,1536]{1,0:T(8,128)(2,1)}, u32[]{:S(2)}, u32[]{:S(2)}) collective-permute-start(bf16[384,1536]{1,0:T(8,128)(2,1)} %collective-permute-done.29.refs_10_), channel_id=1, source_target_pairs={{0,8},{8,0},{16,24},{24,16},{1,9},{9,1},{17,25},{25,17},{2,10},{10... | collective-permute-start | bytes 3538952 | tf_op jit(solution)/shard_map/ppermute | solution.py:856
  222.3 47.1 %collective-permute-start.25 = (bf16[384,1152]{1,0:T(8,128)(2,1)}, bf16[384,1152]{1,0:T(8,128)(2,1)}, u32[]{:S(2)}, u32[]{:S(2)}) collective-permute-start(bf16[384,1152]{1,0:T(8,128)(2,1)} %get-tuple-element.193), channel_id=1, source_target_pairs={{0,8},{8,0},{16,24},{24,16},{1,9},{9,1},{17,25},{25,17},{2,10},{10... | collective-permute-start | bytes 2654216 | tf_op jit(solution)/shard_map/ppermute | solution.py:856
  227.3 46.3 %collective-permute-start.26 = (bf16[384,1152]{1,0:T(8,128)(2,1)}, bf16[384,1152]{1,0:T(8,128)(2,1)}, u32[]{:S(2)}, u32[]{:S(2)}) collective-permute-start(bf16[384,1152]{1,0:T(8,128)(2,1)} %get-tuple-element.195), channel_id=1, source_target_pairs={{0,16},{8,24},{16,0},{24,8},{1,17},{9,25},{17,1},{25,9},{2,18},{10... | collective-permute-start | bytes 2654216 | tf_op jit(solution)/shard_map/ppermute | solution.py:856
  232.0 41.6 %collective-permute-start.27 = (bf16[384,1152]{1,0:T(8,128)(2,1)}, bf16[384,1152]{1,0:T(8,128)(2,1)}, u32[]{:S(2)}, u32[]{:S(2)}) collective-permute-start(bf16[384,1152]{1,0:T(8,128)(2,1)} %get-tuple-element.197), channel_id=1, source_target_pairs={{0,24},{8,16},{16,8},{24,0},{1,25},{9,17},{17,9},{25,1},{2,26},{10... | collective-permute-start | bytes 2654216 | tf_op jit(solution)/shard_map/ppermute | solution.py:856
  269.4 127.8 %collective-permute-start.44 = (bf16[384,1152]{1,0:T(8,128)(2,1)}, bf16[384,1152]{1,0:T(8,128)(2,1)S(1)}, u32[]{:S(2)}, u32[]{:S(2)}) collective-permute-start(bf16[384,1152]{1,0:T(8,128)(2,1)} %get-tuple-element.221), channel_id=1, source_target_pairs={{0,8},{8,0},{16,24},{24,16},{1,9},{9,1},{17,25},{25,17},{2,10},{10... | collective-permute-start | bytes 2654216 | tf_op jit(solution)/shard_map/ppermute | solution.py:856
  273.6 124.2 %collective-permute-start.45 = (bf16[384,1152]{1,0:T(8,128)(2,1)}, bf16[384,1152]{1,0:T(8,128)(2,1)}, u32[]{:S(2)}, u32[]{:S(2)}) collective-permute-start(bf16[384,1152]{1,0:T(8,128)(2,1)} %get-tuple-element.223), channel_id=1, source_target_pairs={{0,16},{8,24},{16,0},{24,8},{1,17},{9,25},{17,1},{25,9},{2,18},{10... | collective-permute-start | bytes 2654216 | tf_op jit(solution)/shard_map/ppermute | solution.py:856
  273.7 124.2 %collective-permute-start.46 = (bf16[384,1152]{1,0:T(8,128)(2,1)S(1)}, bf16[384,1152]{1,0:T(8,128)(2,1)}, u32[]{:S(2)}, u32[]{:S(2)}) collective-permute-start(bf16[384,1152]{1,0:T(8,128)(2,1)S(1)} %copy-done.34), channel_id=1, source_target_pairs={{0,24},{8,16},{16,8},{24,0},{1,25},{9,17},{17,9},{25,1},{2,26},{10... | collective-permute-start | bytes 2654216 | tf_op jit(solution)/shard_map/ppermute | solution.py:856
  275.0 14.8 %collective-permute-start.21 = (bf16[2,96,1152]{2,1,0:T(8,128)(2,1)}, bf16[2,96,1152]{2,1,0:T(8,128)(2,1)S(1)}, u32[]{:S(2)}, u32[]{:S(2)}) collective-permute-start(bf16[2,96,1152]{2,1,0:T(8,128)(2,1)} %get-tuple-element.184), channel_id=1, source_target_pairs={{0,1},{1,0},{2,3},{3,2},{4,5},{5,4},{6,7},{7,6},{8,9},{9,8},{10,11... | collective-permute-start | bytes 1327112 | tf_op jit(solution)/shard_map/ppermute | solution.py:856
  276.4 21.4 %collective-permute-start.32 = (bf16[2,96,1152]{2,1,0:T(8,128)(2,1)}, bf16[2,96,1152]{2,1,0:T(8,128)(2,1)S(1)}, u32[]{:S(2)}, u32[]{:S(2)}) collective-permute-start(bf16[2,96,1152]{2,1,0:T(8,128)(2,1)} %get-tuple-element.203), channel_id=1, source_target_pairs={{0,1},{1,0},{2,3},{3,2},{4,5},{5,4},{6,7},{7,6},{8,9},{9,8},{10,11... | collective-permute-start | bytes 1327112 | tf_op jit(solution)/shard_map/ppermute | solution.py:856
  289.8 20.4 %collective-permute-start.35 = (bf16[2,96,1152]{2,1,0:T(8,128)(2,1)}, bf16[2,96,1152]{2,1,0:T(8,128)(2,1)S(1)}, u32[]{:S(2)}, u32[]{:S(2)}) collective-permute-start(bf16[2,96,1152]{2,1,0:T(8,128)(2,1)} %get-tuple-element.207), channel_id=1, source_target_pairs={{0,1},{1,0},{2,3},{3,2},{4,5},{5,4},{6,7},{7,6},{8,9},{9,8},{10,11... | collective-permute-start | bytes 1327112 | tf_op jit(solution)/shard_map/ppermute | solution.py:856
  297.8 11.0 %collective-permute-start.31 = (bf16[2,96,1152]{2,1,0:T(8,128)(2,1)S(1)}, bf16[2,96,1152]{2,1,0:T(8,128)(2,1)S(1)}, u32[]{:S(2)}, u32[]{:S(2)}) collective-permute-start(bf16[2,96,1152]{2,1,0:T(8,128)(2,1)S(1)} %add_convert_fusion.11), channel_id=1, source_target_pairs={{0,2},{1,3},{6,4},{7,5},{8,10},{9,11},{14,12},{15,13},{16,18},{17,... | collective-permute-start | bytes 1327112 | tf_op jit(solution)/shard_map/ppermute | solution.py:874
  308.8 15.1 %collective-permute-start.20 = (bf16[2,96,1152]{2,1,0:T(8,128)(2,1)S(1)}, bf16[2,96,1152]{2,1,0:T(8,128)(2,1)S(1)}, u32[]{:S(2)}, u32[]{:S(2)}) collective-permute-start(bf16[2,96,1152]{2,1,0:T(8,128)(2,1)S(1)} %copy-done.35), channel_id=1, source_target_pairs={{0,1},{1,0},{2,3},{3,2},{4,5},{5,4},{6,7},{7,6},{8,9},{9,8},{10,11... | collective-permute-start | bytes 1327112 | tf_op jit(solution)/shard_map/ppermute | solution.py:856
  310.3 12.6 %collective-permute-start.34 = (bf16[2,96,1152]{2,1,0:T(8,128)(2,1)S(1)}, bf16[2,96,1152]{2,1,0:T(8,128)(2,1)S(1)}, u32[]{:S(2)}, u32[]{:S(2)}) collective-permute-start(bf16[2,96,1152]{2,1,0:T(8,128)(2,1)S(1)} %add_convert_fusion.10), channel_id=1, source_target_pairs={{0,2},{1,3},{6,4},{7,5},{8,10},{9,11},{14,12},{15,13},{16,18},{17,... | collective-permute-start | bytes 1327112 | tf_op jit(solution)/shard_map/ppermute | solution.py:874
  322.9 0.8 collective-permute-start.33
  323.7 71.2 %collective-permute-start.52 = (bf16[384,1536]{1,0:T(8,128)(2,1)S(1)}, bf16[384,1536]{1,0:T(8,128)(2,1)S(1)}, u32[]{:S(2)}, u32[]{:S(2)}) collective-permute-start(bf16[384,1536]{1,0:T(8,128)(2,1)S(1)} %copy-done.3), channel_id=1, source_target_pairs={{0,16},{8,24},{16,0},{24,8},{1,17},{9,25},{17,1},{25,9},{2,18},{10... | collective-permute-start | bytes 3538952 | tf_op jit(solution)/shard_map/ppermute | solution.py:856
  323.9 21.8 %collective-permute-start.39 = (bf16[2,96,1152]{2,1,0:T(8,128)(2,1)S(1)}, bf16[2,96,1152]{2,1,0:T(8,128)(2,1)S(1)}, u32[]{:S(2)}, u32[]{:S(2)}) collective-permute-start(bf16[2,96,1152]{2,1,0:T(8,128)(2,1)S(1)} %add_convert_fusion.8), channel_id=1, source_target_pairs={{0,2},{1,3},{6,4},{7,5},{8,10},{9,11},{14,12},{15,13},{16,18},{17,... | collective-permute-start | bytes 1327112 | tf_op jit(solution)/shard_map/ppermute | solution.py:874
  345.7 0.8 collective-permute-start.38
  346.5 19.4 %collective-permute-start.37 = (bf16[2,96,1152]{2,1,0:T(8,128)(2,1)S(1)}, bf16[2,96,1152]{2,1,0:T(8,128)(2,1)S(1)}, u32[]{:S(2)}, u32[]{:S(2)}) collective-permute-start(bf16[2,96,1152]{2,1,0:T(8,128)(2,1)S(1)} %add_convert_fusion.6), channel_id=1, source_target_pairs={{2,0},{3,1},{4,6},{5,7},{10,8},{11,9},{12,14},{13,15},{18,16},{19,... | collective-permute-start | bytes 1327112 | tf_op jit(solution)/shard_map/ppermute | solution.py:874
  347.9 47.0 %copy-start = (bf16[384,1152]{1,0:T(8,128)(2,1)S(1)}, bf16[384,1152]{1,0:T(8,128)(2,1)}, u32[]{:S(2)}) copy-start(bf16[384,1152]{1,0:T(8,128)(2,1)} %get-tuple-element.175.refs_1_.refs_9_.refs_5_) | copy-start | bytes 2654212
  365.9 7.2 %collective-permute-start.36 = (bf16[2,96,1152]{2,1,0:T(8,128)(2,1)S(1)}, bf16[2,96,1152]{2,1,0:T(8,128)(2,1)S(1)}, u32[]{:S(2)}, u32[]{:S(2)}) collective-permute-start(bf16[2,96,1152]{2,1,0:T(8,128)(2,1)S(1)} %add_convert_fusion.5), channel_id=1, source_target_pairs={{0,2},{1,3},{6,4},{7,5},{8,10},{9,11},{14,12},{15,13},{16,18},{17,... | collective-permute-start | bytes 1327112 | tf_op jit(solution)/shard_map/ppermute | solution.py:874
  368.2 47.0 %copy-start.2 = (bf16[384,1152]{1,0:T(8,128)(2,1)S(1)}, bf16[384,1152]{1,0:T(8,128)(2,1)}, u32[]{:S(2)}) copy-start(bf16[384,1152]{1,0:T(8,128)(2,1)} %get-tuple-element.177.refs_3_.refs_11_.refs_7_) | copy-start | bytes 2654212
  373.1 0.8 collective-permute-start.42
  373.9 19.4 %collective-permute-start.41 = (bf16[2,96,1152]{2,1,0:T(8,128)(2,1)S(1)}, bf16[2,96,1152]{2,1,0:T(8,128)(2,1)S(1)}, u32[]{:S(2)}, u32[]{:S(2)}) collective-permute-start(bf16[2,96,1152]{2,1,0:T(8,128)(2,1)S(1)} %add_convert_fusion.3), channel_id=1, source_target_pairs={{2,0},{3,1},{4,6},{5,7},{10,8},{11,9},{12,14},{13,15},{18,16},{19,... | collective-permute-start | bytes 1327112 | tf_op jit(solution)/shard_map/ppermute | solution.py:874
  393.3 1.5 collective-permute-start.40
  394.9 21.6 %collective-permute-start.48 = (bf16[384,1152]{1,0:T(8,128)(2,1)S(1)}, bf16[384,1152]{1,0:T(8,128)(2,1)S(1)}, u32[]{:S(2)}, u32[]{:S(2)}) collective-permute-start(bf16[384,1152]{1,0:T(8,128)(2,1)S(1)} %copy-done), channel_id=1, source_target_pairs={{0,8},{8,0},{16,24},{24,16},{1,9},{9,1},{17,25},{25,17},{2,10},{10... | collective-permute-start | bytes 2654216 | tf_op jit(solution)/shard_map/ppermute | solution.py:856
  394.9 20.3 %collective-permute-start.47 = (bf16[2,96,1152]{2,1,0:T(8,128)(2,1)S(1)}, bf16[2,96,1152]{2,1,0:T(8,128)(2,1)S(1)}, u32[]{:S(2)}, u32[]{:S(2)}) collective-permute-start(bf16[2,96,1152]{2,1,0:T(8,128)(2,1)S(1)} %add_convert_fusion.1), channel_id=1, source_target_pairs={{2,0},{3,1},{4,6},{5,7},{10,8},{11,9},{12,14},{13,15},{18,16},{19,... | collective-permute-start | bytes 1327112 | tf_op jit(solution)/shard_map/ppermute | solution.py:874
  397.3 41.7 %collective-permute-start.51 = (bf16[384,1536]{1,0:T(8,128)(2,1)S(1)}, bf16[384,1536]{1,0:T(8,128)(2,1)S(1)}, u32[]{:S(2)}, u32[]{:S(2)}) collective-permute-start(bf16[384,1536]{1,0:T(8,128)(2,1)S(1)} %copy-done.3), channel_id=1, source_target_pairs={{0,8},{8,0},{16,24},{24,16},{1,9},{9,1},{17,25},{25,17},{2,10},{10... | collective-permute-start | bytes 3538952 | tf_op jit(solution)/shard_map/ppermute | solution.py:856
  397.8 42.6 %collective-permute-start.53 = (bf16[384,1536]{1,0:T(8,128)(2,1)S(1)}, bf16[384,1536]{1,0:T(8,128)(2,1)S(1)}, u32[]{:S(2)}, u32[]{:S(2)}) collective-permute-start(bf16[384,1536]{1,0:T(8,128)(2,1)S(1)} %collective-permute-done.52.refs_10_), channel_id=1, source_target_pairs={{0,8},{8,0},{16,24},{24,16},{1,9},{9,1},{17,25},{25,17},{2,10},{10... | collective-permute-start | bytes 3538952 | tf_op jit(solution)/shard_map/ppermute | solution.py:856
  397.8 22.5 %collective-permute-start.49 = (bf16[384,1152]{1,0:T(8,128)(2,1)S(1)}, bf16[384,1152]{1,0:T(8,128)(2,1)S(1)}, u32[]{:S(2)}, u32[]{:S(2)}) collective-permute-start(bf16[384,1152]{1,0:T(8,128)(2,1)S(1)} %copy-done.1), channel_id=1, source_target_pairs={{0,16},{8,24},{16,0},{24,8},{1,17},{9,25},{17,1},{25,9},{2,18},{10... | collective-permute-start | bytes 2654216 | tf_op jit(solution)/shard_map/ppermute | solution.py:856
  415.2 23.1 %collective-permute-start.50 = (bf16[384,1152]{1,0:T(8,128)(2,1)S(1)}, bf16[384,1152]{1,0:T(8,128)(2,1)S(1)}, u32[]{:S(2)}, u32[]{:S(2)}) collective-permute-start(bf16[384,1152]{1,0:T(8,128)(2,1)S(1)} %copy-done.2), channel_id=1, source_target_pairs={{0,24},{8,16},{16,8},{24,0},{1,25},{9,17},{17,9},{25,1},{2,26},{10... | collective-permute-start | bytes 2654216 | tf_op jit(solution)/shard_map/ppermute | solution.py:856
  416.5 35.1 %collective-permute-start.43 = (bf16[2,96,1152]{2,1,0:T(8,128)(2,1)}, bf16[2,96,1152]{2,1,0:T(8,128)(2,1)S(1)}, u32[]{:S(2)}, u32[]{:S(2)}) collective-permute-start(bf16[2,96,1152]{2,1,0:T(8,128)(2,1)} %add_convert_fusion), channel_id=1, source_target_pairs={{2,0},{3,1},{4,6},{5,7},{10,8},{11,9},{12,14},{13,15},{18,16},{19,... | collective-permute-start | bytes 1327112 | tf_op jit(solution)/shard_map/ppermute | solution.py:874
  420.4 40.6 %collective-permute-start.56 = (bf16[2,96,1152]{2,1,0:T(8,128)(2,1)}, bf16[2,96,1152]{2,1,0:T(8,128)(2,1)S(1)}, u32[]{:S(2)}, u32[]{:S(2)}) collective-permute-start(bf16[2,96,1152]{2,1,0:T(8,128)(2,1)} %broadcast_select_fusion.2.refs_1_), channel_id=1, source_target_pairs={{0,1},{1,0},{2,3},{3,2},{4,5},{5,4},{6,7},{7,6},{8,9},{9,8},{10,11... | collective-permute-start | bytes 1327112 | tf_op jit(solution)/shard_map/ppermute | solution.py:856
  438.3 22.7 %collective-permute-start.55 = (bf16[2,96,1152]{2,1,0:T(8,128)(2,1)}, bf16[2,96,1152]{2,1,0:T(8,128)(2,1)S(1)}, u32[]{:S(2)}, u32[]{:S(2)}) collective-permute-start(bf16[2,96,1152]{2,1,0:T(8,128)(2,1)} %broadcast_select_fusion.3.refs_0_), channel_id=1, source_target_pairs={{0,1},{1,0},{2,3},{3,2},{4,5},{5,4},{6,7},{7,6},{8,9},{9,8},{10,11... | collective-permute-start | bytes 1327112 | tf_op jit(solution)/shard_map/ppermute | solution.py:856
  438.9 22.1 %collective-permute-start.57 = (bf16[2,96,1152]{2,1,0:T(8,128)(2,1)S(1)}, bf16[2,96,1152]{2,1,0:T(8,128)(2,1)S(1)}, u32[]{:S(2)}, u32[]{:S(2)}) collective-permute-start(bf16[2,96,1152]{2,1,0:T(8,128)(2,1)S(1)} %broadcast_select_fusion.1.refs_2_), channel_id=1, source_target_pairs={{0,1},{1,0},{2,3},{3,2},{4,5},{5,4},{6,7},{7,6},{8,9},{9,8},{10,11... | collective-permute-start | bytes 1327112 | tf_op jit(solution)/shard_map/ppermute | solution.py:856
  451.6 21.6 %collective-permute-start.54 = (bf16[2,96,1152]{2,1,0:T(8,128)(2,1)S(1)}, bf16[2,96,1152]{2,1,0:T(8,128)(2,1)S(1)}, u32[]{:S(2)}, u32[]{:S(2)}) collective-permute-start(bf16[2,96,1152]{2,1,0:T(8,128)(2,1)S(1)} %broadcast_select_fusion.refs_0_), channel_id=1, source_target_pairs={{0,1},{1,0},{2,3},{3,2},{4,5},{5,4},{6,7},{7,6},{8,9},{9,8},{10,11... | collective-permute-start | bytes 1327112 | tf_op jit(solution)/shard_map/ppermute | solution.py:856
  479.8 8.7 %collective-permute-start.58 = (f32[2,4608]{1,0:T(2,128)S(1)}, f32[2,4608]{1,0:T(2,128)S(1)}, u32[]{:S(2)}, u32[]{:S(2)}) collective-permute-start(f32[2,4608]{1,0:T(2,128)S(1)} %pad_maximum_fusion), channel_id=1, source_target_pairs={{0,8},{8,0},{16,24},{24,16},{1,9},{9,1},{17,25},{25,17},{2,10},{10... | collective-permute-start | bytes 110600 | tf_op jit(solution)/shard_map/ppermute | solution.py:856
  479.9 8.6 %collective-permute-start.59 = (f32[2,4608]{1,0:T(2,128)S(1)}, f32[2,4608]{1,0:T(2,128)S(1)}, u32[]{:S(2)}, u32[]{:S(2)}) collective-permute-start(f32[2,4608]{1,0:T(2,128)S(1)} %pad_maximum_fusion), channel_id=1, source_target_pairs={{0,16},{8,24},{16,0},{24,8},{1,17},{9,25},{17,1},{25,9},{2,18},{10... | collective-permute-start | bytes 110600 | tf_op jit(solution)/shard_map/ppermute | solution.py:856
  481.7 6.8 %collective-permute-start.60 = (f32[2,4608]{1,0:T(2,128)S(1)}, f32[2,4608]{1,0:T(2,128)S(1)}, u32[]{:S(2)}, u32[]{:S(2)}) collective-permute-start(f32[2,4608]{1,0:T(2,128)S(1)} %pad_maximum_fusion), channel_id=1, source_target_pairs={{0,24},{8,16},{16,8},{24,0},{1,25},{9,17},{17,9},{25,1},{2,26},{10... | collective-permute-start | bytes 110600 | tf_op jit(solution)/shard_map/ppermute | solution.py:856
  (33 other events, 642.2 us)
